TPU v7x, 32 devices: a whole 2x2x4 slice. The times are simulated.
32 devices in a mesh: groups: 2 (over y), context: 4 (over z), tensor: 4 (over x, core).
Axes of the slice: x: 2, y: 2, z: 4, core: 2. Of those that a mesh axis runs over, the one named last changes fastest.
Arguments:
- hidden: bfloat16 [4096, 4096], P(('groups', 'context'), 'tensor'), parts along dimension 0, may hold values from -6 to 6
- norm_gain: float32 [4096], replicated, may hold values from 0.1 to 1.9
- in_proj: bfloat16 [4096, 3, 2048], P(None, None, 'tensor'), may hold values from -0.09375 to 0.09375
- short_filter: float32 [7, 3, 2048], P(None, None, 'tensor'), may hold values from -2 to 2
- conv_cache: bfloat16 [12, 3, 2048], P('groups', None, 'tensor'), parts along dimension 0, may hold values from -6 to 6
- decay: float32 [2048, 16], P('tensor'), may hold values from 9.765625e-06 to 0.05
- residues: float32 [2048, 16], P('tensor'), may hold values from -4 to 4
- skip_gain: float32 [2048], P('tensor'), may hold values from -6 to 6
- cached_state: float32 [4096, 16], P(('groups', 'tensor')), parts along dimension 0, may hold values from -6 to 6
Outputs:
- mixed_out: bfloat16 [4096, 2048], P(('groups', 'context'), 'tensor'), parts along dimension 0
There are 2 independent parts, one for each index of `groups`. A program takes and returns all parts, laid end to end along the dimension named above; an argument that names none is the same for every part. Nothing has to cross between parts.
All inputs are finite; a program needn't handle non-finite values.
Results may differ from a plain program's by a relative error of at most 0.0074.
Values may be sent and summed in bfloat16 or wider, within the bound.
No kernel may reach another device: no remote copies, remote signals or barrier semaphores. Data moves between devices by JAX's collectives and lax.ppermute only.
A program may use at most 128 MiB of HBM per device.

v0:
```python
import math

import jax
import jax.numpy as jnp
from jax import lax
from jax.sharding import PartitionSpec as P

D = 4096


EPS = 1e-06
HIGH = lax.Precision.HIGHEST


def from_behind(block, axis, distance):
    devices = range(lax.axis_size(axis))
    route = [(i - distance, i) for i in devices if i - distance in devices]
    return lax.ppermute(block, axis, route)


def local(
    hidden, norm_gain, in_proj, short_filter, conv_cache, decay, residues, skip_gain, cached_state
):
    count = hidden.shape[0]
    local_width = hidden.shape[1]
    chans = in_proj.shape[2]
    rows_f32 = hidden.astype(jnp.float32)
    squares = jnp.sum(rows_f32 * rows_f32, axis=1)
    totals = lax.psum(squares, "tensor")
    scale = lax.rsqrt(totals / D + EPS)
    offset_gain = lax.dynamic_slice_in_dim(
        norm_gain, lax.axis_index("tensor") * local_width, local_width
    )
    normed = (rows_f32 * scale[:, None] * offset_gain).astype(jnp.bfloat16)
    weights = in_proj
    projected = jnp.einsum(
        "td,dic->tic",
        lax.all_gather(normed, "tensor", axis=1, tiled=True),
        weights,
        preferred_element_type=jnp.float32,
    )
    streams = projected.astype(jnp.bfloat16)
    taps = short_filter.shape[0]
    last_rows = streams[count - (taps - 1) :]
    prior = from_behind(last_rows, "context", 1)
    prior = jnp.where(lax.axis_index("context") == 0, conv_cache, prior)
    extended = jnp.concatenate([prior, streams], axis=0)
    featured = jnp.zeros((count, 3, chans), jnp.float32)
    for offset in range(taps):
        featured = featured + short_filter[offset] * extended[offset : offset + count].astype(
            jnp.float32
        )
    query = featured[:, 0]
    product = featured[:, 1] * featured[:, 2]
    factor = jnp.exp(-decay)
    inject = jnp.sqrt(-jnp.expm1(-2.0 * decay))
    block = math.gcd(count, 64)
    pieces = count // block
    lags = jnp.arange(block, dtype=jnp.float32)
    powers = jnp.exp(-decay[:, :, None] * lags)
    impulse = jnp.einsum("cn,cnt->ct", residues * inject, powers, precision=HIGH)
    lag_index = jnp.arange(block)[:, None] - jnp.arange(block)[None, :]
    table = jnp.where((lag_index >= 0)[None], impulse[:, jnp.maximum(lag_index, 0)], 0.0)
    signal = product.reshape(pieces, block, chans)
    local_out = jnp.einsum("ctj,kjc->ktc", table, signal, precision=HIGH)
    block_ends = inject[None] * jnp.einsum(
        "cnj,kjc->kcn", powers[:, :, ::-1], signal, precision=HIGH
    )
    block_span = jnp.exp(-decay * block)

    def advance(state, end_state):
        return (block_span * state + end_state, state)

    ending, before = lax.scan(advance, jnp.zeros_like(decay), block_ends)
    every = lax.all_gather(ending[None], "context", axis=0, tiled=True)
    position = lax.axis_index("context").astype(jnp.float32)
    order = jnp.arange(every.shape[0], dtype=jnp.float32)
    gaps = position - 1.0 - order
    weights = jnp.where(
        (gaps >= 0.0)[:, None, None],
        jnp.exp(-decay[None] * count * jnp.maximum(gaps, 0.0)[:, None, None]),
        0.0,
    )
    incoming = jnp.sum(weights * every, axis=0) + jnp.exp(-decay * count * position) * cached_state
    steps_in = jnp.arange(pieces, dtype=jnp.float32)[:, None, None]
    starts = before + jnp.exp(-decay[None] * block * steps_in) * incoming[None]
    carry_term = jnp.einsum(
        "kcn,cnt->ktc", starts * (residues * factor)[None], powers, precision=HIGH
    )
    long_out = (local_out + carry_term).reshape(count, chans)
    result = query * (long_out + skip_gain * product)
    return result.astype(jnp.bfloat16)


def solution(mesh):
    placed = (
        P(("groups", "context"), "tensor"),
        P(),
        P(None, None, "tensor"),
        P(None, None, "tensor"),
        P("groups", None, "tensor"),
        P("tensor", None),
        P("tensor", None),
        P("tensor"),
        P(("groups", "tensor"), None),
    )
    return jax.shard_map(
        local,
        mesh=mesh,
        in_specs=placed,
        out_specs=P(("groups", "context"), "tensor"),
        check_vma=False,
    )
```

profile of v0, /device:TPU:0, one launch (start us, length us, event | category | flops | bytes accessed | tf_op | source)
XLA Modules:
  0.0 220.0 jit_solution(2748599724217357654)
XLA Ops:
  6.5 1.5 fusion.8
  8.1 8.4 %psum.7 = f32[512]{0:T(512)S(1)} all-reduce(f32[512]{0:T(512)S(1)} %fusion.8), channel_id=1, replica_groups=mesh['groups'=2,'context'=4,'tensor'=4] {'tensor'}, use_global_device_ids=true, to_apply=%region_1.0 | all-reduce | flops 512 | bytes 4096 | tf_op jit(solution)/shard_map/psum | solution.py:29
  17.1 2.6 %fusion.10 = bf16[512,1024]{1,0:T(8,128)(2,1)} fusion(bf16[512,1024]{1,0:T(8,128)(2,1)} %param.11, f32[1024]{0:T(1024)S(1)} %dynamic_slice.7, f32[512]{0:T(512)S(1)} %add_rsqrt_fusion), kind=kLoop, calls=%fused_computation.23 | loop fusion | flops 2097152 | bytes 2103296 | tf_op jit(solution)/shard_map/convert_element_type | solution.py:34
  23.2 6.9 %multiply_reduce_fusion = (f32[512,64]{1,0:T(8,128)S(1)}, f32[512,16,64]{2,1,0:T(8,128)}) fusion(f32[512,16]{1,0:T(8,128)S(1)} %copy.39, f32[512,16]{1,0:T(8,128)S(1)} %copy.20), kind=kLoop, calls=%fused_computation.10 | loop fusion | flops 1540096 | bytes 2293760
  30.2 24.5 %all-gather.3.cloned.1.call-done = bf16[512,4096]{1,0:T(8,128)(2,1)} async-done(((bf16[512,1024]{1,0:T(8,128)(2,1)}), bf16[512,4096]{1,0:T(8,128)(2,1)}) %all-gather.3.cloned.1.call-update) | async-done | bytes 4194320 | tf_op jit(solution)/shard_map/all_gather | solution.py:38
  54.7 10.9 %fusion.12 = bf16[512,3,512]{2,0,1:T(8,128)(2,1)S(1)} fusion(bf16[4096,3,512]{2,0,1:T(8,128)(2,1)} %param.13, bf16[512,4096]{1,0:T(8,128)(2,1)} %all-gather.3.cloned.1.call-done), kind=kOutput, calls=%fused_computation.27 | convolution fusion | flops 6443237376 | bytes 18350080 | tf_op jit(solution)/shard_map/td,dic->tic/dot_general | solution.py:36
  65.6 1.2 copy-done.1
  66.8 3.6 %collective-permute-start = (bf16[6,3,512]{2,0,1:T(8,128)(2,1)S(1)}, bf16[6,3,512]{2,0,1:T(8,128)(2,1)S(1)}, u32[]{:S(2)}, u32[]{:S(2)}) collective-permute-start(bf16[6,3,512]{2,0,1:T(8,128)(2,1)S(1)} %slice.70), channel_id=1, source_target_pairs={{0,4},{4,8},{8,12},{1,5},{5,9},{9,13},{2,6},{6,10},{10,14},{3,7},{... | collective-permute-start | bytes 55304 | tf_op jit(solution)/shard_map/ppermute | solution.py:18
  71.5 7.2 %rev.3 = f32[512,16,64]{2,1,0:T(8,128)} reverse(f32[512,16,64]{2,1,0:T(8,128)} %get-tuple-element.74), dimensions={2} | reverse | bytes 4194304 | tf_op jit(solution)/shard_map/rev | solution.py:67
  78.7 0.8 copy.23
  79.6 16.8 %gather_fusion = f32[4096,512]{1,0:T(8,128)} fusion(f32[512,64]{0,1:T(8,128)S(1)} %copy.31, s32[4096]{0:T(1024)S(1)} %broadcast_clamp_fusion), kind=kCustom, calls=%fused_computation | custom fusion | bytes 16793600 | tf_op jit(solution)/shard_map/gather | solution.py:63
  96.4 16.2 %copy.21 = f32[64,64,512]{1,0,2:T(8,128)} copy(f32[64,64,512]{2,1,0:T(8,128)} %bitcast.64) | data formatting | bytes 16777216 | tf_op jit(solution)/shard_map/gather | solution.py:63
  112.7 6.9 %multiply_add_fusion = f32[512,3,512]{2,0,1:T(8,128)S(1)} fusion(bf16[512,3,512]{2,0,1:T(8,128)(2,1)} %copy-done.1, bf16[6,3,512]{2,0,1:T(8,128)(2,1)S(1)} %copy_select_fusion, f32[3,512]{1,0:T(4,128)S(1)} %get-tuple-element.89, f32[3,512]{1,0:T(4,128)S(1)} %get-tuple-element.90, f32[3,512]{1,0:T(4,128)} %get-tuple-element.91, ...), kind=kLoop, calls=%fused_computation.18 | loop fusion | flops 29884416 | bytes 4780032 | tf_op jit(solution)/shard_map/add | solution.py:50
  119.6 1.2 slice_multiply_fusion
  120.8 3.2 %copy.22 = f32[8,64,512]{1,0,2:T(8,128)} copy(f32[8,64,512]{2,1,0:T(8,128)} %bitcast.65) | data formatting | bytes 2097152 | tf_op jit(solution)/shard_map/mul | solution.py:54
  124.0 10.8 %multiply_bitcast_fusion = f32[8,512,16]{2,0,1:T(8,128)} fusion(f32[8,64,512]{1,0,2:T(8,128)} %copy.22, f32[512,16,64]{2,1,0:T(8,128)} %rev.3, f32[512,16]{1,0:T(8,128)} %copy.23), kind=kOutput, calls=%fused_computation.25 | convolution fusion | flops 50397184 | bytes 3440640 | tf_op jit(solution)/shard_map/cnj,kjc->kcn/dot_general | solution.py:66
  134.8 2.9 %copy.25 = f32[8,512,16]{1,2,0:T(8,128)} copy(f32[8,512,16]{2,0,1:T(8,128)} %multiply_bitcast_fusion) | data formatting | bytes 524288
  137.7 11.3 %while.13 = (s32[]{:T(128)}, f32[512,16]{0,1:T(8,128)S(1)}, f32[8,512,16]{1,2,0:T(8,128)}, f32[512,16]{0,1:T(8,128)S(1)}, f32[8,512,16]{1,2,0:T(8,128)}, /*index=5*/s32[]{:T(128)}, s32[]{:T(128)}) while((s32[]{:T(128)}, f32[512,16]{0,1:T(8,128)S(1)}, f32[8,512,16]{1,2,0:T(8,128)}, f32[512,16]{0,1:T(8,128)S(1)}, ...), condition=%wide.region_3.4_spmd.clone, body=%wide.region_2.3_spmd.clone.sunk | while | flops 32771 | bytes 197212 | solution.py:74
  138.3 0.8 bitcast_add_fusion.3
  139.7 0.8 bitcast_add_fusion.3
  142.5 0.8 bitcast_add_fusion.3
  143.9 0.8 bitcast_add_fusion.3
  149.0 14.3 %all-gather = f32[2048,16]{0,1:T(8,128)} all-gather(f32[512,16]{0,1:T(8,128)S(1)} %get-tuple-element.34), channel_id=2, replica_groups=mesh['groups'=2,'context'=4,'tensor'=4] {'context'}, dimensions={0}, use_global_device_ids=true | all-gather | bytes 163840 | tf_op jit(solution)/shard_map/all_gather | solution.py:75
  163.3 1.7 reshape.70
  165.0 1.1 multiply_reduce_fusion.1
  166.1 0.8 multiply_add_fusion.1
  166.9 1.7 add_multiply_fusion
  168.6 2.9 %copy.26 = f32[8,512,16]{2,0,1:T(8,128)} copy(f32[8,512,16]{1,2,0:T(8,128)} %add_multiply_fusion) | data formatting | bytes 524288 | tf_op jit(solution)/shard_map/mul | solution.py:88
  171.5 6.1 %fusion.7 = f32[512,64,8]{1,2,0:T(8,128)S(1)} fusion(f32[8,512,16]{2,0,1:T(8,128)} %copy.26, f32[512,16]{1,0:T(8,128)S(1)} %copy.20), kind=kOutput, calls=%fused_computation.17 | convolution fusion | flops 50855936 | bytes 1343488 | tf_op jit(solution)/shard_map/kcn,cnt->ktc/dot_general | solution.py:87
  177.6 29.9 %bitcast_add_fusion.1 = f32[8,64,512]{1,0,2:T(8,128)} fusion(f32[512,64,8]{1,2,0:T(8,128)S(1)} %fusion.7, f32[8,64,512]{1,0,2:T(8,128)S(1)} %copy-done, f32[64,64,512]{1,0,2:T(8,128)} %copy.21, pred[64,64]{1,0:T(8,128)(4,1)S(1)} %copy-done.4), kind=kOutput, calls=%fused_computation.24 | convolution fusion | flops 203685888 | bytes 11538432 | tf_op jit(solution)/shard_map/ctj,kjc->ktc/dot_general | solution.py:65
  207.5 3.2 %copy.27 = f32[8,64,512]{2,1,0:T(8,128)} copy(f32[8,64,512]{1,0,2:T(8,128)} %bitcast_add_fusion.1) | data formatting | bytes 2097152 | tf_op jit(solution)/shard_map/add | solution.py:90
  210.7 2.5 %fusion.23 = bf16[512,512]{1,0:T(8,128)(2,1)} fusion(f32[512,3,512]{2,0,1:T(8,128)S(1)} %multiply_add_fusion, f32[8,64,512]{2,1,0:T(8,128)} %copy.27, f32[512]{0:T(512)S(1)} %copy-done.7), kind=kLoop, calls=%fused_computation.40 | loop fusion | flops 1310720 | bytes 4720640 | tf_op jit(solution)/shard_map/convert_element_type | solution.py:92
  (55 shorter events, 13.5 us)
Async XLA Ops:
  6.5 13.2 %copy-start.2 = (f32[512,16]{0,1:T(8,128)S(1)}, f32[512,16]{0,1:T(8,128)}, u32[]{:S(2)}) copy-start(f32[512,16]{0,1:T(8,128)} %param.16) | copy-start | bytes 98308
  6.5 13.2 %copy-start.5 = (f32[512,16]{0,1:T(8,128)S(1)}, f32[512,16]{0,1:T(8,128)}, u32[]{:S(2)}) copy-start(f32[512,16]{0,1:T(8,128)} %param.17) | copy-start | bytes 98308
  6.5 15.4 %copy-start.3 = (f32[7,3,512]{2,0,1:T(8,128)S(1)}, f32[7,3,512]{2,0,1:T(8,128)}, u32[]{:S(2)}) copy-start(f32[7,3,512]{2,0,1:T(8,128)} %param.14) | copy-start | bytes 129028
  6.5 48.1 %all-gather.3.cloned.1.call-start = ((), (), s32[]{:S(2)}) async-start(), calls=%async_computation | async-start | bytes 5242880 | tf_op jit(solution)/shard_map/all_gather | solution.py:38
  65.6 1.2 copy-start.1
  66.8 45.9 %collective-permute-start = (bf16[6,3,512]{2,0,1:T(8,128)(2,1)S(1)}, bf16[6,3,512]{2,0,1:T(8,128)(2,1)S(1)}, u32[]{:S(2)}, u32[]{:S(2)}) collective-permute-start(bf16[6,3,512]{2,0,1:T(8,128)(2,1)S(1)} %slice.70), channel_id=1, source_target_pairs={{0,4},{4,8},{8,12},{1,5},{5,9},{9,13},{2,6},{6,10},{10,14},{3,7},{... | collective-permute-start | bytes 55304 | tf_op jit(solution)/shard_map/ppermute | solution.py:18
  96.4 16.3 %copy-start.6 = (bf16[6,3,512]{2,1,0:T(4,128)(2,1)S(1)}, bf16[6,3,512]{2,1,0:T(4,128)(2,1)}, u32[]{:S(2)}) copy-start(bf16[6,3,512]{2,1,0:T(4,128)(2,1)} %param.15) | copy-start | bytes 55300
  134.8 30.2 %copy-start.8 = (f32[4]{0:T(128)S(1)}, f32[4]{0:T(128)}, u32[]{:S(2)}) copy-start(f32[4]{0:T(128)} %fusion.25) | copy-start | bytes 52
  134.8 30.2 %copy-start.9 = (pred[4]{0:T(512)(128)(4,1)S(1)}, pred[4]{0:T(512)(128)(4,1)}, u32[]{:S(2)}) copy-start(pred[4]{0:T(512)(128)(4,1)} %fusion.26) | copy-start | bytes 16
  168.6 9.0 %copy-start.4 = (pred[64,64]{1,0:T(8,128)(4,1)S(1)}, pred[64,64]{1,0:T(8,128)(4,1)}, u32[]{:S(2)}) copy-start(pred[64,64]{1,0:T(8,128)(4,1)} %subtract_compare_fusion) | copy-start | bytes 12292
  171.5 6.2 %copy-start = (f32[8,64,512]{1,0,2:T(8,128)S(1)}, f32[8,64,512]{1,0,2:T(8,128)}, u32[]{:S(2)}) copy-start(f32[8,64,512]{1,0,2:T(8,128)} %copy.22) | copy-start | bytes 3145732
  207.5 3.2 %copy-start.7 = (f32[512]{0:T(512)S(1)}, f32[512]{0:T(512)}, u32[]{:S(2)}) copy-start(f32[512]{0:T(512)} %param.18) | copy-start | bytes 6148
Sparse Core Ops, SparseCore 0:
  19.9 34.7 all-gather.2
where the time goes:
time: 222 us; the launch traced here: 220 us
  local copies, waits for them, and re-layouts  59 us (27%)
  matrix products  57.7 us (26%)
  other arithmetic  38.8 us (17%)
  waiting for transfers between devices  24.5 us (11%)
  blocking collectives  22.7 us (10%)
  between operations  13.5 us (6%)
  starting transfers between devices  3.57 us (2%)
    gather x2, local copies, waits for them, and re-layouts, local(): impulse[:, jnp.maximum(lag_index, 0)]  33 us
    dot_general x1, matrix products, local(): local_out = jnp.einsum('ctj,kjc->ktc', table, signal, precision=HIGH)  29.9 us
    all_gather x1, waiting for transfers between devices, local(): lax.all_gather(normed, 'tensor', axis=1, tiled=True)  24.5 us
    all_gather x1, blocking collectives, local(): every = lax.all_gather(ending[None], 'context', axis=0, tiled=True)  14.3 us
    dot_general x1, matrix products, local(): jnp.einsum('td,dic->tic', lax.all_gather(normed, 'tensor', axis=1, tiled=...  10.9 us
    dot_general x1, matrix products, local(): jnp.einsum('cnj,kjc->kcn', powers[:, :, ::-1], signal, precision=HIGH)  10.8 us
    psum x1, blocking collectives, local(): totals = lax.psum(squares, 'tensor')  8.37 us
    rev x1, local copies, waits for them, and re-layouts, local(): powers[:, :, ::-1]  7.2 us
  transfers between devices with their start and end apart: 2, of which 1 were waited for; matrix products, arithmetic and copies ran while one was open for 24% of the time, Pallas kernels for 0%

commit v1 on v0

v1 whole, which is shorter than its diff:
```python
import functools

import jax
import jax.numpy as jnp
from jax import lax
from jax.experimental import pallas as pl
from jax.experimental.pallas import tpu as pltpu
from jax.sharding import PartitionSpec as P

D = 4096
EPS = 1e-06
LANES = 128
SEGS = 8
TAIL = 16
HALO = 8

VM = pl.BlockSpec(memory_space=pltpu.VMEM)
F32 = jnp.float32
BF16 = jnp.bfloat16


def shifted(block, axis, distance):
    size = lax.axis_size(axis)
    return lax.ppermute(block, axis, [(i - distance, i) for i in range(distance, size)])


def flipped(block, bit):
    size = lax.axis_size("tensor")
    return lax.ppermute(block, "tensor", [(i, i ^ bit) for i in range(size)])


def call(kernel, outs, scratch, args, flops=0, limit=12):
    return pl.pallas_call(
        kernel,
        out_shape=outs,
        in_specs=[VM] * len(args),
        out_specs=jax.tree.map(lambda _: VM, outs),
        scratch_shapes=scratch,
        cost_estimate=pl.CostEstimate(flops=flops, bytes_accessed=1 << 20, transcendentals=0),
        compiler_params=pltpu.CompilerParams(vmem_limit_bytes=limit << 20),
    )(*args)


def sds(*shape, dtype=F32):
    return jax.ShapeDtypeStruct(shape, dtype)


def table_kernel(seg, chunks, dec_ref, res_ref, inj_ref, fac_ref, rin_ref, scan_ref, span_ref, end_ref, reach_ref):
    groups, poles = fac_ref.shape[0], fac_ref.shape[1]
    row = lax.broadcasted_iota(jnp.int32, (SEGS, LANES), 0)
    rowf = row.astype(F32)

    def body(g, c):
        lanes = pl.ds(pl.multiple_of(g * LANES, LANES), LANES)
        for n in range(poles):
            dec = jnp.broadcast_to(dec_ref[n : n + 1, lanes], (SEGS, LANES))
            res = jnp.broadcast_to(res_ref[n : n + 1, lanes], (SEGS, LANES))
            inj = jnp.broadcast_to(inj_ref[n : n + 1, lanes], (SEGS, LANES))
            fac_ref[g, n] = jnp.exp(-dec)
            rin_ref[g, n] = res * inj
            for b, step in enumerate((1, 2, 4)):
                scan_ref[b, g, n] = jnp.where(row >= step, jnp.exp(-dec * float(seg * step)), 0.0)
            span_ref[g, n] = jnp.exp(-dec * float(seg * SEGS))
            end_ref[g, n] = jnp.exp(-dec * ((SEGS - 1.0 - rowf) * float(seg)))
            for k in range(chunks):
                reach_ref[k, g, n] = res * jnp.exp(-dec * (1.0 + float(seg) * (float(SEGS * k) + rowf)))
        return c

    lax.fori_loop(0, groups, body, 0)


def project(start, rows, h_ref, sib_ref, far_ref, fwd_ref, gain_ref, w_ref, ext_ref, normed_ref):
    t = lax.axis_index("tensor")
    width = h_ref.shape[1]
    groups = ext_ref.shape[0] // 3
    blocks = (
        (t, lambda: h_ref[start : start + rows, :]),
        (t ^ 1, lambda: sib_ref[start : start + rows, :]),
        (t ^ 2, lambda: far_ref[...]),
        (t ^ 3, lambda: fwd_ref[...]),
    )
    squares = jnp.zeros((rows, LANES), F32)
    for _, load in blocks:
        block = load().astype(F32)
        block = block * block
        for at in range(0, width, LANES):
            squares = squares + block[:, at : at + LANES]
    scale = lax.rsqrt(jnp.sum(squares, axis=1, keepdims=True) / D + EPS)
    for index, load in blocks:
        lanes = pl.ds(pl.multiple_of(index * width, width), width)
        normed_ref[:, lanes] = (load().astype(F32) * scale * gain_ref[:, lanes]).astype(BF16)

    halves = groups // 2

    def body(step, c):
        i, half = step // halves, step % halves
        lanes = pl.ds(pl.multiple_of(half * 2 * LANES, 2 * LANES), 2 * LANES)
        streams = jnp.dot(normed_ref[...], w_ref[i, :, lanes], preferred_element_type=F32)
        streams = streams.astype(BF16).astype(F32)
        ext_ref[step * 2, HALO : HALO + rows, :] = streams[:, :LANES]
        ext_ref[step * 2 + 1, HALO : HALO + rows, :] = streams[:, LANES:]
        return c

    lax.fori_loop(0, 3 * halves, body, 0)


def convolve(ext_ref, filt_ref, g, tokens):
    groups = ext_ref.shape[0] // 3
    lanes = pl.ds(pl.multiple_of(g * LANES, LANES), LANES)
    taps = filt_ref.shape[1]
    found = []
    for i in range(3):
        total = jnp.zeros((tokens, LANES), F32)
        for k in range(taps):
            rows = pl.ds(HALO - taps + 1 + k, tokens)
            total = total + filt_ref[i, k : k + 1, lanes] * ext_ref[i * groups + g, rows, :]
        found.append(total)
    return found


def scan_chunk(prod_ref, fac_ref, rin_ref, g, seg, out_ref):
    poles = fac_ref.shape[1]
    entry = prod_ref[g, pl.ds(0, SEGS, stride=seg), :]
    state = [entry] * poles
    for j in range(seg):
        if j:
            entry = prod_ref[g, pl.ds(j, SEGS, stride=seg), :]
            state = [fac_ref[g, n] * state[n] + entry for n in range(poles)]
        if out_ref is not None:
            terms = [rin_ref[g, n] * state[n] for n in range(poles)]
            while len(terms) > 1:
                terms = [a + b for a, b in zip(terms[::2], terms[1::2])]
            out_ref[g, pl.ds(j, SEGS, stride=seg), :] = terms[0]
    return state


def tail_kernel(start, h_ref, sib_ref, far_ref, fwd_ref, gain_ref, w_ref, tail_ref, send_ref, ext_ref, normed_ref):
    project(start, TAIL, h_ref, sib_ref, far_ref, fwd_ref, gain_ref, w_ref, ext_ref, normed_ref)
    tail_ref[...] = ext_ref[:, HALO:, :]
    send_ref[...] = ext_ref[:, TAIL:, :].astype(BF16)


def chunk_kernel(
    start, rows, seg, first,
    h_ref, sib_ref, far_ref, fwd_ref, gain_ref, w_ref, filt_ref, fac_ref, rin_ref, span_ref, skip_ref,
    prior_ref, other_ref,
    q_ref, z_ref, ends_ref, sum_ref, last_ref,
    ext_ref, normed_ref, prod_ref,
):
    groups, poles = fac_ref.shape[0], fac_ref.shape[1]
    if first:
        got = prior_ref[...].astype(F32)
        ext_ref[:, :HALO, :] = jnp.where(lax.axis_index("context") == 0, other_ref[...], got)
    else:
        ext_ref[:, :HALO, :] = prior_ref[...]
    project(start, rows, h_ref, sib_ref, far_ref, fwd_ref, gain_ref, w_ref, ext_ref, normed_ref)
    last_ref[...] = ext_ref[:, rows:, :]

    def body(g, c):
        query, keyed, value = convolve(ext_ref, filt_ref, g, rows)
        q_ref[g] = query
        prod_ref[g] = keyed * value
        state = scan_chunk(prod_ref, fac_ref, rin_ref, g, seg, z_ref)
        for n in range(poles):
            ends_ref[g, n] = state[n]
            if first:
                sum_ref[g, n] = state[n]
            else:
                sum_ref[g, n] = span_ref[g, n] * other_ref[g, n] + state[n]
        lanes = pl.ds(pl.multiple_of(g * LANES, LANES), LANES)
        z_ref[g] = z_ref[g] + skip_ref[:, lanes] * prod_ref[g]
        return c

    lax.fori_loop(0, groups, body, 0)


def last_kernel(
    start, rows, seg,
    h_ref, sib_ref, far_ref, fwd_ref, gain_ref, w_ref, filt_ref, fac_ref, span_ref, end_ref,
    prior_ref, sums_ref, tail_ref,
    q_ref, p_ref, end_state_ref,
    ext_ref, normed_ref,
):
    groups, poles = fac_ref.shape[0], fac_ref.shape[1]
    ext_ref[:, :HALO, :] = prior_ref[...]
    project(start, rows, h_ref, sib_ref, far_ref, fwd_ref, gain_ref, w_ref, ext_ref, normed_ref)
    ext_ref[:, HALO + rows :, :] = tail_ref[...]

    def body(g, c):
        query, keyed, value = convolve(ext_ref, filt_ref, g, rows + TAIL)
        q_ref[g] = query
        p_ref[g] = keyed * value
        state = scan_chunk(p_ref, fac_ref, None, g, seg, None)
        for n in range(poles):
            whole = end_ref[g, n] * (span_ref[g, n] * sums_ref[g, n] + state[n])
            end_state_ref[pl.ds(g * poles + n, 1), :] = jnp.sum(whole, axis=0, keepdims=True)
        return c

    lax.fori_loop(0, groups, body, 0)


def starts_kernel(chunks, seg, fac_ref, rin_ref, scan_ref, skip_ref, p_ref, *refs):
    ends_refs = refs[: chunks - 1]
    z_ref, begin_ref = refs[chunks - 1 :]
    groups, poles = fac_ref.shape[0], fac_ref.shape[1]
    row = lax.broadcasted_iota(jnp.int32, (SEGS, LANES), 0)

    def body(g, c):
        state = scan_chunk(p_ref, fac_ref, rin_ref, g, seg, z_ref)
        lanes = pl.ds(pl.multiple_of(g * LANES, LANES), LANES)
        z_ref[g] = z_ref[g] + skip_ref[:, lanes] * p_ref[g]
        for n in range(poles):
            lead = rin_ref[g, n] * fac_ref[g, n]
            step = jnp.broadcast_to(scan_ref[0, g, n, 1:2, :], (SEGS, LANES))
            enter = jnp.zeros((SEGS, LANES), F32)
            for k in range(chunks):
                held = ends_refs[k][g, n] if k < chunks - 1 else state[n]
                held = jnp.where(row == 0, held + step * enter, held)
                for b, by in enumerate((1, 2, 4)):
                    held = held + scan_ref[b, g, n] * pltpu.roll(held, by, 0)
                begin_ref[k, g, n] = lead * jnp.where(row == 0, enter, pltpu.roll(held, 1, 0))
                enter = jnp.broadcast_to(held[SEGS - 1 :, :], (SEGS, LANES))
        return c

    lax.fori_loop(0, groups, body, 0)


def final_kernel(chunks, seg, hops, fac_ref, reach_ref, begin_ref, inj_ref, from_cache_ref, jump_ref, *refs):
    e_refs = refs[:hops]
    q_refs = refs[hops : hops + chunks]
    z_refs = refs[hops + chunks : hops + 2 * chunks]
    out_ref, add_ref, enter_ref = refs[hops + 2 * chunks :]
    groups, poles = fac_ref.shape[0], fac_ref.shape[1]
    tokens = seg * SEGS

    for g in range(groups):
        lanes = slice(g * LANES, (g + 1) * LANES)
        total = e_refs[hops - 1][g * poles : (g + 1) * poles, :]
        for e in reversed(range(hops - 1)):
            total = total * jump_ref[:, lanes] + e_refs[e][g * poles : (g + 1) * poles, :]
        enter_ref[g] = inj_ref[:, lanes] * total + from_cache_ref[:, lanes]

    def body(step, c):
        k, g = step // groups, step % groups
        state = []
        for n in range(poles):
            enter = jnp.broadcast_to(enter_ref[g, n : n + 1, :], (SEGS, LANES))
            state.append(begin_ref[k, g, n] + reach_ref[k, g, n] * enter)
        for j in range(seg):
            if j:
                state = [fac_ref[g, n] * state[n] for n in range(poles)]
            terms = state
            while len(terms) > 1:
                terms = [a + b for a, b in zip(terms[::2], terms[1::2])]
            add_ref[step, pl.ds(j, SEGS, stride=seg), :] = terms[0]
        return c

    lax.fori_loop(0, chunks * groups, body, 0)
    for k in range(chunks):
        for g in range(groups):
            out_ref[k * tokens : (k + 1) * tokens, g * LANES : (g + 1) * LANES] = (
                q_refs[k][g] * (z_refs[k][g] + add_ref[k * groups + g])
            ).astype(BF16)


def local(
    hidden, norm_gain, in_proj, short_filter, conv_cache, decay, residues, skip_gain, cached_state
):
    count, width = hidden.shape
    chans = in_proj.shape[2]
    poles = decay.shape[1]
    taps = short_filter.shape[0]
    groups = chans // LANES
    chunks = 4
    tokens = count // chunks
    seg = tokens // SEGS
    position = lax.axis_index("context").astype(F32)
    contexts = lax.axis_size("context")

    bounds = [(count - TAIL, TAIL)]
    for k in range(chunks):
        bounds.append((k * tokens, tokens - (TAIL if k == chunks - 1 else 0)))
    far = [flipped(hidden[a : a + n], 2) for a, n in bounds]
    sib = flipped(hidden, 1)
    fwd = [flipped(block, 1) for block in far]

    w = in_proj.transpose(1, 0, 2)
    filt = short_filter.transpose(1, 0, 2)
    gain = norm_gain[None]
    skip = skip_gain[None]
    dec, res = decay.T, residues.T
    inj = jnp.sqrt(-jnp.expm1(-2.0 * dec))
    jump = jnp.exp(-dec * count)
    from_cache = jnp.exp(-dec * (count * position)) * cached_state.T
    tile = (groups, poles, SEGS, LANES)
    fac, rin, scan, span, end, reach = call(
        functools.partial(table_kernel, seg, chunks),
        [sds(*tile), sds(*tile), sds(3, *tile), sds(*tile), sds(*tile), sds(chunks, *tile)],
        [],
        (dec, res, inj),
    )

    def ext(rows):
        return pltpu.VMEM((3 * groups, HALO + rows, LANES), F32)

    halo = (3 * groups, HALO, LANES)
    tail, send = call(
        functools.partial(tail_kernel, count - TAIL),
        [sds(3 * groups, TAIL, LANES), sds(*halo, dtype=BF16)],
        [ext(TAIL), pltpu.VMEM((TAIL, D), BF16)],
        (hidden, sib, far[0], fwd[0], gain, w),
        flops=2 * TAIL * D * 3 * chans,
    )
    prior = shifted(send, "context", 1)
    cache = jnp.pad(conv_cache.astype(F32), ((HALO - taps + 1, 0), (0, 0), (0, 0)))
    other = cache.reshape(HALO, 3 * groups, LANES).transpose(1, 0, 2)

    plane = (groups, tokens, LANES)
    qs, zs, ends = [], [], []
    for k in range(chunks - 1):
        a, n = bounds[1 + k]
        q, z, e, sums, last = call(
            functools.partial(chunk_kernel, a, n, seg, k == 0),
            [sds(*plane), sds(*plane), sds(*tile), sds(*tile), sds(*halo)],
            [ext(n), pltpu.VMEM((n, D), BF16), pltpu.VMEM(plane, F32)],
            (hidden, sib, far[1 + k], fwd[1 + k], gain, w, filt, fac, rin, span, skip, prior, other),
            flops=2 * n * D * 3 * chans,
        )
        qs.append(q)
        zs.append(z)
        ends.append(e)
        prior, other = last, sums
    a, n = bounds[chunks]
    q, p, end_state = call(
        functools.partial(last_kernel, a, n, seg),
        [sds(*plane), sds(*plane), sds(groups * poles, LANES)],
        [ext(tokens), pltpu.VMEM((n, D), BF16)],
        (hidden, sib, far[chunks], fwd[chunks], gain, w, filt, fac, span, end, prior, other, tail),
        flops=2 * n * D * 3 * chans,
    )
    qs.append(q)
    if contexts <= 4:
        before = [shifted(end_state, "context", d) for d in range(1, contexts)]
    else:
        every = lax.all_gather(end_state.reshape(groups, poles, LANES), "context")
        gaps = position - 1.0 - jnp.arange(contexts, dtype=F32)
        rates = dec.reshape(poles, groups, LANES).transpose(1, 0, 2)
        weights = jnp.where(
            (gaps >= 0.0)[:, None, None, None],
            jnp.exp(-rates[None] * count * jnp.maximum(gaps, 0.0)[:, None, None, None]),
            0.0,
        )
        before = [jnp.sum(weights * every, axis=0).reshape(groups * poles, LANES)]
    z, begin = call(
        functools.partial(starts_kernel, chunks, seg),
        [sds(*plane), sds(chunks, *tile)],
        [],
        (fac, rin, scan, skip, p, *ends),
        flops=1 << 30,
    )
    zs.append(z)
    return call(
        functools.partial(final_kernel, chunks, seg, len(before)),
        sds(count, chans, dtype=BF16),
        [pltpu.VMEM((chunks * groups, tokens, LANES), F32), pltpu.VMEM((groups, poles, LANES), F32)],
        (fac, reach, begin, inj, from_cache, jump, *before, *qs, *zs),
    )


def solution(mesh):
    placed = (
        P(("groups", "context"), "tensor"),
        P(),
        P(None, None, "tensor"),
        P(None, None, "tensor"),
        P("groups", None, "tensor"),
        P("tensor", None),
        P("tensor", None),
        P("tensor"),
        P(("groups", "tensor"), None),
    )
    return jax.shard_map(
        local,
        mesh=mesh,
        in_specs=placed,
        out_specs=P(("groups", "context"), "tensor"),
        check_vma=False,
    )
```

time: 222 us -> 77.2 us (0.35)
  matrix products: 57.7 us -> 0 us
  local copies, waits for them, and re-layouts: 59 us -> 22.1 us
  other arithmetic: 38.8 us -> 2.04 us
  Pallas kernels: 0 us -> 26.5 us
  blocking collectives: 22.7 us -> 0 us
  waiting for transfers between devices: 24.5 us -> 5.48 us
  starting transfers between devices: 3.57 us -> 20 us
  between operations: 13.5 us -> 0.22 us
    dot_general x4 -> x0, matrix products: 57.7 us -> none  [the longest x1 29.9 us: local(): local_out = jnp.einsum('ctj,kjc->ktc', table, signal, precision=HIGH)]
    gather x2 -> x0, local copies, waits for them, and re-layouts: 33 us -> none  [local(): impulse[:, jnp.maximum(lag_index, 0)]]
    pallas_call x0 -> x8, Pallas kernels: none -> 26.5 us  [call(): pl.pallas_call(kernel, out_shape=outs, in_specs=[VM] * len(args), out_spe...]
    all_gather x1 -> x0, waiting for transfers between devices: 24.5 us -> none  [local(): lax.all_gather(normed, 'tensor', axis=1, tiled=True)]
    ppermute x1 -> x15, starting transfers between devices: 3.57 us -> 20 us  [the longest x4 11.7 us: shifted(): lax.ppermute(block, axis, [(i - distance, i) for i in range(distance, siz...]
    all_gather x1 -> x0, blocking collectives: 14.3 us -> none  [local(): every = lax.all_gather(ending[None], 'context', axis=0, tiled=True)]
    add x10 -> x0, other arithmetic: 13.9 us -> none  [the longest x1 6.93 us: local(): featured + short_filter[offset] * extended[offset:offset + count].astype(...]
    unnamed x26 -> x36, local copies, waits for them, and re-layouts: 6 us -> 15.4 us
  transfers between devices with their start and end apart: 2 -> 15, of which waited for: 1 -> 2; matrix products, arithmetic and copies ran while one was open for 24% -> 11% of each run, Pallas kernels for 0% -> 25%
where the time goes in v1:
time: 77.2 us; the launch traced here: 76.3 us
  Pallas kernels  26.5 us (34%)
  local copies, waits for them, and re-layouts  22.1 us (29%)
  starting transfers between devices  20 us (26%)
  waiting for transfers between devices  5.48 us (7%)
  other arithmetic  2.04 us (3%)
    pallas_call x8, Pallas kernels, call(): pl.pallas_call(kernel, out_shape=outs, in_specs=[VM] * len(args), out_spe...  26.5 us
    unnamed x36, local copies, waits for them, and re-layouts  15.4 us
    ppermute x4, starting transfers between devices, shifted(): lax.ppermute(block, axis, [(i - distance, i) for i in range(distance, siz...  11.7 us
    ppermute x11, starting transfers between devices, flipped(): return lax.ppermute(block, 'tensor', [(i, i ^ bit) for i in range(size)])  8.32 us
    ppermute x11, waiting for transfers between devices, flipped(): return lax.ppermute(block, 'tensor', [(i, i ^ bit) for i in range(size)])  5.31 us
    slice x3, local copies, waits for them, and re-layouts, local(): far = [flipped(hidden[a:a + n], 2) for a, n in bounds]  4.36 us
    transpose x2, local copies, waits for them, and re-layouts, local(): other = cache.reshape(HALO, 3 * groups, LANES).transpose(1, 0, 2)  2.34 us
  transfers between devices with their start and end apart: 15, of which 2 were waited for; matrix products, arithmetic and copies ran while one was open for 11% of the time, Pallas kernels for 25%

profile of v1, /device:TPU:0, one launch (start us, length us, event | category | flops | bytes accessed | tf_op | source)
XLA Modules:
  0.0 76.3 jit_solution(2692653589291149191)
XLA Ops:
  0.6 2.0 %fusion = (bf16[128,1024]{1,0:T(8,128)(2,1)}, bf16[128,1024]{1,0:T(8,128)(2,1)S(1)}, bf16[128,1024]{1,0:T(8,128)(2,1)}) fusion(bf16[512,1024]{1,0:T(8,128)(2,1)} %h_ref.9), kind=kLoop, calls=%fused_computation.5 | loop fusion | bytes 1572864 | tf_op jit(solution)/shard_map/slice | solution.py:283
  2.5 2.6 %collective-permute-start.7 = (bf16[128,1024]{1,0:T(8,128)(2,1)}, bf16[128,1024]{1,0:T(8,128)(2,1)S(1)}, u32[]{:S(2)}, u32[]{:S(2)}) collective-permute-start(bf16[128,1024]{1,0:T(8,128)(2,1)} %get-tuple-element.61), channel_id=1, source_target_pairs={{0,2},{1,3},{2,0},{3,1},{4,6},{5,7},{6,4},{7,5},{8,10},{9,11},{10,... | collective-permute-start | bytes 786440 | tf_op jit(solution)/shard_map/ppermute | solution.py:29
  5.1 0.8 slice.19
  5.9 2.0 %collective-permute-start.5 = (bf16[128,1024]{1,0:T(8,128)(2,1)S(1)}, bf16[128,1024]{1,0:T(8,128)(2,1)S(1)}, u32[]{:S(2)}, u32[]{:S(2)}) collective-permute-start(bf16[128,1024]{1,0:T(8,128)(2,1)S(1)} %get-tuple-element.62), channel_id=1, source_target_pairs={{0,2},{1,3},{2,0},{3,1},{4,6},{5,7},{6,4},{7,5},{8,10},{9,11},{10,... | collective-permute-start | bytes 786440 | tf_op jit(solution)/shard_map/ppermute | solution.py:29
  7.9 5.3 %collective-permute-done.9.far_ref = bf16[16,1024]{1,0:T(8,128)(2,1)S(1)} collective-permute-done((bf16[16,1024]{1,0:T(8,128)(2,1)S(1)}, bf16[16,1024]{1,0:T(8,128)(2,1)S(1)}, u32[]{:S(2)}, u32[]{:S(2)}) %collective-permute-start.9) | collective-permute-done | bytes 32800 | tf_op jit(solution)/shard_map/ppermute | solution.py:29
  13.2 2.0 %collective-permute-start.3 = (bf16[128,1024]{1,0:T(8,128)(2,1)}, bf16[128,1024]{1,0:T(8,128)(2,1)S(1)}, u32[]{:S(2)}, u32[]{:S(2)}) collective-permute-start(bf16[128,1024]{1,0:T(8,128)(2,1)} %get-tuple-element.63), channel_id=1, source_target_pairs={{0,2},{1,3},{2,0},{3,1},{4,6},{5,7},{6,4},{7,5},{8,10},{9,11},{10,... | collective-permute-start | bytes 786440 | tf_op jit(solution)/shard_map/ppermute | solution.py:29
  15.2 1.6 %slice.15 = bf16[112,1024]{1,0:T(8,128)(2,1)} slice(bf16[512,1024]{1,0:T(8,128)(2,1)} %h_ref.9), slice={[384:496], [0:1024]} | slice | bytes 458752 | tf_op jit(solution)/shard_map/slice | solution.py:283
  16.8 0.6 copy-done.13
  17.7 1.4 %multiply_exponential_fusion = (f32[16,512]{1,0:T(8,128)S(1)}, f32[16,512]{1,0:T(8,128)S(1)}, f32[16,512]{1,0:T(8,128)}) fusion(f32[512,16]{0,1:T(8,128)} %param.14, f32[512,16]{0,1:T(8,128)} %param.17, f32[]{:T(128)S(6)} %mul.26), kind=kLoop, calls=%fused_computation.2 | loop fusion | flops 49152 | bytes 163844 | tf_op jit(solution)/shard_map/exp | solution.py:293
  19.4 4.6 %copy-done = bf16[4096,3,512]{2,0,1:T(8,128)(2,1)S(1)} copy-done((bf16[4096,3,512]{2,0,1:T(8,128)(2,1)S(1)}, bf16[4096,3,512]{2,0,1:T(8,128)(2,1)}, u32[]{:S(2)}) %copy-start) | copy-done | bytes 12582936
  24.0 1.2 %copy-done.2 = bf16[512,1024]{1,0:T(8,128)(2,1)S(1)} copy-done((bf16[512,1024]{1,0:T(8,128)(2,1)S(1)}, bf16[512,1024]{1,0:T(8,128)(2,1)}, u32[]{:S(2)}) %copy-start.2) | copy-done | bytes 1048600
  25.2 0.7 copy-done.5
  26.0 0.8 copy-done.12
  26.7 0.8 copy-done.14
  27.5 3.1 %shard_map.92 = (f32[12,16,128]{2,1,0:T(8,128)S(1)}, bf16[12,8,128]{2,1,0:T(8,128)(2,1)}) custom-call(bf16[512,1024]{1,0:T(8,128)(2,1)S(1)} %copy-done.2, bf16[512,1024]{1,0:T(8,128)(2,1)S(1)} %collective-permute-done.sib_ref, bf16[16,1024]{1,0:T(8,128)(2,1)S(1)} %copy-done.12, bf16[16,1024]{1,0:T(8,128)(2,1)S(1)} %copy-done.14, f32[1,4096]{1,0:T(1,128)S(1)} %bitcast.23, ...), custom_call_target="tpu_custom_call" | custom-call | flops 201326592 | bytes 1048576 | tf_op jit(solution)/shard_map/pallas_call | solution.py:33
  30.6 0.6 copy-done.9
  31.2 4.5 %collective-permute-start.11 = (bf16[12,8,128]{2,1,0:T(8,128)(2,1)}, bf16[12,8,128]{2,1,0:T(8,128)(2,1)}, u32[]{:S(2)}, u32[]{:S(2)}) collective-permute-start(bf16[12,8,128]{2,1,0:T(8,128)(2,1)} %get-tuple-element.39), channel_id=1, source_target_pairs={{0,4},{4,8},{8,12},{1,5},{5,9},{9,13},{2,6},{6,10},{10,14},{3,7},{... | collective-permute-start | bytes 73736 | tf_op jit(solution)/shard_map/ppermute | solution.py:24
  35.8 0.6 pad_convert_fusion
  36.4 1.5 %reshape.5 = f32[8,12,128]{2,1,0:T(8,128)} reshape(f32[8,3,512]{2,1,0:T(4,128)} %pad_convert_fusion) | data formatting | bytes 98304 | tf_op jit(solution)/shard_map/transpose | solution.py:316
  37.9 0.9 %copy.12 = f32[8,12,128]{2,0,1:T(8,128)S(1)} copy(f32[8,12,128]{2,1,0:T(8,128)} %reshape.5) | data formatting | bytes 98304 | tf_op jit(solution)/shard_map/transpose | solution.py:316
  38.8 0.7 copy-done.8
  39.5 0.8 copy-done.15
  41.3 4.6 %copy-done.1 = bf16[4096,3,512]{2,0,1:T(8,128)(2,1)S(1)} copy-done((bf16[4096,3,512]{2,0,1:T(8,128)(2,1)S(1)}, bf16[4096,3,512]{2,0,1:T(8,128)(2,1)}, u32[]{:S(2)}) %copy-start.1) | copy-done | bytes 12582936
  45.9 5.2 %shard_map.93 = (f32[4,128,128]{2,1,0:T(8,128)S(1)}, f32[4,128,128]{2,1,0:T(8,128)S(1)}, f32[4,16,8,128]{3,2,1,0:T(8,128)S(1)}, f32[4,16,8,128]{3,2,1,0:T(8,128)S(1)}, f32[12,8,128]{2,1,0:T(8,128)S(1)}) custom-call(bf16[512,1024]{1,0:T(8,128)(2,1)S(1)} %copy-done.3, bf16[512,1024]{1,0:T(8,128)(2,1)S(1)} %collective-permute-done.sib_ref, ...), custom_call_target="tpu_custom_call" | custom-call | flops 1610612736 | bytes 1048576 | tf_op jit(solution)/shard_map/pallas_call | solution.py:33
  51.1 4.5 %shard_map.94 = (f32[4,128,128]{2,1,0:T(8,128)S(1)}, f32[4,128,128]{2,1,0:T(8,128)S(1)}, f32[4,16,8,128]{3,2,1,0:T(8,128)S(1)}, f32[4,16,8,128]{3,2,1,0:T(8,128)S(1)}, f32[12,8,128]{2,1,0:T(8,128)S(1)}) custom-call(bf16[512,1024]{1,0:T(8,128)(2,1)S(1)} %copy-done.3, bf16[512,1024]{1,0:T(8,128)(2,1)S(1)} %collective-permute-done.sib_ref, ...), custom_call_target="tpu_custom_call" | custom-call | flops 1610612736 | bytes 1048576 | tf_op jit(solution)/shard_map/pallas_call | solution.py:33
  55.6 4.5 %shard_map.95 = (f32[4,128,128]{2,1,0:T(8,128)S(1)}, f32[4,128,128]{2,1,0:T(8,128)S(1)}, f32[4,16,8,128]{3,2,1,0:T(8,128)S(1)}, f32[4,16,8,128]{3,2,1,0:T(8,128)S(1)}, f32[12,8,128]{2,1,0:T(8,128)S(1)}) custom-call(bf16[512,1024]{1,0:T(8,128)(2,1)S(1)} %copy-done.3, bf16[512,1024]{1,0:T(8,128)(2,1)S(1)} %collective-permute-done.sib_ref, ...), custom_call_target="tpu_custom_call" | custom-call | flops 1610612736 | bytes 1048576 | tf_op jit(solution)/shard_map/pallas_call | solution.py:33
  60.1 5.1 %shard_map.96 = (f32[4,128,128]{2,1,0:T(8,128)S(1)}, f32[4,128,128]{2,1,0:T(8,128)S(1)}, f32[64,128]{1,0:T(8,128)S(1)}) custom-call(bf16[512,1024]{1,0:T(8,128)(2,1)S(1)} %copy-done.3, bf16[512,1024]{1,0:T(8,128)(2,1)S(1)} %collective-permute-done.sib_ref, bf16[112,1024]{1,0:T(8,128)(2,1)} %collective-permute-done.1.far_ref, ...), custom_call_target="tpu_custom_call" | custom-call | flops 1409286144 | bytes 1048576 | tf_op jit(solution)/shard_map/pallas_call | solution.py:33
  65.2 2.9 %collective-permute-start.12 = (f32[64,128]{1,0:T(8,128)S(1)}, f32[64,128]{1,0:T(8,128)S(1)}, u32[]{:S(2)}, u32[]{:S(2)}) collective-permute-start(f32[64,128]{1,0:T(8,128)S(1)} %get-tuple-element.52), channel_id=1, source_target_pairs={{0,4},{4,8},{8,12},{1,5},{5,9},{9,13},{2,6},{6,10},{10,14},{3,7},{... | collective-permute-start | bytes 98312 | tf_op jit(solution)/shard_map/ppermute | solution.py:24
  68.1 2.9 %collective-permute-start.13 = (f32[64,128]{1,0:T(8,128)S(1)}, f32[64,128]{1,0:T(8,128)S(1)}, u32[]{:S(2)}, u32[]{:S(2)}) collective-permute-start(f32[64,128]{1,0:T(8,128)S(1)} %get-tuple-element.52), channel_id=1, source_target_pairs={{0,8},{4,12},{1,9},{5,13},{2,10},{6,14},{3,11},{7,15},{16,24},{20,... | collective-permute-start | bytes 98312 | tf_op jit(solution)/shard_map/ppermute | solution.py:24
  71.0 1.3 %collective-permute-start.14 = (f32[64,128]{1,0:T(8,128)S(1)}, f32[64,128]{1,0:T(8,128)S(1)}, u32[]{:S(2)}, u32[]{:S(2)}) collective-permute-start(f32[64,128]{1,0:T(8,128)S(1)} %get-tuple-element.52), channel_id=1, source_target_pairs={{0,12},{1,13},{2,14},{3,15},{16,28},{17,29},{18,30},{19,31}} | collective-permute-start | bytes 98312 | tf_op jit(solution)/shard_map/ppermute | solution.py:24
  72.3 1.4 %shard_map.97 = (f32[4,128,128]{2,1,0:T(8,128)S(1)}, f32[4,4,16,8,128]{4,3,2,1,0:T(8,128)S(1)}) custom-call(f32[4,16,8,128]{3,2,1,0:T(8,128)S(1)} %get-tuple-element.33.fac_ref, f32[4,16,8,128]{3,2,1,0:T(8,128)S(1)} %get-tuple-element.35.rin_ref, f32[3,4,16,8,128]{4,3,2,1,0:T(8,128)S(1)} %get-tuple-element.36.scan_ref, f32[1,512]{1,0:T(1,128)S(1)} %bitcast.34, ...), custom_call_target="tpu_custom_call" | custom-call | flops 1073741824 | bytes 1048576 | tf_op jit(solution)/shard_map/pallas_call | solution.py:33
  73.9 2.4 %shard_map.98 = bf16[512,512]{1,0:T(8,128)(2,1)} custom-call(f32[4,16,8,128]{3,2,1,0:T(8,128)S(1)} %get-tuple-element.33.fac_ref, f32[4,4,16,8,128]{4,3,2,1,0:T(8,128)S(1)} %get-tuple-element.34.reach_ref, f32[4,4,16,8,128]{4,3,2,1,0:T(8,128)S(1)} %get-tuple-element.51.begin_ref, f32[16,512]{1,0:T(8,128)S(1)} %get-tuple-element.65.inj_ref, ...), custom_call_target="tpu_custom_call" | custom-call | bytes 1048576 | tf_op jit(solution)/shard_map/pallas_call | solution.py:33
  (49 shorter events, 2.4 us)
Async XLA Ops:
  0.0 41.3 %copy-start.3 = (bf16[512,1024]{1,0:T(8,128)(2,1)S(1)}, bf16[512,1024]{1,0:T(8,128)(2,1)}, u32[]{:S(2)}) copy-start(bf16[512,1024]{1,0:T(8,128)(2,1)} %h_ref.9) | copy-start | bytes 3145732
  0.0 41.3 %copy-start.6 = (f32[4096]{0:T(1024)S(1)}, f32[4096]{0:T(1024)}, u32[]{:S(2)}) copy-start(f32[4096]{0:T(1024)} %param.10) | copy-start | bytes 49156
  0.0 41.3 %copy-start.16 = (f32[512]{0:T(512)S(1)}, f32[512]{0:T(512)}, u32[]{:S(2)}) copy-start(f32[512]{0:T(512)} %param.16) | copy-start | bytes 6148
  0.0 41.3 %copy-start.4 = (f32[7,3,512]{2,0,1:T(8,128)S(1)}, f32[7,3,512]{2,0,1:T(8,128)}, u32[]{:S(2)}) copy-start(f32[7,3,512]{2,0,1:T(8,128)} %param.12) | copy-start | bytes 129028
  0.0 19.4 %collective-permute-start = (bf16[512,1024]{1,0:T(8,128)(2,1)}, bf16[512,1024]{1,0:T(8,128)(2,1)S(1)}, u32[]{:S(2)}, u32[]{:S(2)}) collective-permute-start(bf16[512,1024]{1,0:T(8,128)(2,1)} %h_ref.9), channel_id=1, source_target_pairs={{0,1},{1,0},{2,3},{3,2},{4,5},{5,4},{6,7},{7,6},{8,9},{9,8},{10,11... | collective-permute-start | bytes 3145736 | tf_op jit(solution)/shard_map/ppermute | solution.py:29
  2.5 14.9 %collective-permute-start.7 = (bf16[128,1024]{1,0:T(8,128)(2,1)}, bf16[128,1024]{1,0:T(8,128)(2,1)S(1)}, u32[]{:S(2)}, u32[]{:S(2)}) collective-permute-start(bf16[128,1024]{1,0:T(8,128)(2,1)} %get-tuple-element.61), channel_id=1, source_target_pairs={{0,2},{1,3},{2,0},{3,1},{4,6},{5,7},{6,4},{7,5},{8,10},{9,11},{10,... | collective-permute-start | bytes 786440 | tf_op jit(solution)/shard_map/ppermute | solution.py:29
  5.9 7.3 %collective-permute-start.9 = (bf16[16,1024]{1,0:T(8,128)(2,1)S(1)}, bf16[16,1024]{1,0:T(8,128)(2,1)S(1)}, u32[]{:S(2)}, u32[]{:S(2)}) collective-permute-start(bf16[16,1024]{1,0:T(8,128)(2,1)S(1)} %slice.19), channel_id=1, source_target_pairs={{0,2},{1,3},{2,0},{3,1},{4,6},{5,7},{6,4},{7,5},{8,10},{9,11},{10,... | collective-permute-start | bytes 98312 | tf_op jit(solution)/shard_map/ppermute | solution.py:29
  5.9 13.3 %collective-permute-start.5 = (bf16[128,1024]{1,0:T(8,128)(2,1)S(1)}, bf16[128,1024]{1,0:T(8,128)(2,1)S(1)}, u32[]{:S(2)}, u32[]{:S(2)}) collective-permute-start(bf16[128,1024]{1,0:T(8,128)(2,1)S(1)} %get-tuple-element.62), channel_id=1, source_target_pairs={{0,2},{1,3},{2,0},{3,1},{4,6},{5,7},{6,4},{7,5},{8,10},{9,11},{10,... | collective-permute-start | bytes 786440 | tf_op jit(solution)/shard_map/ppermute | solution.py:29
  13.2 4.3 %copy-start.11 = (bf16[16,1024]{1,0:T(8,128)(2,1)}, bf16[16,1024]{1,0:T(8,128)(2,1)S(1)}, u32[]{:S(2)}) copy-start(bf16[16,1024]{1,0:T(8,128)(2,1)S(1)} %collective-permute-done.9.far_ref) | copy-start | bytes 98308
  13.2 3.7 %collective-permute-start.10 = (bf16[16,1024]{1,0:T(8,128)(2,1)S(1)}, bf16[16,1024]{1,0:T(8,128)(2,1)S(1)}, u32[]{:S(2)}, u32[]{:S(2)}) collective-permute-start(bf16[16,1024]{1,0:T(8,128)(2,1)S(1)} %collective-permute-done.9.far_ref), channel_id=1, source_target_pairs={{0,1},{1,0},{2,3},{3,2},{4,5},{5,4},{6,7},{7,6},{8,9},{9,8},{10,11... | collective-permute-start | bytes 98312 | tf_op jit(solution)/shard_map/ppermute | solution.py:29
  13.2 27.6 %collective-permute-start.3 = (bf16[128,1024]{1,0:T(8,128)(2,1)}, bf16[128,1024]{1,0:T(8,128)(2,1)S(1)}, u32[]{:S(2)}, u32[]{:S(2)}) collective-permute-start(bf16[128,1024]{1,0:T(8,128)(2,1)} %get-tuple-element.63), channel_id=1, source_target_pairs={{0,2},{1,3},{2,0},{3,1},{4,6},{5,7},{6,4},{7,5},{8,10},{9,11},{10,... | collective-permute-start | bytes 786440 | tf_op jit(solution)/shard_map/ppermute | solution.py:29
  16.8 18.9 %copy-start.17 = (bf16[6,3,512]{2,1,0:T(4,128)(2,1)S(1)}, bf16[6,3,512]{2,1,0:T(4,128)(2,1)}, u32[]{:S(2)}) copy-start(bf16[6,3,512]{2,1,0:T(4,128)(2,1)} %param.13) | copy-start | bytes 55300
  17.4 23.2 %collective-permute-start.1 = (bf16[112,1024]{1,0:T(8,128)(2,1)}, bf16[112,1024]{1,0:T(8,128)(2,1)}, u32[]{:S(2)}, u32[]{:S(2)}) collective-permute-start(bf16[112,1024]{1,0:T(8,128)(2,1)} %slice.15), channel_id=1, source_target_pairs={{0,2},{1,3},{2,0},{3,1},{4,6},{5,7},{6,4},{7,5},{8,10},{9,11},{10,... | collective-permute-start | bytes 688136 | tf_op jit(solution)/shard_map/ppermute | solution.py:29
  17.5 23.8 %collective-permute-start.8 = (bf16[128,1024]{1,0:T(8,128)(2,1)S(1)}, bf16[128,1024]{1,0:T(8,128)(2,1)S(1)}, u32[]{:S(2)}, u32[]{:S(2)}) collective-permute-start(bf16[128,1024]{1,0:T(8,128)(2,1)S(1)} %collective-permute-done.7.far_ref), channel_id=1, source_target_pairs={{0,1},{1,0},{2,3},{3,2},{4,5},{5,4},{6,7},{7,6},{8,9},{9,8},{10,11... | collective-permute-start | bytes 786440 | tf_op jit(solution)/shard_map/ppermute | solution.py:29
  19.1 31.9 %collective-permute-start.6 = (bf16[128,1024]{1,0:T(8,128)(2,1)S(1)}, bf16[128,1024]{1,0:T(8,128)(2,1)S(1)}, u32[]{:S(2)}, u32[]{:S(2)}) collective-permute-start(bf16[128,1024]{1,0:T(8,128)(2,1)S(1)} %collective-permute-done.5.far_ref), channel_id=1, source_target_pairs={{0,1},{1,0},{2,3},{3,2},{4,5},{5,4},{6,7},{7,6},{8,9},{9,8},{10,11... | collective-permute-start | bytes 786440 | tf_op jit(solution)/shard_map/ppermute | solution.py:29
  19.4 4.6 %copy-start = (bf16[4096,3,512]{2,0,1:T(8,128)(2,1)S(1)}, bf16[4096,3,512]{2,0,1:T(8,128)(2,1)}, u32[]{:S(2)}) copy-start(bf16[4096,3,512]{2,0,1:T(8,128)(2,1)} %param.11) | copy-start | bytes 37748740
  24.0 1.2 %copy-start.2 = (bf16[512,1024]{1,0:T(8,128)(2,1)S(1)}, bf16[512,1024]{1,0:T(8,128)(2,1)}, u32[]{:S(2)}) copy-start(bf16[512,1024]{1,0:T(8,128)(2,1)} %h_ref.9) | copy-start | bytes 3145732
  25.2 0.7 copy-start.5
  26.0 0.8 copy-start.12
  26.7 0.8 copy-start.14
  30.6 0.6 copy-start.9
  31.2 10.0 %collective-permute-start.11 = (bf16[12,8,128]{2,1,0:T(8,128)(2,1)}, bf16[12,8,128]{2,1,0:T(8,128)(2,1)}, u32[]{:S(2)}, u32[]{:S(2)}) collective-permute-start(bf16[12,8,128]{2,1,0:T(8,128)(2,1)} %get-tuple-element.39), channel_id=1, source_target_pairs={{0,4},{4,8},{8,12},{1,5},{5,9},{9,13},{2,6},{6,10},{10,14},{3,7},{... | collective-permute-start | bytes 73736 | tf_op jit(solution)/shard_map/ppermute | solution.py:24
  38.7 0.8 copy-start.8
  39.5 0.8 copy-start.15
  40.7 19.4 %collective-permute-start.2 = (bf16[112,1024]{1,0:T(8,128)(2,1)}, bf16[112,1024]{1,0:T(8,128)(2,1)S(1)}, u32[]{:S(2)}, u32[]{:S(2)}) collective-permute-start(bf16[112,1024]{1,0:T(8,128)(2,1)} %collective-permute-done.1.far_ref), channel_id=1, source_target_pairs={{0,1},{1,0},{2,3},{3,2},{4,5},{5,4},{6,7},{7,6},{8,9},{9,8},{10,11... | collective-permute-start | bytes 688136 | tf_op jit(solution)/shard_map/ppermute | solution.py:29
  40.8 14.8 %collective-permute-start.4 = (bf16[128,1024]{1,0:T(8,128)(2,1)S(1)}, bf16[128,1024]{1,0:T(8,128)(2,1)S(1)}, u32[]{:S(2)}, u32[]{:S(2)}) collective-permute-start(bf16[128,1024]{1,0:T(8,128)(2,1)S(1)} %collective-permute-done.3.far_ref), channel_id=1, source_target_pairs={{0,1},{1,0},{2,3},{3,2},{4,5},{5,4},{6,7},{7,6},{8,9},{9,8},{10,11... | collective-permute-start | bytes 786440 | tf_op jit(solution)/shard_map/ppermute | solution.py:29
  41.3 4.6 %copy-start.1 = (bf16[4096,3,512]{2,0,1:T(8,128)(2,1)S(1)}, bf16[4096,3,512]{2,0,1:T(8,128)(2,1)}, u32[]{:S(2)}) copy-start(bf16[4096,3,512]{2,0,1:T(8,128)(2,1)} %param.11) | copy-start | bytes 37748740
  51.1 9.0 %copy-start.10 = (f32[12,16,128]{2,1,0:T(8,128)S(1)}, f32[12,16,128]{2,1,0:T(8,128)}, u32[]{:S(2)}) copy-start(f32[12,16,128]{2,1,0:T(8,128)} %copy-done.9) | copy-start | bytes 294916
  60.1 13.8 %copy-start.7 = (f32[16,512]{1,0:T(8,128)S(1)}, f32[16,512]{1,0:T(8,128)}, u32[]{:S(2)}) copy-start(f32[16,512]{1,0:T(8,128)} %get-tuple-element.66.from_cache_ref) | copy-start | bytes 98308
  65.2 8.5 %collective-permute-start.12 = (f32[64,128]{1,0:T(8,128)S(1)}, f32[64,128]{1,0:T(8,128)S(1)}, u32[]{:S(2)}, u32[]{:S(2)}) collective-permute-start(f32[64,128]{1,0:T(8,128)S(1)} %get-tuple-element.52), channel_id=1, source_target_pairs={{0,4},{4,8},{8,12},{1,5},{5,9},{9,13},{2,6},{6,10},{10,14},{3,7},{... | collective-permute-start | bytes 98312 | tf_op jit(solution)/shard_map/ppermute | solution.py:24
  68.1 5.6 %collective-permute-start.13 = (f32[64,128]{1,0:T(8,128)S(1)}, f32[64,128]{1,0:T(8,128)S(1)}, u32[]{:S(2)}, u32[]{:S(2)}) collective-permute-start(f32[64,128]{1,0:T(8,128)S(1)} %get-tuple-element.52), channel_id=1, source_target_pairs={{0,8},{4,12},{1,9},{5,13},{2,10},{6,14},{3,11},{7,15},{16,24},{20,... | collective-permute-start | bytes 98312 | tf_op jit(solution)/shard_map/ppermute | solution.py:24
  71.0 2.9 %collective-permute-start.14 = (f32[64,128]{1,0:T(8,128)S(1)}, f32[64,128]{1,0:T(8,128)S(1)}, u32[]{:S(2)}, u32[]{:S(2)}) collective-permute-start(f32[64,128]{1,0:T(8,128)S(1)} %get-tuple-element.52), channel_id=1, source_target_pairs={{0,12},{1,13},{2,14},{3,15},{16,28},{17,29},{18,30},{19,31}} | collective-permute-start | bytes 98312 | tf_op jit(solution)/shard_map/ppermute | solution.py:24
  (1 other events, 0.6 us)

commit v2 on v1

v2 whole, which is shorter than its diff:
```python
import functools

import jax
import jax.numpy as jnp
from jax import lax
from jax.experimental import pallas as pl
from jax.experimental.pallas import tpu as pltpu
from jax.sharding import PartitionSpec as P

D = 4096
EPS = 1e-06
LANES = 128
SEGS = 8
TAIL = 16
HALO = 8

VM = pl.BlockSpec(memory_space=pltpu.VMEM)
F32 = jnp.float32
BF16 = jnp.bfloat16


def shifted(block, axis, distance):
    size = lax.axis_size(axis)
    return lax.ppermute(block, axis, [(i - distance, i) for i in range(distance, size)])


def flipped(block, bit):
    size = lax.axis_size("tensor")
    return lax.ppermute(block, "tensor", [(i, i ^ bit) for i in range(size)])


def call(kernel, outs, scratch, args, flops=0, limit=12, anywhere=()):
    specs = [pl.BlockSpec(memory_space=pltpu.HBM) if i in anywhere else VM for i in range(len(args))]
    args = [pltpu.with_memory_space_constraint(x, pltpu.HBM) if i in anywhere else x for i, x in enumerate(args)]
    return pl.pallas_call(
        kernel,
        out_shape=outs,
        in_specs=specs,
        out_specs=jax.tree.map(lambda _: VM, outs, is_leaf=lambda o: hasattr(o, "dtype")),
        scratch_shapes=scratch,
        cost_estimate=pl.CostEstimate(flops=flops, bytes_accessed=1024, transcendentals=0),
        compiler_params=pltpu.CompilerParams(vmem_limit_bytes=limit << 20),
    )(*args)


def kept(*shape, dtype=F32):
    return pltpu.VMEM(shape, dtype)


def sds(*shape, dtype=F32):
    return jax.ShapeDtypeStruct(shape, dtype)


def open_kernel(pieces, h_any, *refs):
    *out_refs, sem = refs
    copies, which = [], 0
    for parts, out_ref in zip(pieces, out_refs):
        at = 0
        for start, rows in parts:
            copies.append(
                pltpu.make_async_copy(
                    h_any.at[start : start + rows, :], out_ref.at[at : at + rows, :], sem.at[which]
                )
            )
            at += rows
            which += 1
    for copy in copies:
        copy.start()
    for copy in copies:
        copy.wait()


def stage_kernel(
    seg, chunks, w_any, dec_ref, res_ref, inj_ref,
    w_ref, fac_ref, rin_ref, scan_ref, span_ref, end_ref, reach_ref, sem,
):
    copies = [pltpu.make_async_copy(w_any, w_ref, sem.at[0])]
    for copy in copies:
        copy.start()
    groups, poles = fac_ref.shape[0], fac_ref.shape[1]
    row = lax.broadcasted_iota(jnp.int32, (SEGS, LANES), 0)
    rowf = row.astype(F32)

    def body(g, c):
        lanes = pl.ds(pl.multiple_of(g * LANES, LANES), LANES)
        for n in range(poles):
            dec = jnp.broadcast_to(dec_ref[n : n + 1, lanes], (SEGS, LANES))
            res = jnp.broadcast_to(res_ref[n : n + 1, lanes], (SEGS, LANES))
            inj = jnp.broadcast_to(inj_ref[n : n + 1, lanes], (SEGS, LANES))
            fac_ref[g, n] = jnp.exp(-dec)
            rin_ref[g, n] = res * inj
            for b, step in enumerate((1, 2, 4)):
                scan_ref[b, g, n] = jnp.where(row >= step, jnp.exp(-dec * float(seg * step)), 0.0)
            span_ref[g, n] = jnp.exp(-dec * float(seg * SEGS))
            end_ref[g, n] = jnp.exp(-dec * ((SEGS - 1.0 - rowf) * float(seg)))
            for k in range(chunks):
                reach_ref[k, g, n] = res * jnp.exp(-dec * (1.0 + float(seg) * (float(SEGS * k) + rowf)))
        return c

    lax.fori_loop(0, groups, body, 0)
    for copy in copies:
        copy.wait()


def project(parts, h_ref, sib_ref, far_ref, fwd_ref, gain_ref, w_ref, normed_ref, put):
    t = lax.axis_index("tensor")
    width = h_ref.shape[1]
    groups = w_ref.shape[2] // LANES
    at = 0
    for start, rows in parts:
        here = slice(at, at + rows)
        at += rows
        blocks = (
            (t, h_ref, here),
            (t ^ 1, sib_ref, slice(start, start + rows)),
            (t ^ 2, far_ref, here),
            (t ^ 3, fwd_ref, here),
        )
        squares = jnp.zeros((rows, LANES), F32)
        for _, ref, where in blocks:
            block = ref[where, :].astype(F32)
            block = block * block
            for lane in range(0, width, LANES):
                squares = squares + block[:, lane : lane + LANES]
        scale = lax.rsqrt(jnp.sum(squares, axis=1, keepdims=True) / D + EPS)
        for index, ref, where in blocks:
            lanes = pl.ds(pl.multiple_of(index * width, width), width)
            normed_ref[here, lanes] = (ref[where, :].astype(F32) * scale * gain_ref[:, lanes]).astype(BF16)

    halves = groups // 2

    def body(step, c):
        i, half = step // halves, step % halves
        lanes = pl.ds(pl.multiple_of(half * 2 * LANES, 2 * LANES), 2 * LANES)
        streams = jnp.dot(normed_ref[...], w_ref[i, :, lanes], preferred_element_type=F32)
        streams = streams.astype(BF16).astype(F32)
        put(step * 2, streams[:, :LANES])
        put(step * 2 + 1, streams[:, LANES:])
        return c

    lax.fori_loop(0, 3 * halves, body, 0)


def convolve(ext_ref, filt_ref, g, first, tokens, streams=(0, 1, 2)):
    groups = ext_ref.shape[0] // 3
    lanes = pl.ds(pl.multiple_of(g * LANES, LANES), LANES)
    taps = filt_ref.shape[1]
    found = []
    for i in streams:
        total = jnp.zeros((tokens, LANES), F32)
        for k in range(taps):
            rows = pl.ds(first + HALO - taps + 1 + k, tokens)
            total = total + filt_ref[i, k : k + 1, lanes] * ext_ref[i * groups + g, rows, :]
        found.append(total)
    return found


def scan_unit(prod_ref, fac_ref, rin_ref, g, first, seg, out_ref):
    poles = fac_ref.shape[1]
    entry = prod_ref[g, pl.ds(first, SEGS, stride=seg), :]
    state = [entry] * poles
    for j in range(seg):
        rows = pl.ds(first + j, SEGS, stride=seg)
        if j:
            entry = prod_ref[g, rows, :]
            state = [fac_ref[g, n] * state[n] + entry for n in range(poles)]
        if out_ref is not None:
            terms = [rin_ref[g, n] * state[n] for n in range(poles)]
            while len(terms) > 1:
                terms = [a + b for a, b in zip(terms[::2], terms[1::2])]
            out_ref[g, rows, :] = terms[0]
    return state


def head_kernel(
    parts, h_ref, sib_ref, far_ref, fwd_ref, gain_ref, w_ref, tail_ref, send_ref, body_ref, normed_ref
):
    def put(at, streams):
        tail_ref[at] = streams[:TAIL]
        send_ref[at] = streams[TAIL - HALO : TAIL].astype(BF16)
        body_ref[at] = streams[TAIL:]

    project(parts, h_ref, sib_ref, far_ref, fwd_ref, gain_ref, w_ref, normed_ref, put)


def chunk_kernel(
    parts, units, seg, first,
    h_ref, sib_ref, far_ref, fwd_ref, gain_ref, w_ref, filt_ref, fac_ref, rin_ref, span_ref, skip_ref,
    prior_ref, other_ref, body_ref,
    q_ref, z_ref, ends_ref, sum_ref, last_ref,
    ext_ref, normed_ref, prod_ref,
):
    groups, poles = fac_ref.shape[0], fac_ref.shape[1]
    tokens = seg * SEGS
    base = HALO
    if first:
        got = prior_ref[...].astype(F32)
        ext_ref[:, :HALO, :] = jnp.where(lax.axis_index("context") == 0, other_ref[...], got)
        base += body_ref.shape[1]
        ext_ref[:, HALO:base, :] = body_ref[...]
    else:
        ext_ref[:, :HALO, :] = prior_ref[...]
    rows = sum(n for _, n in parts)

    def put(at, streams):
        ext_ref[at, base : base + rows, :] = streams

    project(parts, h_ref, sib_ref, far_ref, fwd_ref, gain_ref, w_ref, normed_ref, put)
    last_ref[...] = ext_ref[:, base + rows - HALO :, :]

    def body(g, c):
        lanes = pl.ds(pl.multiple_of(g * LANES, LANES), LANES)
        for u in range(units):
            here = slice(u * tokens, (u + 1) * tokens)
            query, keyed, value = convolve(ext_ref, filt_ref, g, u * tokens, tokens)
            q_ref[g, here, :] = query
            prod_ref[g, here, :] = keyed * value
            state = scan_unit(prod_ref, fac_ref, rin_ref, g, u * tokens, seg, z_ref)
            for n in range(poles):
                ends_ref[u, g, n] = state[n]
                if u:
                    sum_ref[g, n] = span_ref[g, n] * sum_ref[g, n] + state[n]
                elif first:
                    sum_ref[g, n] = state[n]
                else:
                    sum_ref[g, n] = span_ref[g, n] * other_ref[g, n] + state[n]
        z_ref[g] = z_ref[g] + skip_ref[:, lanes] * prod_ref[g]
        return c

    lax.fori_loop(0, groups, body, 0)


def last_kernel(
    parts, seg,
    h_ref, sib_ref, far_ref, fwd_ref, gain_ref, w_ref, filt_ref, fac_ref, span_ref, end_ref,
    prior_ref, sums_ref, tail_ref,
    q_ref, p_ref, end_state_ref,
    ext_ref, normed_ref,
):
    groups, poles = fac_ref.shape[0], fac_ref.shape[1]
    rows = sum(n for _, n in parts)
    ext_ref[:, :HALO, :] = prior_ref[...]

    def put(at, streams):
        ext_ref[at, HALO : HALO + rows, :] = streams

    project(parts, h_ref, sib_ref, far_ref, fwd_ref, gain_ref, w_ref, normed_ref, put)
    ext_ref[:, HALO + rows :, :] = tail_ref[...]

    def body(g, c):
        query, keyed, value = convolve(ext_ref, filt_ref, g, 0, rows + TAIL)
        q_ref[g] = query
        p_ref[g] = keyed * value
        state = scan_unit(p_ref, fac_ref, None, g, 0, seg, None)
        for n in range(poles):
            whole = end_ref[g, n] * (span_ref[g, n] * sums_ref[g, n] + state[n])
            end_state_ref[pl.ds(g * poles + n, 1), :] = jnp.sum(whole, axis=0, keepdims=True)
        return c

    lax.fori_loop(0, groups, body, 0)


def starts_kernel(chunks, seg, fac_ref, rin_ref, scan_ref, skip_ref, p_ref, *refs):
    *ends_refs, z_ref, begin_ref = refs
    ends_refs = [ref.at[u] for ref in ends_refs for u in range(ref.shape[0])]
    groups, poles = fac_ref.shape[0], fac_ref.shape[1]
    row = lax.broadcasted_iota(jnp.int32, (SEGS, LANES), 0)

    def body(g, c):
        state = scan_unit(p_ref, fac_ref, rin_ref, g, 0, seg, z_ref)
        lanes = pl.ds(pl.multiple_of(g * LANES, LANES), LANES)
        z_ref[g] = z_ref[g] + skip_ref[:, lanes] * p_ref[g]
        for n in range(poles):
            lead = rin_ref[g, n] * fac_ref[g, n]
            step = jnp.broadcast_to(scan_ref[0, g, n, 1:2, :], (SEGS, LANES))
            enter = jnp.zeros((SEGS, LANES), F32)
            for k in range(chunks):
                held = ends_refs[k][g, n] if k < chunks - 1 else state[n]
                held = jnp.where(row == 0, held + step * enter, held)
                for b, by in enumerate((1, 2, 4)):
                    held = held + scan_ref[b, g, n] * pltpu.roll(held, by, 0)
                begin_ref[k, g, n] = lead * jnp.where(row == 0, enter, pltpu.roll(held, 1, 0))
                enter = jnp.broadcast_to(held[SEGS - 1 :, :], (SEGS, LANES))
        return c

    lax.fori_loop(0, groups, body, 0)


def final_kernel(
    chunks, seg, hops, pieces, wrapped, fac_ref, reach_ref, begin_ref, inj_ref, from_cache_ref, jump_ref, *refs
):
    e_refs = refs[:hops]
    q_refs = refs[hops : hops + pieces]
    z_refs = refs[hops + pieces : hops + 2 * pieces]
    out_ref, add_ref, enter_ref = refs[hops + 2 * pieces :]
    groups, poles = fac_ref.shape[0], fac_ref.shape[1]
    tokens = seg * SEGS
    position = lax.axis_index("context")

    def before(e, rows):
        found = e_refs[e][rows, :]
        return jnp.where(position > e, found, 0.0) if wrapped else found

    for g in range(groups):
        lanes = slice(g * LANES, (g + 1) * LANES)
        rows = slice(g * poles, (g + 1) * poles)
        total = before(hops - 1, rows)
        for e in reversed(range(hops - 1)):
            total = total * jump_ref[:, lanes] + before(e, rows)
        enter_ref[g] = inj_ref[:, lanes] * total + from_cache_ref[:, lanes]

    def body(step, c):
        k, g = step // groups, step % groups
        state = []
        for n in range(poles):
            enter = jnp.broadcast_to(enter_ref[g, n : n + 1, :], (SEGS, LANES))
            state.append(begin_ref[k, g, n] + reach_ref[k, g, n] * enter)
        for j in range(seg):
            if j:
                state = [fac_ref[g, n] * state[n] for n in range(poles)]
            terms = state
            while len(terms) > 1:
                terms = [a + b for a, b in zip(terms[::2], terms[1::2])]
            add_ref[step, pl.ds(j, SEGS, stride=seg), :] = terms[0]
        return c

    lax.fori_loop(0, chunks * groups, body, 0)
    k = 0
    for q_ref, z_ref in zip(q_refs, z_refs):
        for u in range(q_ref.shape[1] // tokens):
            here = slice(u * tokens, (u + 1) * tokens)
            for g in range(groups):
                out_ref[k * tokens : (k + 1) * tokens, g * LANES : (g + 1) * LANES] = (
                    q_ref[g, here, :] * (z_ref[g, here, :] + add_ref[k * groups + g])
                ).astype(BF16)
            k += 1


def local(
    hidden, norm_gain, in_proj, short_filter, conv_cache, decay, residues, skip_gain, cached_state
):
    count, width = hidden.shape
    chans = in_proj.shape[2]
    poles = decay.shape[1]
    taps = short_filter.shape[0]
    groups = chans // LANES
    chunks = 4
    tokens = count // chunks
    seg = tokens // SEGS
    position = lax.axis_index("context").astype(F32)
    contexts = lax.axis_size("context")

    head = [(count - TAIL, TAIL), (0, tokens)]
    rest = [[(k * tokens, tokens - (TAIL if k == chunks - 1 else 0))] for k in range(1, chunks)]
    own = call(
        functools.partial(open_kernel, [head] + rest),
        [kept(sum(n for _, n in parts), width, dtype=BF16) for parts in [head] + rest],
        [pltpu.SemaphoreType.DMA((chunks + 1,))],
        (hidden,),
        anywhere=(0,),
    )
    hidden, own = lax.optimization_barrier((hidden, own))
    far = [flipped(block, 2) for block in own]
    sib = flipped(hidden, 1)

    filt = short_filter.transpose(1, 0, 2)
    gain = norm_gain[None]
    skip = skip_gain[None]
    dec, res = decay.T, residues.T
    inj = jnp.sqrt(-jnp.expm1(-2.0 * dec))
    jump = jnp.exp(-dec * count)
    from_cache = jnp.exp(-dec * (count * position)) * cached_state.T
    cache = jnp.pad(conv_cache.astype(F32), ((HALO - taps + 1, 0), (0, 0), (0, 0)))
    cache = cache.reshape(HALO, 3 * groups, LANES).transpose(1, 0, 2)
    tile = (groups, poles, SEGS, LANES)
    w = in_proj.transpose(1, 0, 2)
    w, inj, jump, from_cache, cache = lax.optimization_barrier((w, inj, jump, from_cache, cache))
    w, fac, rin, scan, span, end, reach = call(
        functools.partial(stage_kernel, seg, chunks),
        [
            kept(*w.shape, dtype=BF16), kept(*tile), kept(*tile),
            kept(3, *tile), kept(*tile), kept(*tile), kept(chunks, *tile),
        ],
        [pltpu.SemaphoreType.DMA((1,))],
        (w, dec, res, inj),
        anywhere=(0,),
    )

    def ext(rows):
        return pltpu.VMEM((3 * groups, HALO + rows, LANES), F32)

    halo = (3 * groups, HALO, LANES)
    work = 2 * D * 3 * chans
    fwd = flipped(far[0], 1)
    tail, send, body = call(
        functools.partial(head_kernel, head),
        [sds(3 * groups, TAIL, LANES), sds(*halo, dtype=BF16), sds(3 * groups, tokens, LANES)],
        [pltpu.VMEM((TAIL + tokens, D), BF16)],
        (own[0], sib, far[0], fwd, gain, w),
    )
    prior, other, after = shifted(send, "context", 1), cache, body
    qs, zs, ends = [], [], []
    for k in range(1, chunks - 1):
        (n,) = [n for _, n in rest[k - 1]]
        units = 2 if k == 1 else 1
        plane = (groups, units * tokens, LANES)
        arrived, after = lax.optimization_barrier((far[k], after))
        fwd = flipped(arrived, 1)
        q, z, e, sums, last = call(
            functools.partial(chunk_kernel, rest[k - 1], units, seg, k == 1),
            [sds(*plane), sds(*plane), sds(units, *tile), sds(*tile), sds(*halo)],
            [ext(units * tokens), pltpu.VMEM((n, D), BF16), pltpu.VMEM(plane, F32)],
            (own[k], sib, arrived, fwd, gain, w, filt, fac, rin, span, skip, prior, other, body),
            )
        qs.append(q)
        zs.append(z)
        ends.append(e)
        prior, other, after = last, sums, last
    ((a, n),) = rest[-1]
    plane = (groups, tokens, LANES)
    arrived, after = lax.optimization_barrier((far[-1], after))
    fwd = flipped(arrived, 1)
    q, p, end_state = call(
        functools.partial(last_kernel, rest[-1], seg),
        [sds(*plane), sds(*plane), sds(groups * poles, LANES)],
        [ext(tokens), pltpu.VMEM((n, D), BF16)],
        (own[-1], sib, arrived, fwd, gain, w, filt, fac, span, end, prior, other, tail),
    )
    qs.append(q)
    wrapped = contexts <= 4
    if wrapped:
        before = [
            lax.ppermute(end_state, "context", [(i, (i + d) % contexts) for i in range(contexts)])
            for d in range(1, contexts)
        ]
    else:
        every = lax.all_gather(end_state.reshape(groups, poles, LANES), "context")
        gaps = position - 1.0 - jnp.arange(contexts, dtype=F32)
        rates = dec.reshape(poles, groups, LANES).transpose(1, 0, 2)
        weights = jnp.where(
            (gaps >= 0.0)[:, None, None, None],
            jnp.exp(-rates[None] * count * jnp.maximum(gaps, 0.0)[:, None, None, None]),
            0.0,
        )
        before = [jnp.sum(weights * every, axis=0).reshape(groups * poles, LANES)]
    z, begin = call(
        functools.partial(starts_kernel, chunks, seg),
        [sds(*plane), sds(chunks, *tile)],
        [],
        (fac, rin, scan, skip, p, *ends),
    )
    zs.append(z)
    return call(
        functools.partial(final_kernel, chunks, seg, len(before), len(qs), wrapped),
        sds(count, chans, dtype=BF16),
        [pltpu.VMEM((chunks * groups, tokens, LANES), F32), pltpu.VMEM((groups, poles, LANES), F32)],
        (fac, reach, begin, inj, from_cache, jump, *before, *qs, *zs),
    )


def solution(mesh):
    placed = (
        P(("groups", "context"), "tensor"),
        P(),
        P(None, None, "tensor"),
        P(None, None, "tensor"),
        P("groups", None, "tensor"),
        P("tensor", None),
        P("tensor", None),
        P("tensor"),
        P(("groups", "tensor"), None),
    )
    return jax.shard_map(
        local,
        mesh=mesh,
        in_specs=placed,
        out_specs=P(("groups", "context"), "tensor"),
        check_vma=False,
    )
```

time: 77.2 us -> 62.2 us (0.81)
  local copies, waits for them, and re-layouts: 22.1 us -> 1.57 us
  waiting for transfers between devices: 5.48 us -> 14.9 us
  starting transfers between devices: 20 us -> 16.2 us
  Pallas kernels: 26.5 us -> 27.4 us
    unnamed x36 -> x10, local copies, waits for them, and re-layouts: 15.4 us -> 1.52 us
    ppermute x4 -> x1, starting transfers between devices: 11.7 us -> 3.47 us  [shifted(): lax.ppermute(block, axis, [(i - distance, i) for i in range(distance, siz...]
    ppermute x11 -> x9, waiting for transfers between devices: 5.31 us -> 12.2 us  [flipped(): return lax.ppermute(block, 'tensor', [(i, i ^ bit) for i in range(size)])]
    ppermute x0 -> x3, starting transfers between devices: none -> 6.3 us  [local(): lax.ppermute(end_state, 'context', [(i, (i + d) % contexts) for i in rang...]
    slice x3 -> x0, local copies, waits for them, and re-layouts: 4.36 us -> none  [local(): far = [flipped(hidden[a:a + n], 2) for a, n in bounds]]
    transpose x2, local copies, waits for them, and re-layouts: 2.34 us -> 0.05 us  [local(): cache = cache.reshape(HALO, 3 * groups, LANES).transpose(1, 0, 2)]
    ppermute x11 -> x9, starting transfers between devices: 8.32 us -> 6.46 us  [flipped(): return lax.ppermute(block, 'tensor', [(i, i ^ bit) for i in range(size)])]
    exp x1 -> x0, other arithmetic: 1.4 us -> none  [local(): jump = jnp.exp(-dec * count)]
  transfers between devices with their start and end apart: 15 -> 13, of which waited for: 2 -> 7; matrix products, arithmetic and copies ran while one was open for 11% -> 3% of each run, Pallas kernels for 25% -> 32%
where the time goes in v2:
time: 62.2 us; the launch traced here: 61.8 us
  Pallas kernels  27.4 us (44%)
  starting transfers between devices  16.2 us (26%)
  waiting for transfers between devices  14.9 us (24%)
  local copies, waits for them, and re-layouts  1.57 us (3%)
  other arithmetic  1.57 us (3%)
    pallas_call x8, Pallas kernels, call(): pl.pallas_call(kernel, out_shape=outs, in_specs=specs, out_specs=jax.tree...  27.4 us
    ppermute x9, waiting for transfers between devices, flipped(): return lax.ppermute(block, 'tensor', [(i, i ^ bit) for i in range(size)])  12.2 us
    ppermute x9, starting transfers between devices, flipped(): return lax.ppermute(block, 'tensor', [(i, i ^ bit) for i in range(size)])  6.46 us
    ppermute x3, starting transfers between devices, local(): lax.ppermute(end_state, 'context', [(i, (i + d) % contexts) for i in rang...  6.3 us
    ppermute x1, starting transfers between devices, shifted(): lax.ppermute(block, axis, [(i - distance, i) for i in range(distance, siz...  3.47 us
    unnamed x10, local copies, waits for them, and re-layouts  1.52 us
    ppermute x1, waiting for transfers between devices, shifted(): lax.ppermute(block, axis, [(i - distance, i) for i in range(distance, siz...  1.5 us
  transfers between devices with their start and end apart: 13, of which 7 were waited for; matrix products, arithmetic and copies ran while one was open for 3% of the time, Pallas kernels for 32%

profile of v2, /device:TPU:0, one launch (start us, length us, event | category | flops | bytes accessed | tf_op | source)
XLA Modules:
  0.0 61.8 jit_solution(1624039870396605516)
XLA Ops:
  0.0 1.2 %shard_map.92 = (bf16[144,1024]{1,0:T(8,128)(2,1)S(1)}, bf16[128,1024]{1,0:T(8,128)(2,1)S(1)}, bf16[128,1024]{1,0:T(8,128)(2,1)S(1)}, bf16[112,1024]{1,0:T(8,128)(2,1)S(1)}) custom-call(bf16[512,1024]{1,0:T(8,128)(2,1)} %h_any.1), custom_call_target="tpu_custom_call" | custom-call | bytes 1024 | tf_op jit(solution)/shard_map/pallas_call | solution.py:35
  1.3 0.6 collective-permute-start
  1.8 2.6 %collective-permute-start.4 = (bf16[144,1024]{1,0:T(8,128)(2,1)S(1)}, bf16[144,1024]{1,0:T(8,128)(2,1)S(1)}, u32[]{:S(2)}, u32[]{:S(2)}) collective-permute-start(bf16[144,1024]{1,0:T(8,128)(2,1)S(1)} %get-tuple-element.61.h_ref), channel_id=1, source_target_pairs={{0,2},{1,3},{2,0},{3,1},{4,6},{5,7},{6,4},{7,5},{8,10},{9,11},{10,... | collective-permute-start | bytes 884744 | tf_op jit(solution)/shard_map/ppermute | solution.py:29
  4.4 0.1 collective-permute-start.3
  4.4 7.8 %collective-permute-done.4.far_ref = bf16[144,1024]{1,0:T(8,128)(2,1)S(1)} collective-permute-done((bf16[144,1024]{1,0:T(8,128)(2,1)S(1)}, bf16[144,1024]{1,0:T(8,128)(2,1)S(1)}, u32[]{:S(2)}, u32[]{:S(2)}) %collective-permute-start.4) | collective-permute-done | bytes 294944 | tf_op jit(solution)/shard_map/ppermute | solution.py:29
  12.2 0.0 collective-permute-start.5
  12.2 0.8 %pad_convert_fusion = f32[8,3,512]{2,1,0:T(4,128)S(1)} fusion(bf16[6,3,512]{2,1,0:T(4,128)(2,1)} %param.13), kind=kLoop, calls=%fused_computation.2 | loop fusion | flops 12288 | bytes 67584 | tf_op jit(solution)/shard_map/transpose | solution.py:374
  13.1 0.8 %bitcast_multiply_fusion = (f32[16,512]{1,0:T(8,128)S(1)}, f32[16,512]{1,0:T(8,128)S(1)}, f32[16,512]{1,0:T(8,128)S(1)}) fusion(f32[512,16]{0,1:T(8,128)} %param.17, f32[]{:T(128)S(6)} %mul.28, f32[512,16]{0,1:T(8,128)} %param.14), kind=kLoop, calls=%fused_computation.1 | loop fusion | flops 49152 | bytes 163844 | tf_op jit(solution)/shard_map/mul | solution.py:372
  13.9 0.0 copy-start.2
  13.9 0.7 %copy-done.2 = f32[512,16]{0,1:T(8,128)S(1)} copy-done((f32[512,16]{0,1:T(8,128)S(1)}, f32[512,16]{0,1:T(8,128)}, u32[]{:S(2)}) %copy-start.2) | copy-done | bytes 32792
  14.6 0.8 %copy-done.3 = f32[512,16]{0,1:T(8,128)S(1)} copy-done((f32[512,16]{0,1:T(8,128)S(1)}, f32[512,16]{0,1:T(8,128)}, u32[]{:S(2)}) %copy-start.3) | copy-done | bytes 32792
  15.4 4.6 %shard_map.91 = (bf16[3,4096,512]{2,1,0:T(8,128)(2,1)S(1)}, f32[4,16,8,128]{3,2,1,0:T(8,128)S(1)}, f32[4,16,8,128]{3,2,1,0:T(8,128)S(1)}, f32[3,4,16,8,128]{4,3,...) custom-call(bf16[3,4096,512]{2,1,0:T(8,128)(2,1)} %bitcast.27, ...), custom_call_target="tpu_custom_call" | custom-call | bytes 1024 | tf_op jit(solution)/shard_map/pallas_call | solution.py:35
  20.0 3.6 %shard_map.93 = (f32[12,16,128]{2,1,0:T(8,128)S(1)}, bf16[12,8,128]{2,1,0:T(8,128)(2,1)S(1)}, f32[12,128,128]{2,1,0:T(8,128)S(1)}) custom-call(bf16[144,1024]{1,0:T(8,128)(2,1)S(1)} %get-tuple-element.61.h_ref, bf16[512,1024]{1,0:T(8,128)(2,1)S(1)} %collective-permute-done.sib_ref, bf16[144,1024]{1,0:T(8,128)(2,1)S(1)} %collective-permute-done.4.far_ref, ...), custom_call_target="tpu_custom_call" | custom-call | bytes 1024 | tf_op jit(solution)/shard_map/pallas_call | solution.py:35
  23.7 0.6 collective-permute-start.6
  24.2 2.0 %collective-permute-start.2 = (bf16[128,1024]{1,0:T(8,128)(2,1)S(1)}, bf16[128,1024]{1,0:T(8,128)(2,1)S(1)}, u32[]{:S(2)}, u32[]{:S(2)}) collective-permute-start(bf16[128,1024]{1,0:T(8,128)(2,1)S(1)} %get-tuple-element.59.h_ref), channel_id=1, source_target_pairs={{0,2},{1,3},{2,0},{3,1},{4,6},{5,7},{6,4},{7,5},{8,10},{9,11},{10,... | collective-permute-start | bytes 786440 | tf_op jit(solution)/shard_map/ppermute | solution.py:29
  26.2 3.5 %collective-permute-start.7 = (bf16[12,8,128]{2,1,0:T(8,128)(2,1)S(1)}, bf16[12,8,128]{2,1,0:T(8,128)(2,1)S(1)}, u32[]{:S(2)}, u32[]{:S(2)}) collective-permute-start(bf16[12,8,128]{2,1,0:T(8,128)(2,1)S(1)} %get-tuple-element.66), channel_id=1, source_target_pairs={{0,4},{4,8},{8,12},{1,5},{5,9},{9,13},{2,6},{6,10},{10,14},{3,7},{... | collective-permute-start | bytes 73736 | tf_op jit(solution)/shard_map/ppermute | solution.py:24
  29.7 1.5 %collective-permute-done.7.prior_ref = bf16[12,8,128]{2,1,0:T(8,128)(2,1)S(1)} collective-permute-done((bf16[12,8,128]{2,1,0:T(8,128)(2,1)S(1)}, bf16[12,8,128]{2,1,0:T(8,128)(2,1)S(1)}, u32[]{:S(2)}, u32[]{:S(2)}) %collective-permute-start.7) | collective-permute-done | bytes 24608 | tf_op jit(solution)/shard_map/ppermute | solution.py:24
  31.2 5.6 %shard_map.94 = (f32[4,256,128]{2,1,0:T(8,128)S(1)}, f32[4,256,128]{2,1,0:T(8,128)S(1)}, f32[2,4,16,8,128]{4,3,2,1,0:T(8,128)S(1)}, f32[4,16,8,128]{3,2,1,0:T(8,128)S(1)}, f32[12,8,128]{2,1,0:T(8,128)S(1)}) custom-call(bf16[128,1024]{1,0:T(8,128)(2,1)S(1)} %get-tuple-element.60.h_ref, bf16[512,1024]{1,0:T(8,128)(2,1)S(1)} %collective-permute-done.sib_ref, ...), custom_call_target="tpu_custom_call" | custom-call | bytes 1024 | tf_op jit(solution)/shard_map/pallas_call | solution.py:35
  36.8 0.1 collective-permute-start.8
  36.9 0.6 collective-permute-start.1
  37.5 0.9 %collective-permute-done.8.fwd_ref = bf16[128,1024]{1,0:T(8,128)(2,1)S(1)} collective-permute-done((bf16[128,1024]{1,0:T(8,128)(2,1)S(1)}, bf16[128,1024]{1,0:T(8,128)(2,1)S(1)}, u32[]{:S(2)}, u32[]{:S(2)}) %collective-permute-start.8) | collective-permute-done | bytes 262176 | tf_op jit(solution)/shard_map/ppermute | solution.py:29
  38.4 4.5 %shard_map.95 = (f32[4,128,128]{2,1,0:T(8,128)S(1)}, f32[4,128,128]{2,1,0:T(8,128)S(1)}, f32[1,4,16,8,128]{4,3,2,1,0:T(8,128)S(1)}, f32[4,16,8,128]{3,2,1,0:T(8,128)S(1)}, f32[12,8,128]{2,1,0:T(8,128)S(1)}) custom-call(bf16[128,1024]{1,0:T(8,128)(2,1)S(1)} %get-tuple-element.59.h_ref, bf16[512,1024]{1,0:T(8,128)(2,1)S(1)} %collective-permute-done.sib_ref, ...), custom_call_target="tpu_custom_call" | custom-call | bytes 1024 | tf_op jit(solution)/shard_map/pallas_call | solution.py:35
  42.9 2.0 %collective-permute-done.1.far_ref = bf16[112,1024]{1,0:T(8,128)(2,1)S(1)} collective-permute-done((bf16[112,1024]{1,0:T(8,128)(2,1)S(1)}, bf16[112,1024]{1,0:T(8,128)(2,1)S(1)}, u32[]{:S(2)}, u32[]{:S(2)}) %collective-permute-start.1) | collective-permute-done | bytes 229408 | tf_op jit(solution)/shard_map/ppermute | solution.py:29
  44.9 1.5 %collective-permute-done.9.fwd_ref = bf16[112,1024]{1,0:T(8,128)(2,1)S(1)} collective-permute-done((bf16[112,1024]{1,0:T(8,128)(2,1)S(1)}, bf16[112,1024]{1,0:T(8,128)(2,1)S(1)}, u32[]{:S(2)}, u32[]{:S(2)}) %collective-permute-start.9) | collective-permute-done | bytes 229408 | tf_op jit(solution)/shard_map/ppermute | solution.py:29
  46.4 4.1 %shard_map.96 = (f32[4,128,128]{2,1,0:T(8,128)S(1)}, f32[4,128,128]{2,1,0:T(8,128)S(1)}, f32[64,128]{1,0:T(8,128)S(1)}) custom-call(bf16[112,1024]{1,0:T(8,128)(2,1)S(1)} %get-tuple-element.57.h_ref, bf16[512,1024]{1,0:T(8,128)(2,1)S(1)} %collective-permute-done.sib_ref, bf16[112,1024]{1,0:T(8,128)(2,1)S(1)} %collective-permute-done.1.far_ref, ...), custom_call_target="tpu_custom_call" | custom-call | bytes 1024 | tf_op jit(solution)/shard_map/pallas_call | solution.py:35
  50.5 2.4 %collective-permute-start.10 = (f32[64,128]{1,0:T(8,128)S(1)}, f32[64,128]{1,0:T(8,128)S(1)}, u32[]{:S(2)}, u32[]{:S(2)}) collective-permute-start(f32[64,128]{1,0:T(8,128)S(1)} %get-tuple-element.82), channel_id=1, source_target_pairs={{0,4},{4,8},{8,12},{12,0},{1,5},{5,9},{9,13},{13,1},{2,6},{6,10},{... | collective-permute-start | bytes 98312 | tf_op jit(solution)/shard_map/ppermute | solution.py:433
  52.9 2.6 %collective-permute-start.11 = (f32[64,128]{1,0:T(8,128)S(1)}, f32[64,128]{1,0:T(8,128)S(1)}, u32[]{:S(2)}, u32[]{:S(2)}) collective-permute-start(f32[64,128]{1,0:T(8,128)S(1)} %get-tuple-element.82), channel_id=1, source_target_pairs={{0,8},{4,12},{8,0},{12,4},{1,9},{5,13},{9,1},{13,5},{2,10},{6,14},... | collective-permute-start | bytes 98312 | tf_op jit(solution)/shard_map/ppermute | solution.py:433
  55.5 1.3 %collective-permute-start.12 = (f32[64,128]{1,0:T(8,128)S(1)}, f32[64,128]{1,0:T(8,128)S(1)}, u32[]{:S(2)}, u32[]{:S(2)}) collective-permute-start(f32[64,128]{1,0:T(8,128)S(1)} %get-tuple-element.82), channel_id=1, source_target_pairs={{0,12},{4,0},{8,4},{12,8},{1,13},{5,1},{9,5},{13,9},{2,14},{6,2},{... | collective-permute-start | bytes 98312 | tf_op jit(solution)/shard_map/ppermute | solution.py:433
  56.9 1.4 %shard_map.97 = (f32[4,128,128]{2,1,0:T(8,128)S(1)}, f32[4,4,16,8,128]{4,3,2,1,0:T(8,128)S(1)}) custom-call(f32[4,16,8,128]{3,2,1,0:T(8,128)S(1)} %get-tuple-element.49.fac_ref, f32[4,16,8,128]{3,2,1,0:T(8,128)S(1)} %get-tuple-element.51.rin_ref, f32[3,4,16,8,128]{4,3,2,1,0:T(8,128)S(1)} %get-tuple-element.52.scan_ref, f32[1,512]{1,0:T(1,128)S(1)} %bitcast.26, ...), custom_call_target="tpu_custom_call" | custom-call | bytes 1024 | tf_op jit(solution)/shard_map/pallas_call | solution.py:35
  58.2 0.1 collective-permute-done.11.refs_1_
  58.3 1.1 %collective-permute-done.12.refs_2_ = f32[64,128]{1,0:T(8,128)S(1)} collective-permute-done((f32[64,128]{1,0:T(8,128)S(1)}, f32[64,128]{1,0:T(8,128)S(1)}, u32[]{:S(2)}, u32[]{:S(2)}) %collective-permute-start.12) | collective-permute-done | bytes 32800 | tf_op jit(solution)/shard_map/ppermute | solution.py:433
  59.4 2.4 %shard_map.98 = bf16[512,512]{1,0:T(8,128)(2,1)} custom-call(f32[4,16,8,128]{3,2,1,0:T(8,128)S(1)} %get-tuple-element.49.fac_ref, f32[4,4,16,8,128]{4,3,2,1,0:T(8,128)S(1)} %get-tuple-element.50.reach_ref, f32[4,4,16,8,128]{4,3,2,1,0:T(8,128)S(1)} %get-tuple-element.79.begin_ref, f32[16,512]{1,0:T(8,128)S(1)} %get-tuple-element.48.inj_ref, ...), custom_call_target="tpu_custom_call" | custom-call | bytes 1024 | tf_op jit(solution)/shard_map/pallas_call | solution.py:35
  (16 shorter events, 0.1 us)
Async XLA Ops:
  0.0 20.0 %copy-start.1 = (f32[4096]{0:T(1024)S(1)}, f32[4096]{0:T(1024)}, u32[]{:S(2)}) copy-start(f32[4096]{0:T(1024)} %param.10) | copy-start | bytes 49156
  1.3 18.8 %collective-permute-start = (bf16[512,1024]{1,0:T(8,128)(2,1)}, bf16[512,1024]{1,0:T(8,128)(2,1)S(1)}, u32[]{:S(2)}, u32[]{:S(2)}) collective-permute-start(bf16[512,1024]{1,0:T(8,128)(2,1)} %h_any.1), channel_id=1, source_target_pairs={{0,1},{1,0},{2,3},{3,2},{4,5},{5,4},{6,7},{7,6},{8,9},{9,8},{10,11... | collective-permute-start | bytes 3145736 | tf_op jit(solution)/shard_map/ppermute | solution.py:29
  1.8 10.4 %collective-permute-start.4 = (bf16[144,1024]{1,0:T(8,128)(2,1)S(1)}, bf16[144,1024]{1,0:T(8,128)(2,1)S(1)}, u32[]{:S(2)}, u32[]{:S(2)}) collective-permute-start(bf16[144,1024]{1,0:T(8,128)(2,1)S(1)} %get-tuple-element.61.h_ref), channel_id=1, source_target_pairs={{0,2},{1,3},{2,0},{3,1},{4,6},{5,7},{6,4},{7,5},{8,10},{9,11},{10,... | collective-permute-start | bytes 884744 | tf_op jit(solution)/shard_map/ppermute | solution.py:29
  4.4 19.3 %collective-permute-start.3 = (bf16[128,1024]{1,0:T(8,128)(2,1)S(1)}, bf16[128,1024]{1,0:T(8,128)(2,1)S(1)}, u32[]{:S(2)}, u32[]{:S(2)}) collective-permute-start(bf16[128,1024]{1,0:T(8,128)(2,1)S(1)} %get-tuple-element.60.h_ref), channel_id=1, source_target_pairs={{0,2},{1,3},{2,0},{3,1},{4,6},{5,7},{6,4},{7,5},{8,10},{9,11},{10,... | collective-permute-start | bytes 786440 | tf_op jit(solution)/shard_map/ppermute | solution.py:29
  12.2 7.8 %collective-permute-start.5 = (bf16[144,1024]{1,0:T(8,128)(2,1)S(1)}, bf16[144,1024]{1,0:T(8,128)(2,1)S(1)}, u32[]{:S(2)}, u32[]{:S(2)}) collective-permute-start(bf16[144,1024]{1,0:T(8,128)(2,1)S(1)} %collective-permute-done.4.far_ref), channel_id=1, source_target_pairs={{0,1},{1,0},{2,3},{3,2},{4,5},{5,4},{6,7},{7,6},{8,9},{9,8},{10,11... | collective-permute-start | bytes 884744 | tf_op jit(solution)/shard_map/ppermute | solution.py:29
  13.9 0.8 %copy-start.2 = (f32[512,16]{0,1:T(8,128)S(1)}, f32[512,16]{0,1:T(8,128)}, u32[]{:S(2)}) copy-start(f32[512,16]{0,1:T(8,128)} %param.14) | copy-start | bytes 98308
  14.6 0.8 %copy-start.3 = (f32[512,16]{0,1:T(8,128)S(1)}, f32[512,16]{0,1:T(8,128)}, u32[]{:S(2)}) copy-start(f32[512,16]{0,1:T(8,128)} %param.15) | copy-start | bytes 98308
  15.4 15.8 %copy-start = (f32[7,3,512]{2,0,1:T(8,128)S(1)}, f32[7,3,512]{2,0,1:T(8,128)}, u32[]{:S(2)}) copy-start(f32[7,3,512]{2,0,1:T(8,128)} %param.12) | copy-start | bytes 129028
  15.4 15.8 %copy-start.4 = (f32[512]{0:T(512)S(1)}, f32[512]{0:T(512)}, u32[]{:S(2)}) copy-start(f32[512]{0:T(512)} %param.16) | copy-start | bytes 6148
  23.7 7.6 %collective-permute-start.6 = (bf16[128,1024]{1,0:T(8,128)(2,1)S(1)}, bf16[128,1024]{1,0:T(8,128)(2,1)S(1)}, u32[]{:S(2)}, u32[]{:S(2)}) collective-permute-start(bf16[128,1024]{1,0:T(8,128)(2,1)S(1)} %collective-permute-done.3.far_ref), channel_id=1, source_target_pairs={{0,1},{1,0},{2,3},{3,2},{4,5},{5,4},{6,7},{7,6},{8,9},{9,8},{10,11... | collective-permute-start | bytes 786440 | tf_op jit(solution)/shard_map/ppermute | solution.py:29
  24.2 12.6 %collective-permute-start.2 = (bf16[128,1024]{1,0:T(8,128)(2,1)S(1)}, bf16[128,1024]{1,0:T(8,128)(2,1)S(1)}, u32[]{:S(2)}, u32[]{:S(2)}) collective-permute-start(bf16[128,1024]{1,0:T(8,128)(2,1)S(1)} %get-tuple-element.59.h_ref), channel_id=1, source_target_pairs={{0,2},{1,3},{2,0},{3,1},{4,6},{5,7},{6,4},{7,5},{8,10},{9,11},{10,... | collective-permute-start | bytes 786440 | tf_op jit(solution)/shard_map/ppermute | solution.py:29
  26.2 5.0 %collective-permute-start.7 = (bf16[12,8,128]{2,1,0:T(8,128)(2,1)S(1)}, bf16[12,8,128]{2,1,0:T(8,128)(2,1)S(1)}, u32[]{:S(2)}, u32[]{:S(2)}) collective-permute-start(bf16[12,8,128]{2,1,0:T(8,128)(2,1)S(1)} %get-tuple-element.66), channel_id=1, source_target_pairs={{0,4},{4,8},{8,12},{1,5},{5,9},{9,13},{2,6},{6,10},{10,14},{3,7},{... | collective-permute-start | bytes 73736 | tf_op jit(solution)/shard_map/ppermute | solution.py:24
  36.8 1.6 %collective-permute-start.8 = (bf16[128,1024]{1,0:T(8,128)(2,1)S(1)}, bf16[128,1024]{1,0:T(8,128)(2,1)S(1)}, u32[]{:S(2)}, u32[]{:S(2)}) collective-permute-start(bf16[128,1024]{1,0:T(8,128)(2,1)S(1)} %collective-permute-done.2.far_ref), channel_id=1, source_target_pairs={{0,1},{1,0},{2,3},{3,2},{4,5},{5,4},{6,7},{7,6},{8,9},{9,8},{10,11... | collective-permute-start | bytes 786440 | tf_op jit(solution)/shard_map/ppermute | solution.py:29
  36.9 8.0 %collective-permute-start.1 = (bf16[112,1024]{1,0:T(8,128)(2,1)S(1)}, bf16[112,1024]{1,0:T(8,128)(2,1)S(1)}, u32[]{:S(2)}, u32[]{:S(2)}) collective-permute-start(bf16[112,1024]{1,0:T(8,128)(2,1)S(1)} %get-tuple-element.57.h_ref), channel_id=1, source_target_pairs={{0,2},{1,3},{2,0},{3,1},{4,6},{5,7},{6,4},{7,5},{8,10},{9,11},{10,... | collective-permute-start | bytes 688136 | tf_op jit(solution)/shard_map/ppermute | solution.py:29
  44.9 1.5 %collective-permute-start.9 = (bf16[112,1024]{1,0:T(8,128)(2,1)S(1)}, bf16[112,1024]{1,0:T(8,128)(2,1)S(1)}, u32[]{:S(2)}, u32[]{:S(2)}) collective-permute-start(bf16[112,1024]{1,0:T(8,128)(2,1)S(1)} %collective-permute-done.1.far_ref), channel_id=1, source_target_pairs={{0,1},{1,0},{2,3},{3,2},{4,5},{5,4},{6,7},{7,6},{8,9},{9,8},{10,11... | collective-permute-start | bytes 688136 | tf_op jit(solution)/shard_map/ppermute | solution.py:29
  50.5 7.7 %collective-permute-start.10 = (f32[64,128]{1,0:T(8,128)S(1)}, f32[64,128]{1,0:T(8,128)S(1)}, u32[]{:S(2)}, u32[]{:S(2)}) collective-permute-start(f32[64,128]{1,0:T(8,128)S(1)} %get-tuple-element.82), channel_id=1, source_target_pairs={{0,4},{4,8},{8,12},{12,0},{1,5},{5,9},{9,13},{13,1},{2,6},{6,10},{... | collective-permute-start | bytes 98312 | tf_op jit(solution)/shard_map/ppermute | solution.py:433
  52.9 5.4 %collective-permute-start.11 = (f32[64,128]{1,0:T(8,128)S(1)}, f32[64,128]{1,0:T(8,128)S(1)}, u32[]{:S(2)}, u32[]{:S(2)}) collective-permute-start(f32[64,128]{1,0:T(8,128)S(1)} %get-tuple-element.82), channel_id=1, source_target_pairs={{0,8},{4,12},{8,0},{12,4},{1,9},{5,13},{9,1},{13,5},{2,10},{6,14},... | collective-permute-start | bytes 98312 | tf_op jit(solution)/shard_map/ppermute | solution.py:433
  55.5 3.9 %collective-permute-start.12 = (f32[64,128]{1,0:T(8,128)S(1)}, f32[64,128]{1,0:T(8,128)S(1)}, u32[]{:S(2)}, u32[]{:S(2)}) collective-permute-start(f32[64,128]{1,0:T(8,128)S(1)} %get-tuple-element.82), channel_id=1, source_target_pairs={{0,12},{4,0},{8,4},{12,8},{1,13},{5,1},{9,5},{13,9},{2,14},{6,2},{... | collective-permute-start | bytes 98312 | tf_op jit(solution)/shard_map/ppermute | solution.py:433

commit v3 on v2

v3 whole, which is shorter than its diff:
```python
import functools

import jax
import jax.numpy as jnp
from jax import lax
from jax.experimental import pallas as pl
from jax.experimental.pallas import tpu as pltpu
from jax.sharding import PartitionSpec as P

D = 4096
EPS = 1e-06
LANES = 128
SEGS = 8
TAIL = 16
HALO = 8
NOTES = 16

VM = pl.BlockSpec(memory_space=pltpu.VMEM)
F32 = jnp.float32
BF16 = jnp.bfloat16


def shifted(block, axis, distance):
    size = lax.axis_size(axis)
    return lax.ppermute(block, axis, [(i - distance, i) for i in range(distance, size)])


def flipped(block, bit):
    size = lax.axis_size("tensor")
    return lax.ppermute(block, "tensor", [(i, i ^ bit) for i in range(size)])


def call(kernel, outs, scratch, args, flops=0, limit=12, anywhere=()):
    specs = [pl.BlockSpec(memory_space=pltpu.HBM) if i in anywhere else VM for i in range(len(args))]
    args = [pltpu.with_memory_space_constraint(x, pltpu.HBM) if i in anywhere else x for i, x in enumerate(args)]
    return pl.pallas_call(
        kernel,
        out_shape=outs,
        in_specs=specs,
        out_specs=jax.tree.map(lambda _: VM, outs, is_leaf=lambda o: hasattr(o, "dtype")),
        scratch_shapes=scratch,
        cost_estimate=pl.CostEstimate(flops=flops, bytes_accessed=1024, transcendentals=0),
        compiler_params=pltpu.CompilerParams(vmem_limit_bytes=limit << 20),
    )(*args)


def kept(*shape, dtype=F32):
    return pltpu.VMEM(shape, dtype)


def sds(*shape, dtype=F32):
    return jax.ShapeDtypeStruct(shape, dtype)


def open_kernel(pieces, h_any, *refs):
    *out_refs, squares_ref, h_ref, sem = refs
    count, width = h_ref.shape
    whole = pltpu.make_async_copy(h_any, h_ref, sem.at[0])
    whole.start()
    copies = []
    for parts, out_ref in zip(pieces, out_refs):
        at = 0
        for start, rows in parts:
            copies.append(
                pltpu.make_async_copy(
                    h_any.at[start : start + rows, :], out_ref.at[at : at + rows, :], sem.at[1 + len(copies)]
                )
            )
            at += rows
    for copy in copies:
        copy.start()
    whole.wait()
    sums = []
    for at in range(0, count, LANES):
        squares = row_squares(h_ref, slice(at, at + LANES))
        squares_ref[at : at + LANES, :] = squares
        sums.append(jnp.sum(jnp.transpose(squares), axis=0, keepdims=True))
    rest = jnp.concatenate(sums, axis=1)
    terms = []
    for _ in range(3):
        term = rest.astype(BF16).astype(F32)
        rest = rest - term
        terms.append(term)
    coded = jnp.concatenate(terms + [jnp.zeros((NOTES - 3, count), F32)], axis=0).astype(BF16)
    for copy in copies:
        copy.wait()
    first = out_refs[0]
    at = first.shape[0] - NOTES
    first[at:, :count] = coded
    first[at:, count:] = jnp.zeros((NOTES, width - count), BF16)


def row_squares(ref, rows):
    block = ref[rows, :].astype(F32)
    block = block * block
    total = block[:, :LANES]
    for lane in range(LANES, block.shape[1], LANES):
        total = total + block[:, lane : lane + LANES]
    return total


def stage_kernel(
    seg, chunks, w_any, dec_ref, res_ref, inj_ref,
    w_ref, fac_ref, rin_ref, scan_ref, span_ref, end_ref, reach_ref, sem,
):
    copies = [pltpu.make_async_copy(w_any, w_ref, sem.at[0])]
    for copy in copies:
        copy.start()
    groups, poles = fac_ref.shape[0], fac_ref.shape[1]
    row = lax.broadcasted_iota(jnp.int32, (SEGS, LANES), 0)
    rowf = row.astype(F32)

    def body(g, c):
        lanes = pl.ds(pl.multiple_of(g * LANES, LANES), LANES)
        for n in range(poles):
            dec = jnp.broadcast_to(dec_ref[n : n + 1, lanes], (SEGS, LANES))
            res = jnp.broadcast_to(res_ref[n : n + 1, lanes], (SEGS, LANES))
            inj = jnp.broadcast_to(inj_ref[n : n + 1, lanes], (SEGS, LANES))
            fac_ref[g, n] = jnp.exp(-dec)
            rin_ref[g, n] = res * inj
            for b, step in enumerate((1, 2, 4)):
                scan_ref[b, g, n] = jnp.where(row >= step, jnp.exp(-dec * float(seg * step)), 0.0)
            span_ref[g, n] = jnp.exp(-dec * float(seg * SEGS))
            end_ref[g, n] = jnp.exp(-dec * ((SEGS - 1.0 - rowf) * float(seg)))
            for k in range(chunks):
                reach_ref[k, g, n] = res * jnp.exp(-dec * (1.0 + float(seg) * (float(SEGS * k) + rowf)))
        return c

    lax.fori_loop(0, groups, body, 0)
    for copy in copies:
        copy.wait()


def normed_block(ref, rows, scale_ref, start, gain_ref, index):
    width = ref.shape[1]
    lanes = pl.ds(pl.multiple_of(index * width, width), width)
    count = rows.stop - rows.start
    scale = scale_ref[start : start + count, :]
    scale = jnp.concatenate([scale] * (width // LANES), axis=1)
    return (ref[rows, :].astype(F32) * scale * gain_ref[:, lanes]).astype(BF16)


def put_block(normed_ref, rows, index, block):
    width = block.shape[1]
    normed_ref[rows, pl.ds(pl.multiple_of(index * width, width), width)] = block


def multiply(normed_ref, w_ref, start, put):
    groups = w_ref.shape[2] // LANES
    halves = groups // 2
    depth = normed_ref.shape[1]

    def body(step, c):
        i, half = step // halves, step % halves
        lanes = pl.ds(pl.multiple_of(half * 2 * LANES, 2 * LANES), 2 * LANES)
        rows = pl.ds(start, depth)
        products = jnp.dot(normed_ref[...], w_ref[i, rows, lanes], preferred_element_type=F32)
        put(step * 2, products[:, :LANES])
        put(step * 2 + 1, products[:, LANES:])
        return c

    lax.fori_loop(0, 3 * halves, body, 0)


def rounded(streams):
    return streams.astype(BF16).astype(F32)


def convolve(ext_ref, filt_ref, g, first, tokens, streams=(0, 1, 2)):
    groups = ext_ref.shape[0] // 3
    lanes = pl.ds(pl.multiple_of(g * LANES, LANES), LANES)
    taps = filt_ref.shape[1]
    found = []
    for i in streams:
        total = jnp.zeros((tokens, LANES), F32)
        for k in range(taps):
            rows = pl.ds(first + HALO - taps + 1 + k, tokens)
            total = total + filt_ref[i, k : k + 1, lanes] * ext_ref[i * groups + g, rows, :]
        found.append(total)
    return found


def scan_unit(prod_ref, fac_ref, rin_ref, g, first, seg, out_ref):
    poles = fac_ref.shape[1]
    entry = prod_ref[g, pl.ds(first, SEGS, stride=seg), :]
    state = [entry] * poles
    for j in range(seg):
        rows = pl.ds(first + j, SEGS, stride=seg)
        if j:
            entry = prod_ref[g, rows, :]
            state = [fac_ref[g, n] * state[n] + entry for n in range(poles)]
        if out_ref is not None:
            terms = [rin_ref[g, n] * state[n] for n in range(poles)]
            while len(terms) > 1:
                terms = [a + b for a, b in zip(terms[::2], terms[1::2])]
            out_ref[g, rows, :] = terms[0]
    return state


def head_kernel(
    parts, a_ref, sib_ref, far_ref, fwd_ref, squares_ref, gain_ref, w_ref,
    scale_ref, tail_ref, send_ref, body_ref, normed_ref,
):
    t = lax.axis_index("tensor")
    count = squares_ref.shape[0]
    at = far_ref.shape[0] - NOTES
    notes = jnp.zeros((1, count), F32)
    for ref in (far_ref, fwd_ref):
        coded = ref[at:, :count].astype(F32)
        notes = notes + ((coded[0:1] + coded[1:2]) + coded[2:3])
    for row in range(0, count, LANES):
        rows = slice(row, row + LANES)
        others = jnp.transpose(jnp.broadcast_to(notes[:, rows], (LANES, LANES)))
        near = jnp.sum(squares_ref[rows, :] + row_squares(sib_ref, rows), axis=1, keepdims=True)
        scale_ref[rows, :] = lax.rsqrt((near + others) / D + EPS)
    at = 0
    for start, rows in parts:
        here = slice(at, at + rows)
        there = slice(start, start + rows)
        at += rows
        for index, ref, where in ((t, a_ref, here), (t ^ 1, sib_ref, there), (t ^ 2, far_ref, here), (t ^ 3, fwd_ref, here)):
            put_block(normed_ref, here, index, normed_block(ref, where, scale_ref, start, gain_ref, index))

    def put(at, products):
        streams = rounded(products)
        tail_ref[at] = streams[:TAIL]
        send_ref[at] = streams[TAIL - HALO : TAIL].astype(BF16)
        body_ref[at] = streams[TAIL:]

    multiply(normed_ref, w_ref, 0, put)


def near_kernel(parts, *refs):
    own_refs = refs[: len(parts)]
    sib_ref, scale_ref, gain_ref, w_ref, part_ref, normed_ref = refs[len(parts) :]
    t = lax.axis_index("tensor")
    depth = normed_ref.shape[1]
    at = 0
    for own_ref, (start, rows) in zip(own_refs, parts):
        here = slice(at, at + rows)
        at += rows
        own = normed_block(own_ref, slice(0, rows), scale_ref, start, gain_ref, t)
        put_block(normed_ref, here, t & 1, own)
        sib = normed_block(sib_ref, slice(start, start + rows), scale_ref, start, gain_ref, t ^ 1)
        put_block(normed_ref, here, (t & 1) ^ 1, sib)

    def put(at, products):
        part_ref[at] = products

    multiply(normed_ref, w_ref, pl.multiple_of((t >> 1) * depth, depth), put)


def far_part(start, rows, offset, far_ref, fwd_ref, scale_ref, gain_ref, w_ref, part_ref, ext_ref, base, normed_ref):
    t = lax.axis_index("tensor")
    depth = normed_ref.shape[1]
    here = slice(0, rows)
    put_block(normed_ref, here, t & 1, normed_block(far_ref, here, scale_ref, start, gain_ref, t ^ 2))
    put_block(normed_ref, here, (t & 1) ^ 1, normed_block(fwd_ref, here, scale_ref, start, gain_ref, t ^ 3))

    def put(at, products):
        ext_ref[at, base : base + rows, :] = rounded(part_ref[at, offset : offset + rows, :] + products)

    multiply(normed_ref, w_ref, pl.multiple_of(((t >> 1) ^ 1) * depth, depth), put)


def chunk_kernel(
    start, rows, offset, units, seg, first,
    far_ref, fwd_ref, scale_ref, gain_ref, w_ref, part_ref, filt_ref, fac_ref, rin_ref, span_ref, skip_ref,
    prior_ref, other_ref, body_ref,
    q_ref, z_ref, ends_ref, sum_ref, last_ref,
    ext_ref, normed_ref, prod_ref,
):
    groups, poles = fac_ref.shape[0], fac_ref.shape[1]
    tokens = seg * SEGS
    if first:
        got = prior_ref[...].astype(F32)
        ext_ref[:, :HALO, :] = jnp.where(lax.axis_index("context") == 0, other_ref[...], got)
        base = HALO + body_ref.shape[1]
        ext_ref[:, HALO:base, :] = body_ref[...]
    else:
        base = prior_ref.shape[1]
        ext_ref[:, :base, :] = prior_ref[...]
    far_part(start, rows, offset, far_ref, fwd_ref, scale_ref, gain_ref, w_ref, part_ref, ext_ref, base, normed_ref)
    last_ref[...] = ext_ref[:, units * tokens :, :]

    def body(g, c):
        lanes = pl.ds(pl.multiple_of(g * LANES, LANES), LANES)
        query, keyed, value = convolve(ext_ref, filt_ref, g, 0, units * tokens)
        q_ref[g] = query
        prod_ref[g] = keyed * value
        for u in range(units):
            state = scan_unit(prod_ref, fac_ref, rin_ref, g, u * tokens, seg, z_ref)
            for n in range(poles):
                ends_ref[u, g, n] = state[n]
                if u:
                    sum_ref[g, n] = span_ref[g, n] * sum_ref[g, n] + state[n]
                elif first:
                    sum_ref[g, n] = state[n]
                else:
                    sum_ref[g, n] = span_ref[g, n] * other_ref[g, n] + state[n]
        z_ref[g] = z_ref[g] + skip_ref[:, lanes] * prod_ref[g]
        return c

    lax.fori_loop(0, groups, body, 0)


def last_kernel(
    start, rows, offset, units, seg,
    far_ref, fwd_ref, scale_ref, gain_ref, w_ref, part_ref, filt_ref, fac_ref, span_ref, end_ref,
    prior_ref, sums_ref, tail_ref,
    q_ref, p_ref, end_state_ref,
    ext_ref, normed_ref,
):
    groups, poles = fac_ref.shape[0], fac_ref.shape[1]
    tokens = seg * SEGS
    base = prior_ref.shape[1]
    ext_ref[:, :base, :] = prior_ref[...]
    ext_ref[:, base + rows :, :] = tail_ref[...]
    far_part(start, rows, offset, far_ref, fwd_ref, scale_ref, gain_ref, w_ref, part_ref, ext_ref, base, normed_ref)

    def body(g, c):
        query, keyed, value = convolve(ext_ref, filt_ref, g, 0, units * tokens)
        q_ref[g] = query
        p_ref[g] = keyed * value
        whole = [sums_ref[g, n] for n in range(poles)]
        for u in range(units):
            state = scan_unit(p_ref, fac_ref, None, g, u * tokens, seg, None)
            whole = [span_ref[g, n] * whole[n] + state[n] for n in range(poles)]
        for n in range(poles):
            found = jnp.sum(end_ref[g, n] * whole[n], axis=0, keepdims=True)
            end_state_ref[pl.ds(g * poles + n, 1), :] = found
        return c

    lax.fori_loop(0, groups, body, 0)


def starts_kernel(seg, fac_ref, rin_ref, scan_ref, skip_ref, p_ref, *refs):
    *ends_refs, z_ref, begin_ref, mine_ref = refs
    ends_refs = [ref.at[u] for ref in (*ends_refs, mine_ref) for u in range(ref.shape[0])]
    groups, poles = fac_ref.shape[0], fac_ref.shape[1]
    row = lax.broadcasted_iota(jnp.int32, (SEGS, LANES), 0)

    def body(g, c):
        for u in range(mine_ref.shape[0]):
            state = scan_unit(p_ref, fac_ref, rin_ref, g, u * seg * SEGS, seg, z_ref)
            for n in range(poles):
                mine_ref[u, g, n] = state[n]
        lanes = pl.ds(pl.multiple_of(g * LANES, LANES), LANES)
        z_ref[g] = z_ref[g] + skip_ref[:, lanes] * p_ref[g]

        def pole(n, c):
            lead = rin_ref[g, n] * fac_ref[g, n]
            step = jnp.broadcast_to(scan_ref[0, g, n, 1:2, :], (SEGS, LANES))
            enter = jnp.zeros((SEGS, LANES), F32)
            for k, ends_ref in enumerate(ends_refs):
                held = ends_ref[g, n]
                held = jnp.where(row == 0, held + step * enter, held)
                for b, by in enumerate((1, 2, 4)):
                    held = held + scan_ref[b, g, n] * pltpu.roll(held, by, 0)
                begin_ref[k, g, n] = lead * jnp.where(row == 0, enter, pltpu.roll(held, 1, 0))
                enter = jnp.broadcast_to(held[SEGS - 1 :, :], (SEGS, LANES))
            return c

        lax.fori_loop(0, poles, pole, 0, unroll=4)
        return c

    lax.fori_loop(0, groups, body, 0)


def final_kernel(
    units, seg, hops, pieces, paired, fac_ref, reach_ref, begin_ref, inj_ref, from_cache_ref, jump_ref, *refs
):
    e_refs = refs[:hops]
    q_refs = refs[hops : hops + pieces]
    z_refs = refs[hops + pieces : hops + 2 * pieces]
    out_ref, add_ref, enter_ref = refs[hops + 2 * pieces :]
    groups, poles = fac_ref.shape[0], fac_ref.shape[1]
    tokens = seg * SEGS
    position = lax.axis_index("context")

    for g in range(groups):
        lanes = slice(g * LANES, (g + 1) * LANES)
        rows = slice(g * poles, (g + 1) * poles)
        jump = jump_ref[:, lanes]
        total = jnp.zeros((poles, LANES), F32)
        for e in range(hops):
            found = e_refs[e][rows, :]
            if paired:
                source = position ^ (e + 1)
                gap = position - 1 - source
                for step in range(1, hops):
                    found = jnp.where(gap >= step, found * jump, found)
                found = jnp.where(gap >= 0, found, 0.0)
            total = total + found
        enter_ref[g] = inj_ref[:, lanes] * total + from_cache_ref[:, lanes]

    def body(step, c):
        k, g = step // groups, step % groups
        state = []
        for n in range(poles):
            enter = jnp.broadcast_to(enter_ref[g, n : n + 1, :], (SEGS, LANES))
            state.append(begin_ref[k, g, n] + reach_ref[k, g, n] * enter)
        for j in range(seg):
            if j:
                state = [fac_ref[g, n] * state[n] for n in range(poles)]
            terms = state
            while len(terms) > 1:
                terms = [a + b for a, b in zip(terms[::2], terms[1::2])]
            add_ref[step, pl.ds(j, SEGS, stride=seg), :] = terms[0]
        return c

    lax.fori_loop(0, units * groups, body, 0)
    k = 0
    for q_ref, z_ref in zip(q_refs, z_refs):
        for u in range(q_ref.shape[1] // tokens):
            here = slice(u * tokens, (u + 1) * tokens)
            for g in range(groups):
                out_ref[k * tokens : (k + 1) * tokens, g * LANES : (g + 1) * LANES] = (
                    q_ref[g, here, :] * (z_ref[g, here, :] + add_ref[k * groups + g])
                ).astype(BF16)
            k += 1


def local(
    hidden, norm_gain, in_proj, short_filter, conv_cache, decay, residues, skip_gain, cached_state
):
    count, width = hidden.shape
    chans = in_proj.shape[2]
    poles = decay.shape[1]
    taps = short_filter.shape[0]
    groups = chans // LANES
    units = 8
    tokens = count // units
    seg = tokens // SEGS
    position = lax.axis_index("context").astype(F32)
    contexts = lax.axis_size("context")

    head = [(count - TAIL, TAIL), (0, tokens)]
    sizes = [2 * tokens, 2 * tokens + TAIL, 3 * tokens - 2 * TAIL]
    taken = [3, 2, 3]
    rest, at = [], tokens
    for size in sizes:
        rest.append((at, size))
        at += size
    *own, squares = call(
        functools.partial(open_kernel, [head] + [[part] for part in rest]),
        [kept(tokens + TAIL + NOTES, width, dtype=BF16)]
        + [kept(n, width, dtype=BF16) for _, n in rest]
        + [kept(count, LANES)],
        [pltpu.VMEM((count, width), BF16), pltpu.SemaphoreType.DMA((len(rest) + 3,))],
        (hidden,),
        anywhere=(0,),
    )
    far = [flipped(block, 2) for block in own]
    hidden, own = lax.optimization_barrier((hidden, own))
    sib = flipped(hidden, 1)

    filt = short_filter.transpose(1, 0, 2)
    gain = norm_gain[None]
    skip = skip_gain[None]
    dec, res = decay.T, residues.T
    inj = jnp.sqrt(-jnp.expm1(-2.0 * dec))
    jump = jnp.exp(-dec * count)
    from_cache = jnp.exp(-dec * (count * position)) * cached_state.T
    cache = jnp.pad(conv_cache.astype(F32), ((HALO - taps + 1, 0), (0, 0), (0, 0)))
    cache = cache.reshape(HALO, 3 * groups, LANES).transpose(1, 0, 2)
    tile = (groups, poles, SEGS, LANES)
    w = in_proj.transpose(1, 0, 2)
    w, inj, jump, from_cache, cache = lax.optimization_barrier((w, inj, jump, from_cache, cache))
    w, fac, rin, scan, span, end, reach = call(
        functools.partial(stage_kernel, seg, units),
        [
            kept(*w.shape, dtype=BF16), kept(*tile), kept(*tile),
            kept(3, *tile), kept(*tile), kept(*tile), kept(units, *tile),
        ],
        [pltpu.SemaphoreType.DMA((1,))],
        (w, dec, res, inj),
        anywhere=(0,),
    )

    def streams_of(rows, dtype=F32):
        return sds(3 * groups, rows, LANES, dtype=dtype)

    arrived, fac = lax.optimization_barrier((far[0], fac))
    fwd = flipped(arrived, 1)
    scale, tail, send, body = call(
        functools.partial(head_kernel, head),
        [sds(count, LANES), streams_of(TAIL), streams_of(HALO, BF16), streams_of(tokens)],
        [pltpu.VMEM((TAIL + tokens, D), BF16)],
        (own[0], sib, arrived, fwd, squares, gain, w),
    )
    prior = shifted(send, "context", 1)
    later = sum(sizes)
    part = call(
        functools.partial(near_kernel, rest),
        streams_of(later),
        [pltpu.VMEM((later, 2 * width), BF16)],
        (*own[1:], sib, scale, gain, w),
    )
    other, after = cache, part
    qs, zs, ends = [], [], []
    offset = 0
    for k, ((a, n), some) in enumerate(zip(rest, taken)):
        plane = (groups, some * tokens, LANES)
        arrived, after = lax.optimization_barrier((far[1 + k], after))
        fwd = flipped(arrived, 1)
        args = (arrived, fwd, scale, gain, w, part, filt, fac)
        own_rows = (body.shape[1] + HALO if k == 0 else prior.shape[1]) + n
        normed = pltpu.VMEM((n, 2 * width), BF16)
        if k < len(rest) - 1:
            q, z, e, sums, last = call(
                functools.partial(chunk_kernel, a, n, offset, some, seg, k == 0),
                [sds(*plane), sds(*plane), sds(some, *tile), sds(*tile), streams_of(own_rows - some * tokens)],
                [pltpu.VMEM((3 * groups, own_rows, LANES), F32), normed, pltpu.VMEM(plane, F32)],
                (*args, rin, span, skip, prior, other, body),
            )
            zs.append(z)
            ends.append(e)
            prior, other, after = last, sums, last
        else:
            q, p, end_state = call(
                functools.partial(last_kernel, a, n, offset, some, seg),
                [sds(*plane), sds(*plane), sds(groups * poles, LANES)],
                [pltpu.VMEM((3 * groups, own_rows + TAIL, LANES), F32), normed],
                (*args, span, end, prior, other, tail),
            )
        qs.append(q)
        offset += n
    paired = contexts == 4
    if paired:
        before = [
            lax.ppermute(end_state, "context", [(i, i ^ d) for i in range(contexts)]) for d in range(1, contexts)
        ]
    else:
        every = lax.all_gather(end_state.reshape(groups, poles, LANES), "context")
        gaps = position - 1.0 - jnp.arange(contexts, dtype=F32)
        rates = dec.reshape(poles, groups, LANES).transpose(1, 0, 2)
        weights = jnp.where(
            (gaps >= 0.0)[:, None, None, None],
            jnp.exp(-rates[None] * count * jnp.maximum(gaps, 0.0)[:, None, None, None]),
            0.0,
        )
        before = [jnp.sum(weights * every, axis=0).reshape(groups * poles, LANES)]
    z, begin = call(
        functools.partial(starts_kernel, seg),
        [sds(*plane), sds(units, *tile)],
        [pltpu.VMEM((taken[-1], *tile), F32)],
        (fac, rin, scan, skip, p, *ends),
    )
    zs.append(z)
    return call(
        functools.partial(final_kernel, units, seg, len(before), len(qs), paired),
        sds(count, chans, dtype=BF16),
        [pltpu.VMEM((units * groups, tokens, LANES), F32), pltpu.VMEM((groups, poles, LANES), F32)],
        (fac, reach, begin, inj, from_cache, jump, *before, *qs, *zs),
    )


def solution(mesh):
    placed = (
        P(("groups", "context"), "tensor"),
        P(),
        P(None, None, "tensor"),
        P(None, None, "tensor"),
        P("groups", None, "tensor"),
        P("tensor", None),
        P("tensor", None),
        P("tensor"),
        P(("groups", "tensor"), None),
    )
    return jax.shard_map(
        local,
        mesh=mesh,
        in_specs=placed,
        out_specs=P(("groups", "context"), "tensor"),
        check_vma=False,
    )
```

time: 62.2 us -> 55.2 us (0.89)
  waiting for transfers between devices: 14.9 us -> 5.99 us
  Pallas kernels: 27.4 us -> 29.8 us
    ppermute x9, waiting for transfers between devices: 12.2 us -> 3.08 us  [flipped(): return lax.ppermute(block, 'tensor', [(i, i ^ bit) for i in range(size)])]
    pallas_call x8 -> x9, Pallas kernels: 27.4 us -> 29.8 us  [call(): pl.pallas_call(kernel, out_shape=outs, in_specs=specs, out_specs=jax.tree...]
    ppermute x3, starting transfers between devices: 6.3 us -> 5.04 us  [local(): lax.ppermute(end_state, 'context', [(i, i ^ d) for i in range(contexts)])]
    ppermute x9, starting transfers between devices: 6.46 us -> 7.12 us  [flipped(): return lax.ppermute(block, 'tensor', [(i, i ^ bit) for i in range(size)])]
  transfers between devices with their start and end apart: 13 -> 13, of which waited for: 7 -> 4; matrix products, arithmetic and copies ran while one was open for 3% -> 3% of each run, Pallas kernels for 32% -> 41%
where the time goes in v3:
time: 55.2 us; the launch traced here: 54.8 us
  Pallas kernels  29.8 us (54%)
  starting transfers between devices  15.6 us (28%)
  waiting for transfers between devices  5.99 us (11%)
  other arithmetic  1.57 us (3%)
  local copies, waits for them, and re-layouts  1.57 us (3%)
    pallas_call x9, Pallas kernels, call(): pl.pallas_call(kernel, out_shape=outs, in_specs=specs, out_specs=jax.tree...  29.8 us
    ppermute x9, starting transfers between devices, flipped(): return lax.ppermute(block, 'tensor', [(i, i ^ bit) for i in range(size)])  7.12 us
    ppermute x3, starting transfers between devices, local(): lax.ppermute(end_state, 'context', [(i, i ^ d) for i in range(contexts)])  5.04 us
    ppermute x1, starting transfers between devices, shifted(): lax.ppermute(block, axis, [(i - distance, i) for i in range(distance, siz...  3.47 us
    ppermute x9, waiting for transfers between devices, flipped(): return lax.ppermute(block, 'tensor', [(i, i ^ bit) for i in range(size)])  3.08 us
    unnamed x10, local copies, waits for them, and re-layouts  1.53 us
    ppermute x1, waiting for transfers between devices, shifted(): lax.ppermute(block, axis, [(i - distance, i) for i in range(distance, siz...  1.5 us
    ppermute x3, waiting for transfers between devices, local(): lax.ppermute(end_state, 'context', [(i, i ^ d) for i in range(contexts)])  1.4 us
  transfers between devices with their start and end apart: 13, of which 4 were waited for; matrix products, arithmetic and copies ran while one was open for 3% of the time, Pallas kernels for 41%

profile of v3, /device:TPU:0, one launch (start us, length us, event | category | flops | bytes accessed | tf_op | source)
XLA Modules:
  0.0 54.8 jit_solution(13034082539545832921)
XLA Ops:
  0.0 1.6 %shard_map.91 = (bf16[96,1024]{1,0:T(8,128)(2,1)S(1)}, bf16[128,1024]{1,0:T(8,128)(2,1)S(1)}, bf16[144,1024]{1,0:T(8,128)(2,1)S(1)}, bf16[160,1024]{1,0:T(8,128)(2,1)S(1)}, f32[512,128]{1,0:T(8,128)S(1)}) custom-call(bf16[512,1024]{1,0:T(8,128)(2,1)} %h_any.1), custom_call_target="tpu_custom_call" | custom-call | bytes 1024 | tf_op jit(solution)/shard_map/pallas_call | solution.py:36
  1.6 0.6 %collective-permute-start.4 = (bf16[512,1024]{1,0:T(8,128)(2,1)}, bf16[512,1024]{1,0:T(8,128)(2,1)S(1)}, u32[]{:S(2)}, u32[]{:S(2)}) collective-permute-start(bf16[512,1024]{1,0:T(8,128)(2,1)} %h_any.1), channel_id=1, source_target_pairs={{0,1},{1,0},{2,3},{3,2},{4,5},{5,4},{6,7},{7,6},{8,9},{9,8},{10,11... | collective-permute-start | bytes 3145736 | tf_op jit(solution)/shard_map/ppermute | solution.py:30
  2.2 2.6 %collective-permute-start = (bf16[96,1024]{1,0:T(8,128)(2,1)S(1)}, bf16[96,1024]{1,0:T(8,128)(2,1)S(1)}, u32[]{:S(2)}, u32[]{:S(2)}) collective-permute-start(bf16[96,1024]{1,0:T(8,128)(2,1)S(1)} %get-tuple-element.66.a_ref), channel_id=1, source_target_pairs={{0,2},{1,3},{2,0},{3,1},{4,6},{5,7},{6,4},{7,5},{8,10},{9,11},{10,... | collective-permute-start | bytes 589832 | tf_op jit(solution)/shard_map/ppermute | solution.py:30
  4.7 0.1 collective-permute-start.3
  4.8 0.8 %bitcast_multiply_fusion = (f32[16,512]{1,0:T(8,128)S(1)}, f32[16,512]{1,0:T(8,128)S(1)}, f32[16,512]{1,0:T(8,128)S(1)}) fusion(f32[512,16]{0,1:T(8,128)} %param.17, f32[]{:T(128)S(6)} %mul.28, f32[512,16]{0,1:T(8,128)} %param.14), kind=kLoop, calls=%fused_computation.1 | loop fusion | flops 49152 | bytes 163844 | tf_op jit(solution)/shard_map/mul | solution.py:464
  5.6 0.8 %pad_convert_fusion = f32[8,3,512]{2,1,0:T(4,128)S(1)} fusion(bf16[6,3,512]{2,1,0:T(4,128)(2,1)} %param.13), kind=kLoop, calls=%fused_computation.2 | loop fusion | flops 12288 | bytes 67584 | tf_op jit(solution)/shard_map/transpose | solution.py:466
  6.5 0.0 copy-start.2
  6.5 0.7 %copy-done.2 = f32[512,16]{0,1:T(8,128)S(1)} copy-done((f32[512,16]{0,1:T(8,128)S(1)}, f32[512,16]{0,1:T(8,128)}, u32[]{:S(2)}) %copy-start.2) | copy-done | bytes 32792
  7.2 0.8 %copy-done.3 = f32[512,16]{0,1:T(8,128)S(1)} copy-done((f32[512,16]{0,1:T(8,128)S(1)}, f32[512,16]{0,1:T(8,128)}, u32[]{:S(2)}) %copy-start.3) | copy-done | bytes 32792
  8.0 4.6 %shard_map.92 = (bf16[3,4096,512]{2,1,0:T(8,128)(2,1)S(1)}, f32[4,16,8,128]{3,2,1,0:T(8,128)S(1)}, f32[4,16,8,128]{3,2,1,0:T(8,128)S(1)}, f32[3,4,16,8,128]{4,3,...) custom-call(bf16[3,4096,512]{2,1,0:T(8,128)(2,1)} %bitcast.28, ...), custom_call_target="tpu_custom_call" | custom-call | bytes 1024 | tf_op jit(solution)/shard_map/pallas_call | solution.py:36
  12.6 0.0 collective-permute-done.far_ref
  12.6 0.2 collective-permute-start.5
  12.8 1.9 %collective-permute-start.2 = (bf16[144,1024]{1,0:T(8,128)(2,1)S(1)}, bf16[144,1024]{1,0:T(8,128)(2,1)S(1)}, u32[]{:S(2)}, u32[]{:S(2)}) collective-permute-start(bf16[144,1024]{1,0:T(8,128)(2,1)S(1)} %get-tuple-element.63.refs_1_), channel_id=1, source_target_pairs={{0,2},{1,3},{2,0},{3,1},{4,6},{5,7},{6,4},{7,5},{8,10},{9,11},{10,... | collective-permute-start | bytes 884744 | tf_op jit(solution)/shard_map/ppermute | solution.py:30
  14.7 3.5 %shard_map.93 = (f32[512,128]{1,0:T(8,128)S(1)}, f32[12,16,128]{2,1,0:T(8,128)S(1)}, bf16[12,8,128]{2,1,0:T(8,128)(2,1)S(1)}, f32[12,64,128]{2,1,0:T(8,128)S(1)}) custom-call(bf16[96,1024]{1,0:T(8,128)(2,1)S(1)} %get-tuple-element.66.a_ref, bf16[512,1024]{1,0:T(8,128)(2,1)S(1)} %collective-permute-done.4.sib_ref.refs_3_, ...), custom_call_target="tpu_custom_call" | custom-call | bytes 1024 | tf_op jit(solution)/shard_map/pallas_call | solution.py:36
  18.2 0.0 copy-start.4
  18.2 4.5 %shard_map.94.part_ref = f32[12,432,128]{2,1,0:T(8,128)S(1)} custom-call(bf16[128,1024]{1,0:T(8,128)(2,1)S(1)} %get-tuple-element.62.refs_0_, bf16[144,1024]{1,0:T(8,128)(2,1)S(1)} %get-tuple-element.63.refs_1_, bf16[160,1024]{1,0:T(8,128)(2,1)S(1)} %get-tuple-element.64.refs_2_, bf16[512,1024]{1,0:T(8,128)(2,1)S(1)} %collective-permute-done.4.sib_ref.refs_3_, ...), custom_call_target="tpu_custom_call" | custom-call | bytes 1024 | tf_op jit(solution)/shard_map/pallas_call | solution.py:36
  22.7 0.2 collective-permute-start.6
  22.9 1.4 %collective-permute-start.1 = (bf16[160,1024]{1,0:T(8,128)(2,1)S(1)}, bf16[160,1024]{1,0:T(8,128)(2,1)S(1)}, u32[]{:S(2)}, u32[]{:S(2)}) collective-permute-start(bf16[160,1024]{1,0:T(8,128)(2,1)S(1)} %get-tuple-element.64.refs_2_), channel_id=1, source_target_pairs={{0,2},{1,3},{2,0},{3,1},{4,6},{5,7},{6,4},{7,5},{8,10},{9,11},{10,... | collective-permute-start | bytes 983048 | tf_op jit(solution)/shard_map/ppermute | solution.py:30
  24.3 3.5 %collective-permute-start.7 = (bf16[12,8,128]{2,1,0:T(8,128)(2,1)S(1)}, bf16[12,8,128]{2,1,0:T(8,128)(2,1)S(1)}, u32[]{:S(2)}, u32[]{:S(2)}) collective-permute-start(bf16[12,8,128]{2,1,0:T(8,128)(2,1)S(1)} %get-tuple-element.73), channel_id=1, source_target_pairs={{0,4},{4,8},{8,12},{1,5},{5,9},{9,13},{2,6},{6,10},{10,14},{3,7},{... | collective-permute-start | bytes 73736 | tf_op jit(solution)/shard_map/ppermute | solution.py:25
  27.8 1.5 %collective-permute-done.7.prior_ref = bf16[12,8,128]{2,1,0:T(8,128)(2,1)S(1)} collective-permute-done((bf16[12,8,128]{2,1,0:T(8,128)(2,1)S(1)}, bf16[12,8,128]{2,1,0:T(8,128)(2,1)S(1)}, u32[]{:S(2)}, u32[]{:S(2)}) %collective-permute-start.7) | collective-permute-done | bytes 24608 | tf_op jit(solution)/shard_map/ppermute | solution.py:25
  29.3 3.7 %shard_map.95 = (f32[4,192,128]{2,1,0:T(8,128)S(1)}, f32[4,192,128]{2,1,0:T(8,128)S(1)}, f32[3,4,16,8,128]{4,3,2,1,0:T(8,128)S(1)}, f32[4,16,8,128]{3,2,1,0:T(8,128)S(1)}, f32[12,8,128]{2,1,0:T(8,128)S(1)}) custom-call(bf16[128,1024]{1,0:T(8,128)(2,1)S(1)} %collective-permute-done.3.far_ref, bf16[128,1024]{1,0:T(8,128)(2,1)S(1)} %collective-permute-done.6.fwd_ref, ...), custom_call_target="tpu_custom_call" | custom-call | bytes 1024 | tf_op jit(solution)/shard_map/pallas_call | solution.py:36
  32.9 0.1 collective-permute-start.8
  33.0 1.6 %collective-permute-done.8.fwd_ref = bf16[144,1024]{1,0:T(8,128)(2,1)S(1)} collective-permute-done((bf16[144,1024]{1,0:T(8,128)(2,1)S(1)}, bf16[144,1024]{1,0:T(8,128)(2,1)S(1)}, u32[]{:S(2)}, u32[]{:S(2)}) %collective-permute-start.8) | collective-permute-done | bytes 294944 | tf_op jit(solution)/shard_map/ppermute | solution.py:30
  34.6 3.2 %shard_map.96 = (f32[4,128,128]{2,1,0:T(8,128)S(1)}, f32[4,128,128]{2,1,0:T(8,128)S(1)}, f32[2,4,16,8,128]{4,3,2,1,0:T(8,128)S(1)}, f32[4,16,8,128]{3,2,1,0:T(8,128)S(1)}, f32[12,24,128]{2,1,0:T(8,128)S(1)}) custom-call(bf16[144,1024]{1,0:T(8,128)(2,1)S(1)} %collective-permute-done.2.far_ref, bf16[144,1024]{1,0:T(8,128)(2,1)S(1)} %collective-permute-done.8.fwd_ref, ...), custom_call_target="tpu_custom_call" | custom-call | bytes 1024 | tf_op jit(solution)/shard_map/pallas_call | solution.py:36
  37.8 0.2 collective-permute-start.9
  38.0 1.5 %collective-permute-done.9.fwd_ref = bf16[160,1024]{1,0:T(8,128)(2,1)S(1)} collective-permute-done((bf16[160,1024]{1,0:T(8,128)(2,1)S(1)}, bf16[160,1024]{1,0:T(8,128)(2,1)S(1)}, u32[]{:S(2)}, u32[]{:S(2)}) %collective-permute-start.9) | collective-permute-done | bytes 327712 | tf_op jit(solution)/shard_map/ppermute | solution.py:30
  39.5 3.4 %shard_map.97 = (f32[4,192,128]{2,1,0:T(8,128)S(1)}, f32[4,192,128]{2,1,0:T(8,128)S(1)}, f32[64,128]{1,0:T(8,128)S(1)}) custom-call(bf16[160,1024]{1,0:T(8,128)(2,1)S(1)} %collective-permute-done.1.far_ref, bf16[160,1024]{1,0:T(8,128)(2,1)S(1)} %collective-permute-done.9.fwd_ref, f32[512,128]{1,0:T(8,128)S(1)} %get-tuple-element.70.refs_4_.scale_ref, ...), custom_call_target="tpu_custom_call" | custom-call | bytes 1024 | tf_op jit(solution)/shard_map/pallas_call | solution.py:36
  43.0 4.4 %collective-permute-start.12 = (f32[64,128]{1,0:T(8,128)S(1)}, f32[64,128]{1,0:T(8,128)S(1)}, u32[]{:S(2)}, u32[]{:S(2)}) collective-permute-start(f32[64,128]{1,0:T(8,128)S(1)} %get-tuple-element.90), channel_id=1, source_target_pairs={{0,12},{4,8},{8,4},{12,0},{1,13},{5,9},{9,5},{13,1},{2,14},{6,10},... | collective-permute-start | bytes 98312 | tf_op jit(solution)/shard_map/ppermute | solution.py:532
  47.4 0.6 %collective-permute-start.10 = (f32[64,128]{1,0:T(8,128)S(1)}, f32[64,128]{1,0:T(8,128)S(1)}, u32[]{:S(2)}, u32[]{:S(2)}) collective-permute-start(f32[64,128]{1,0:T(8,128)S(1)} %get-tuple-element.90), channel_id=1, source_target_pairs={{0,4},{4,0},{8,12},{12,8},{1,5},{5,1},{9,13},{13,9},{2,6},{6,2},{1... | collective-permute-start | bytes 98312 | tf_op jit(solution)/shard_map/ppermute | solution.py:532
  48.0 2.8 %shard_map.98 = (f32[4,192,128]{2,1,0:T(8,128)S(1)}, f32[8,4,16,8,128]{4,3,2,1,0:T(8,128)S(1)}) custom-call(f32[4,16,8,128]{3,2,1,0:T(8,128)S(1)} %get-tuple-element.55.fac_ref, f32[4,16,8,128]{3,2,1,0:T(8,128)S(1)} %get-tuple-element.57.rin_ref, f32[3,4,16,8,128]{4,3,2,1,0:T(8,128)S(1)} %get-tuple-element.58.scan_ref, f32[1,512]{1,0:T(1,128)S(1)} %bitcast.27, ...), custom_call_target="tpu_custom_call" | custom-call | bytes 1024 | tf_op jit(solution)/shard_map/pallas_call | solution.py:36
  50.8 1.4 %collective-permute-done.11.refs_1_ = f32[64,128]{1,0:T(8,128)S(1)} collective-permute-done((f32[64,128]{1,0:T(8,128)S(1)}, f32[64,128]{1,0:T(8,128)S(1)}, u32[]{:S(2)}, u32[]{:S(2)}) %collective-permute-start.11) | collective-permute-done | bytes 32800 | tf_op jit(solution)/shard_map/ppermute | solution.py:532
  52.2 2.6 %shard_map.99 = bf16[512,512]{1,0:T(8,128)(2,1)} custom-call(f32[4,16,8,128]{3,2,1,0:T(8,128)S(1)} %get-tuple-element.55.fac_ref, f32[8,4,16,8,128]{4,3,2,1,0:T(8,128)S(1)} %get-tuple-element.56.reach_ref, f32[8,4,16,8,128]{4,3,2,1,0:T(8,128)S(1)} %get-tuple-element.87.begin_ref, f32[16,512]{1,0:T(8,128)S(1)} %get-tuple-element.53.inj_ref, ...), custom_call_target="tpu_custom_call" | custom-call | bytes 1024 | tf_op jit(solution)/shard_map/pallas_call | solution.py:36
  (17 shorter events, 0.1 us)
Async XLA Ops:
  1.6 13.1 %collective-permute-start.4 = (bf16[512,1024]{1,0:T(8,128)(2,1)}, bf16[512,1024]{1,0:T(8,128)(2,1)S(1)}, u32[]{:S(2)}, u32[]{:S(2)}) collective-permute-start(bf16[512,1024]{1,0:T(8,128)(2,1)} %h_any.1), channel_id=1, source_target_pairs={{0,1},{1,0},{2,3},{3,2},{4,5},{5,4},{6,7},{7,6},{8,9},{9,8},{10,11... | collective-permute-start | bytes 3145736 | tf_op jit(solution)/shard_map/ppermute | solution.py:30
  2.2 10.4 %collective-permute-start = (bf16[96,1024]{1,0:T(8,128)(2,1)S(1)}, bf16[96,1024]{1,0:T(8,128)(2,1)S(1)}, u32[]{:S(2)}, u32[]{:S(2)}) collective-permute-start(bf16[96,1024]{1,0:T(8,128)(2,1)S(1)} %get-tuple-element.66.a_ref), channel_id=1, source_target_pairs={{0,2},{1,3},{2,0},{3,1},{4,6},{5,7},{6,4},{7,5},{8,10},{9,11},{10,... | collective-permute-start | bytes 589832 | tf_op jit(solution)/shard_map/ppermute | solution.py:30
  4.7 18.0 %collective-permute-start.3 = (bf16[128,1024]{1,0:T(8,128)(2,1)S(1)}, bf16[128,1024]{1,0:T(8,128)(2,1)S(1)}, u32[]{:S(2)}, u32[]{:S(2)}) collective-permute-start(bf16[128,1024]{1,0:T(8,128)(2,1)S(1)} %get-tuple-element.62.refs_0_), channel_id=1, source_target_pairs={{0,2},{1,3},{2,0},{3,1},{4,6},{5,7},{6,4},{7,5},{8,10},{9,11},{10,... | collective-permute-start | bytes 786440 | tf_op jit(solution)/shard_map/ppermute | solution.py:30
  6.5 0.8 %copy-start.2 = (f32[512,16]{0,1:T(8,128)S(1)}, f32[512,16]{0,1:T(8,128)}, u32[]{:S(2)}) copy-start(f32[512,16]{0,1:T(8,128)} %param.14) | copy-start | bytes 98308
  7.2 0.8 %copy-start.3 = (f32[512,16]{0,1:T(8,128)S(1)}, f32[512,16]{0,1:T(8,128)}, u32[]{:S(2)}) copy-start(f32[512,16]{0,1:T(8,128)} %param.15) | copy-start | bytes 98308
  8.0 6.7 %copy-start.1 = (f32[4096]{0:T(1024)S(1)}, f32[4096]{0:T(1024)}, u32[]{:S(2)}) copy-start(f32[4096]{0:T(1024)} %param.10) | copy-start | bytes 49156
  12.6 2.1 %collective-permute-start.5 = (bf16[96,1024]{1,0:T(8,128)(2,1)S(1)}, bf16[96,1024]{1,0:T(8,128)(2,1)S(1)}, u32[]{:S(2)}, u32[]{:S(2)}) collective-permute-start(bf16[96,1024]{1,0:T(8,128)(2,1)S(1)} %collective-permute-done.far_ref), channel_id=1, source_target_pairs={{0,1},{1,0},{2,3},{3,2},{4,5},{5,4},{6,7},{7,6},{8,9},{9,8},{10,11... | collective-permute-start | bytes 589832 | tf_op jit(solution)/shard_map/ppermute | solution.py:30
  12.8 20.2 %collective-permute-start.2 = (bf16[144,1024]{1,0:T(8,128)(2,1)S(1)}, bf16[144,1024]{1,0:T(8,128)(2,1)S(1)}, u32[]{:S(2)}, u32[]{:S(2)}) collective-permute-start(bf16[144,1024]{1,0:T(8,128)(2,1)S(1)} %get-tuple-element.63.refs_1_), channel_id=1, source_target_pairs={{0,2},{1,3},{2,0},{3,1},{4,6},{5,7},{6,4},{7,5},{8,10},{9,11},{10,... | collective-permute-start | bytes 884744 | tf_op jit(solution)/shard_map/ppermute | solution.py:30
  18.2 11.1 %copy-start = (f32[7,3,512]{2,0,1:T(8,128)S(1)}, f32[7,3,512]{2,0,1:T(8,128)}, u32[]{:S(2)}) copy-start(f32[7,3,512]{2,0,1:T(8,128)} %param.12) | copy-start | bytes 129028
  18.2 11.1 %copy-start.4 = (f32[512]{0:T(512)S(1)}, f32[512]{0:T(512)}, u32[]{:S(2)}) copy-start(f32[512]{0:T(512)} %param.16) | copy-start | bytes 6148
  22.7 6.6 %collective-permute-start.6 = (bf16[128,1024]{1,0:T(8,128)(2,1)S(1)}, bf16[128,1024]{1,0:T(8,128)(2,1)S(1)}, u32[]{:S(2)}, u32[]{:S(2)}) collective-permute-start(bf16[128,1024]{1,0:T(8,128)(2,1)S(1)} %collective-permute-done.3.far_ref), channel_id=1, source_target_pairs={{0,1},{1,0},{2,3},{3,2},{4,5},{5,4},{6,7},{7,6},{8,9},{9,8},{10,11... | collective-permute-start | bytes 786440 | tf_op jit(solution)/shard_map/ppermute | solution.py:30
  22.9 14.9 %collective-permute-start.1 = (bf16[160,1024]{1,0:T(8,128)(2,1)S(1)}, bf16[160,1024]{1,0:T(8,128)(2,1)S(1)}, u32[]{:S(2)}, u32[]{:S(2)}) collective-permute-start(bf16[160,1024]{1,0:T(8,128)(2,1)S(1)} %get-tuple-element.64.refs_2_), channel_id=1, source_target_pairs={{0,2},{1,3},{2,0},{3,1},{4,6},{5,7},{6,4},{7,5},{8,10},{9,11},{10,... | collective-permute-start | bytes 983048 | tf_op jit(solution)/shard_map/ppermute | solution.py:30
  24.3 5.0 %collective-permute-start.7 = (bf16[12,8,128]{2,1,0:T(8,128)(2,1)S(1)}, bf16[12,8,128]{2,1,0:T(8,128)(2,1)S(1)}, u32[]{:S(2)}, u32[]{:S(2)}) collective-permute-start(bf16[12,8,128]{2,1,0:T(8,128)(2,1)S(1)} %get-tuple-element.73), channel_id=1, source_target_pairs={{0,4},{4,8},{8,12},{1,5},{5,9},{9,13},{2,6},{6,10},{10,14},{3,7},{... | collective-permute-start | bytes 73736 | tf_op jit(solution)/shard_map/ppermute | solution.py:25
  32.9 1.6 %collective-permute-start.8 = (bf16[144,1024]{1,0:T(8,128)(2,1)S(1)}, bf16[144,1024]{1,0:T(8,128)(2,1)S(1)}, u32[]{:S(2)}, u32[]{:S(2)}) collective-permute-start(bf16[144,1024]{1,0:T(8,128)(2,1)S(1)} %collective-permute-done.2.far_ref), channel_id=1, source_target_pairs={{0,1},{1,0},{2,3},{3,2},{4,5},{5,4},{6,7},{7,6},{8,9},{9,8},{10,11... | collective-permute-start | bytes 884744 | tf_op jit(solution)/shard_map/ppermute | solution.py:30
  37.8 1.7 %collective-permute-start.9 = (bf16[160,1024]{1,0:T(8,128)(2,1)S(1)}, bf16[160,1024]{1,0:T(8,128)(2,1)S(1)}, u32[]{:S(2)}, u32[]{:S(2)}) collective-permute-start(bf16[160,1024]{1,0:T(8,128)(2,1)S(1)} %collective-permute-done.1.far_ref), channel_id=1, source_target_pairs={{0,1},{1,0},{2,3},{3,2},{4,5},{5,4},{6,7},{7,6},{8,9},{9,8},{10,11... | collective-permute-start | bytes 983048 | tf_op jit(solution)/shard_map/ppermute | solution.py:30
  43.0 7.8 %collective-permute-start.12 = (f32[64,128]{1,0:T(8,128)S(1)}, f32[64,128]{1,0:T(8,128)S(1)}, u32[]{:S(2)}, u32[]{:S(2)}) collective-permute-start(f32[64,128]{1,0:T(8,128)S(1)} %get-tuple-element.90), channel_id=1, source_target_pairs={{0,12},{4,8},{8,4},{12,0},{1,13},{5,9},{9,5},{13,1},{2,14},{6,10},... | collective-permute-start | bytes 98312 | tf_op jit(solution)/shard_map/ppermute | solution.py:532
  47.4 4.8 %collective-permute-start.11 = (f32[64,128]{1,0:T(8,128)S(1)}, f32[64,128]{1,0:T(8,128)S(1)}, u32[]{:S(2)}, u32[]{:S(2)}) collective-permute-start(f32[64,128]{1,0:T(8,128)S(1)} %get-tuple-element.90), channel_id=1, source_target_pairs={{0,8},{4,12},{8,0},{12,4},{1,9},{5,13},{9,1},{13,5},{2,10},{6,14},... | collective-permute-start | bytes 98312 | tf_op jit(solution)/shard_map/ppermute | solution.py:532
  47.4 4.8 %collective-permute-start.10 = (f32[64,128]{1,0:T(8,128)S(1)}, f32[64,128]{1,0:T(8,128)S(1)}, u32[]{:S(2)}, u32[]{:S(2)}) collective-permute-start(f32[64,128]{1,0:T(8,128)S(1)} %get-tuple-element.90), channel_id=1, source_target_pairs={{0,4},{4,0},{8,12},{12,8},{1,5},{5,1},{9,13},{13,9},{2,6},{6,2},{1... | collective-permute-start | bytes 98312 | tf_op jit(solution)/shard_map/ppermute | solution.py:532

commit v4 on v3

--- a/solution.py
+++ b/solution.py
@@ -13,7 +13,7 @@
 SEGS = 8
 TAIL = 16
 HALO = 8
-NOTES = 16
+NOTES = 8
 
 VM = pl.BlockSpec(memory_space=pltpu.VMEM)
 F32 = jnp.float32
@@ -23,6 +23,11 @@
 def shifted(block, axis, distance):
     size = lax.axis_size(axis)
     return lax.ppermute(block, axis, [(i - distance, i) for i in range(distance, size)])
+
+
+def paired_with(block, bits):
+    size = lax.axis_size("context")
+    return lax.ppermute(block, "context", [(i, i ^ bits) for i in range(size)])
 
 
 def flipped(block, bit):
@@ -100,12 +105,27 @@
 
 
 def stage_kernel(
-    seg, chunks, w_any, dec_ref, res_ref, inj_ref,
-    w_ref, fac_ref, rin_ref, scan_ref, span_ref, end_ref, reach_ref, sem,
+    seg, chunks, w_any, dec_any, res_any, cache_any, inj_ref,
+    w_ref, fac_ref, rin_ref, scan_ref, span_ref, end_ref, reach_ref, prior_ref,
+    dec_ref, res_ref, cache_ref, sem,
 ):
-    copies = [pltpu.make_async_copy(w_any, w_ref, sem.at[0])]
-    for copy in copies:
+    weights = pltpu.make_async_copy(w_any, w_ref, sem.at[0])
+    small = [
+        pltpu.make_async_copy(dec_any, dec_ref, sem.at[1]),
+        pltpu.make_async_copy(res_any, res_ref, sem.at[2]),
+        pltpu.make_async_copy(cache_any, cache_ref, sem.at[3]),
+    ]
+    for copy in (*small, weights):
         copy.start()
+    for copy in small:
+        copy.wait()
+    cache = cache_ref[...].astype(F32)
+    streams, chans = cache.shape[1:]
+    for i in range(streams):
+        for g in range(chans // LANES):
+            rows = cache[:, i, g * LANES : (g + 1) * LANES]
+            rows = jnp.concatenate([jnp.zeros((HALO - rows.shape[0], LANES), F32), rows], axis=0)
+            prior_ref[i * (chans // LANES) + g] = rows
     groups, poles = fac_ref.shape[0], fac_ref.shape[1]
     row = lax.broadcasted_iota(jnp.int32, (SEGS, LANES), 0)
     rowf = row.astype(F32)
@@ -127,8 +147,7 @@
         return c
 
     lax.fori_loop(0, groups, body, 0)
-    for copy in copies:
-        copy.wait()
+    weights.wait()
 
 
 def normed_block(ref, rows, scale_ref, start, gain_ref, index):
@@ -205,21 +224,21 @@
     count = squares_ref.shape[0]
     at = far_ref.shape[0] - NOTES
     notes = jnp.zeros((1, count), F32)
-    for ref in (far_ref, fwd_ref):
+    for ref in (sib_ref, far_ref, fwd_ref):
         coded = ref[at:, :count].astype(F32)
         notes = notes + ((coded[0:1] + coded[1:2]) + coded[2:3])
     for row in range(0, count, LANES):
         rows = slice(row, row + LANES)
         others = jnp.transpose(jnp.broadcast_to(notes[:, rows], (LANES, LANES)))
-        near = jnp.sum(squares_ref[rows, :] + row_squares(sib_ref, rows), axis=1, keepdims=True)
-        scale_ref[rows, :] = lax.rsqrt((near + others) / D + EPS)
+        mine = jnp.sum(squares_ref[rows, :], axis=1, keepdims=True)
+        scale_ref[rows, :] = lax.rsqrt((mine + others) / D + EPS)
     at = 0
     for start, rows in parts:
         here = slice(at, at + rows)
-        there = slice(start, start + rows)
         at += rows
-        for index, ref, where in ((t, a_ref, here), (t ^ 1, sib_ref, there), (t ^ 2, far_ref, here), (t ^ 3, fwd_ref, here)):
-            put_block(normed_ref, here, index, normed_block(ref, where, scale_ref, start, gain_ref, index))
+        for bits, ref in enumerate((a_ref, sib_ref, far_ref, fwd_ref)):
+            index = t ^ bits
+            put_block(normed_ref, here, index, normed_block(ref, here, scale_ref, start, gain_ref, index))
 
     def put(at, products):
         streams = rounded(products)
@@ -266,15 +285,18 @@
 def chunk_kernel(
     start, rows, offset, units, seg, first,
     far_ref, fwd_ref, scale_ref, gain_ref, w_ref, part_ref, filt_ref, fac_ref, rin_ref, span_ref, skip_ref,
-    prior_ref, other_ref, body_ref,
-    q_ref, z_ref, ends_ref, sum_ref, last_ref,
-    ext_ref, normed_ref, prod_ref,
+    other_ref, body_ref, *refs,
 ):
+    *prior_refs, q_ref, z_ref, ends_ref, sum_ref, last_ref, ext_ref, normed_ref, prod_ref = refs
+    prior_ref = prior_refs[0]
     groups, poles = fac_ref.shape[0], fac_ref.shape[1]
     tokens = seg * SEGS
     if first:
+        position = lax.axis_index("context")
         got = prior_ref[...].astype(F32)
-        ext_ref[:, :HALO, :] = jnp.where(lax.axis_index("context") == 0, other_ref[...], got)
+        if len(prior_refs) > 1:
+            got = jnp.where((position & 1) == 1, got, prior_refs[1][...].astype(F32))
+        ext_ref[:, :HALO, :] = jnp.where(position == 0, other_ref[...], got)
         base = HALO + body_ref.shape[1]
         ext_ref[:, HALO:base, :] = body_ref[...]
     else:
@@ -452,9 +474,6 @@
         anywhere=(0,),
     )
     far = [flipped(block, 2) for block in own]
-    hidden, own = lax.optimization_barrier((hidden, own))
-    sib = flipped(hidden, 1)
-
     filt = short_filter.transpose(1, 0, 2)
     gain = norm_gain[None]
     skip = skip_gain[None]
@@ -462,34 +481,39 @@
     inj = jnp.sqrt(-jnp.expm1(-2.0 * dec))
     jump = jnp.exp(-dec * count)
     from_cache = jnp.exp(-dec * (count * position)) * cached_state.T
-    cache = jnp.pad(conv_cache.astype(F32), ((HALO - taps + 1, 0), (0, 0), (0, 0)))
-    cache = cache.reshape(HALO, 3 * groups, LANES).transpose(1, 0, 2)
     tile = (groups, poles, SEGS, LANES)
     w = in_proj.transpose(1, 0, 2)
-    w, inj, jump, from_cache, cache = lax.optimization_barrier((w, inj, jump, from_cache, cache))
-    w, fac, rin, scan, span, end, reach = call(
+    w, inj, jump, from_cache = lax.optimization_barrier((w, inj, jump, from_cache))
+    w, fac, rin, scan, span, end, reach, cache = call(
         functools.partial(stage_kernel, seg, units),
         [
             kept(*w.shape, dtype=BF16), kept(*tile), kept(*tile),
-            kept(3, *tile), kept(*tile), kept(*tile), kept(units, *tile),
+            kept(3, *tile), kept(*tile), kept(*tile), kept(units, *tile), kept(3 * groups, HALO, LANES),
         ],
-        [pltpu.SemaphoreType.DMA((1,))],
-        (w, dec, res, inj),
-        anywhere=(0,),
+        [
+            pltpu.VMEM(dec.shape, F32), pltpu.VMEM(res.shape, F32), pltpu.VMEM(conv_cache.shape, BF16),
+            pltpu.SemaphoreType.DMA((4,)),
+        ],
+        (w, dec, res, conv_cache, inj),
+        anywhere=(0, 1, 2, 3),
     )
 
     def streams_of(rows, dtype=F32):
         return sds(3 * groups, rows, LANES, dtype=dtype)
 
-    arrived, fac = lax.optimization_barrier((far[0], fac))
-    fwd = flipped(arrived, 1)
+    arrived, mine, hidden, fac = lax.optimization_barrier((far[0], own[0], hidden, fac))
+    fwd, sib_first = flipped(arrived, 1), flipped(mine, 1)
+    sib = flipped(hidden, 1)
     scale, tail, send, body = call(
         functools.partial(head_kernel, head),
         [sds(count, LANES), streams_of(TAIL), streams_of(HALO, BF16), streams_of(tokens)],
         [pltpu.VMEM((TAIL + tokens, D), BF16)],
-        (own[0], sib, arrived, fwd, squares, gain, w),
-    )
-    prior = shifted(send, "context", 1)
+        (own[0], sib_first, arrived, fwd, squares, gain, w),
+    )
+    if contexts == 4:
+        prior = paired_with(send, 1), paired_with(send, 3)
+    else:
+        prior = (shifted(send, "context", 1),)
     later = sum(sizes)
     part = call(
         functools.partial(near_kernel, rest),
@@ -503,34 +527,32 @@
     for k, ((a, n), some) in enumerate(zip(rest, taken)):
         plane = (groups, some * tokens, LANES)
         arrived, after = lax.optimization_barrier((far[1 + k], after))
-        fwd = flipped(arrived, 1)
+        fwd = after = flipped(arrived, 1)
         args = (arrived, fwd, scale, gain, w, part, filt, fac)
-        own_rows = (body.shape[1] + HALO if k == 0 else prior.shape[1]) + n
+        own_rows = (body.shape[1] + HALO if k == 0 else prior[0].shape[1]) + n
         normed = pltpu.VMEM((n, 2 * width), BF16)
         if k < len(rest) - 1:
             q, z, e, sums, last = call(
                 functools.partial(chunk_kernel, a, n, offset, some, seg, k == 0),
                 [sds(*plane), sds(*plane), sds(some, *tile), sds(*tile), streams_of(own_rows - some * tokens)],
                 [pltpu.VMEM((3 * groups, own_rows, LANES), F32), normed, pltpu.VMEM(plane, F32)],
-                (*args, rin, span, skip, prior, other, body),
+                (*args, rin, span, skip, other, body, *prior),
             )
             zs.append(z)
             ends.append(e)
-            prior, other, after = last, sums, last
+            prior, other, after = (last,), sums, last if k else after
         else:
             q, p, end_state = call(
                 functools.partial(last_kernel, a, n, offset, some, seg),
                 [sds(*plane), sds(*plane), sds(groups * poles, LANES)],
                 [pltpu.VMEM((3 * groups, own_rows + TAIL, LANES), F32), normed],
-                (*args, span, end, prior, other, tail),
+                (*args, span, end, *prior, other, tail),
             )
         qs.append(q)
         offset += n
     paired = contexts == 4
     if paired:
-        before = [
-            lax.ppermute(end_state, "context", [(i, i ^ d) for i in range(contexts)]) for d in range(1, contexts)
-        ]
+        before = [paired_with(end_state, d) for d in range(1, contexts)]
     else:
         every = lax.all_gather(end_state.reshape(groups, poles, LANES), "context")
         gaps = position - 1.0 - jnp.arange(contexts, dtype=F32)

time: 55.2 us -> 55.4 us (level)
  waiting for transfers between devices: 5.99 us -> 9.55 us
  local copies, waits for them, and re-layouts: 1.57 us -> 0.08 us
  starting transfers between devices: 15.6 us -> 14.7 us
  other arithmetic: 1.57 us -> 0.81 us
    ppermute x9 -> x10, waiting for transfers between devices: 3.08 us -> 5.72 us  [flipped(): return lax.ppermute(block, 'tensor', [(i, i ^ bit) for i in range(size)])]
    unnamed x10 -> x8, local copies, waits for them, and re-layouts: 1.53 us -> 0.08 us
    ppermute x4 -> x5, waiting for transfers between devices: 2.91 us -> 3.83 us  [paired_with(): return lax.ppermute(block, 'context', [(i, i ^ bits) for i in range(size)])]
    transpose x1 -> x0, other arithmetic: 0.75 us -> none  [local(): cache = cache.reshape(HALO, 3 * groups, LANES).transpose(1, 0, 2)]
    ppermute x9 -> x10, starting transfers between devices: 7.12 us -> 6.64 us  [flipped(): return lax.ppermute(block, 'tensor', [(i, i ^ bit) for i in range(size)])]
    ppermute x4 -> x5, starting transfers between devices: 8.52 us -> 8.06 us  [paired_with(): return lax.ppermute(block, 'context', [(i, i ^ bits) for i in range(size)])]
  transfers between devices with their start and end apart: 13 -> 15, of which waited for: 4 -> 6; matrix products, arithmetic and copies ran while one was open for 3% -> 1% of each run, Pallas kernels for 41% -> 40%
where the time goes in v4:
time: 55.4 us; the launch traced here: 55.2 us
  Pallas kernels  29.9 us (54%)
  starting transfers between devices  14.7 us (27%)
  waiting for transfers between devices  9.55 us (17%)
  other arithmetic  0.81 us (1%)
    pallas_call x9, Pallas kernels, call(): pl.pallas_call(kernel, out_shape=outs, in_specs=specs, out_specs=jax.tree...  29.9 us
    ppermute x5, starting transfers between devices, paired_with(): return lax.ppermute(block, 'context', [(i, i ^ bits) for i in range(size)])  8.06 us
    ppermute x10, starting transfers between devices, flipped(): return lax.ppermute(block, 'tensor', [(i, i ^ bit) for i in range(size)])  6.64 us
    ppermute x10, waiting for transfers between devices, flipped(): return lax.ppermute(block, 'tensor', [(i, i ^ bit) for i in range(size)])  5.72 us
    ppermute x5, waiting for transfers between devices, paired_with(): return lax.ppermute(block, 'context', [(i, i ^ bits) for i in range(size)])  3.83 us
  transfers between devices with their start and end apart: 15, of which 6 were waited for; matrix products, arithmetic and copies ran while one was open for 1% of the time, Pallas kernels for 40%

profile of v4, /device:TPU:0, one launch (start us, length us, event | category | flops | bytes accessed | tf_op | source)
XLA Modules:
  0.0 55.2 jit_solution(7797231255859230990)
XLA Ops:
  0.0 1.6 %shard_map.91 = (bf16[88,1024]{1,0:T(8,128)(2,1)S(1)}, bf16[128,1024]{1,0:T(8,128)(2,1)S(1)}, bf16[144,1024]{1,0:T(8,128)(2,1)S(1)}, bf16[160,1024]{1,0:T(8,128)(2,1)S(1)}, f32[512,128]{1,0:T(8,128)S(1)}) custom-call(bf16[512,1024]{1,0:T(8,128)(2,1)} %h_any.1), custom_call_target="tpu_custom_call" | custom-call | bytes 1024 | tf_op jit(solution)/shard_map/pallas_call | solution.py:41
  1.6 3.0 %collective-permute-start = (bf16[88,1024]{1,0:T(8,128)(2,1)S(1)}, bf16[88,1024]{1,0:T(8,128)(2,1)S(1)}, u32[]{:S(2)}, u32[]{:S(2)}) collective-permute-start(bf16[88,1024]{1,0:T(8,128)(2,1)S(1)} %get-tuple-element.60.a_ref), channel_id=1, source_target_pairs={{0,2},{1,3},{2,0},{3,1},{4,6},{5,7},{6,4},{7,5},{8,10},{9,11},{10,... | collective-permute-start | bytes 540680 | tf_op jit(solution)/shard_map/ppermute | solution.py:35
  4.7 0.8 %bitcast_multiply_fusion = (f32[16,512]{1,0:T(8,128)S(1)}, f32[16,512]{1,0:T(8,128)S(1)}, f32[16,512]{1,0:T(8,128)S(1)}) fusion(f32[512,16]{0,1:T(8,128)} %param.17, f32[]{:T(128)S(6)} %mul.28, f32[512,16]{0,1:T(8,128)} %param.14), kind=kLoop, calls=%fused_computation | loop fusion | flops 49152 | bytes 163844 | tf_op jit(solution)/shard_map/mul | solution.py:483
  5.5 0.0 copy-start.3
  5.5 0.0 copy-start.1
  5.5 4.8 %shard_map.92 = (bf16[3,4096,512]{2,1,0:T(8,128)(2,1)S(1)}, f32[4,16,8,128]{3,2,1,0:T(8,128)S(1)}, f32[4,16,8,128]{3,2,1,0:T(8,128)S(1)}, f32[3,4,16,8,128]{4,3,...) custom-call(bf16[3,4096,512]{2,1,0:T(8,128)(2,1)} %bitcast.22, ...), custom_call_target="tpu_custom_call" | custom-call | bytes 1024 | tf_op jit(solution)/shard_map/pallas_call | solution.py:41
  10.3 0.1 copy-done.3
  10.3 0.0 collective-permute-start.4
  10.4 0.6 %collective-permute-start.3 = (bf16[128,1024]{1,0:T(8,128)(2,1)S(1)}, bf16[128,1024]{1,0:T(8,128)(2,1)S(1)}, u32[]{:S(2)}, u32[]{:S(2)}) collective-permute-start(bf16[128,1024]{1,0:T(8,128)(2,1)S(1)} %get-tuple-element.58.refs_0_), channel_id=1, source_target_pairs={{0,2},{1,3},{2,0},{3,1},{4,6},{5,7},{6,4},{7,5},{8,10},{9,11},{10,... | collective-permute-start | bytes 786440 | tf_op jit(solution)/shard_map/ppermute | solution.py:35
  11.0 0.2 collective-permute-start.5
  11.2 0.3 collective-permute-start.6
  11.5 1.5 %collective-permute-start.2 = (bf16[144,1024]{1,0:T(8,128)(2,1)S(1)}, bf16[144,1024]{1,0:T(8,128)(2,1)S(1)}, u32[]{:S(2)}, u32[]{:S(2)}) collective-permute-start(bf16[144,1024]{1,0:T(8,128)(2,1)S(1)} %get-tuple-element.57.refs_1_), channel_id=1, source_target_pairs={{0,2},{1,3},{2,0},{3,1},{4,6},{5,7},{6,4},{7,5},{8,10},{9,11},{10,... | collective-permute-start | bytes 884744 | tf_op jit(solution)/shard_map/ppermute | solution.py:35
  13.0 0.3 collective-permute-done.5.sib_ref
  13.3 0.3 collective-permute-done.6.fwd_ref
  13.5 3.4 %shard_map.93 = (f32[512,128]{1,0:T(8,128)S(1)}, f32[12,16,128]{2,1,0:T(8,128)S(1)}, bf16[12,8,128]{2,1,0:T(8,128)(2,1)S(1)}, f32[12,64,128]{2,1,0:T(8,128)S(1)}) custom-call(bf16[88,1024]{1,0:T(8,128)(2,1)S(1)} %get-tuple-element.60.a_ref, bf16[88,1024]{1,0:T(8,128)(2,1)S(1)} %collective-permute-done.5.sib_ref, ...), custom_call_target="tpu_custom_call" | custom-call | bytes 1024 | tf_op jit(solution)/shard_map/pallas_call | solution.py:41
  17.0 0.0 copy-start
  17.0 4.5 %shard_map.94.part_ref = f32[12,432,128]{2,1,0:T(8,128)S(1)} custom-call(bf16[128,1024]{1,0:T(8,128)(2,1)S(1)} %get-tuple-element.58.refs_0_, bf16[144,1024]{1,0:T(8,128)(2,1)S(1)} %get-tuple-element.57.refs_1_, bf16[160,1024]{1,0:T(8,128)(2,1)S(1)} %get-tuple-element.56.refs_2_, bf16[512,1024]{1,0:T(8,128)(2,1)S(1)} %collective-permute-done.4.refs_3_, ...), custom_call_target="tpu_custom_call" | custom-call | bytes 1024 | tf_op jit(solution)/shard_map/pallas_call | solution.py:41
  21.5 0.2 collective-permute-start.7
  21.7 0.7 %collective-permute-start.1 = (bf16[160,1024]{1,0:T(8,128)(2,1)S(1)}, bf16[160,1024]{1,0:T(8,128)(2,1)S(1)}, u32[]{:S(2)}, u32[]{:S(2)}) collective-permute-start(bf16[160,1024]{1,0:T(8,128)(2,1)S(1)} %get-tuple-element.56.refs_2_), channel_id=1, source_target_pairs={{0,2},{1,3},{2,0},{3,1},{4,6},{5,7},{6,4},{7,5},{8,10},{9,11},{10,... | collective-permute-start | bytes 983048 | tf_op jit(solution)/shard_map/ppermute | solution.py:35
  22.4 3.5 %collective-permute-done.2.far_ref = bf16[144,1024]{1,0:T(8,128)(2,1)S(1)} collective-permute-done((bf16[144,1024]{1,0:T(8,128)(2,1)S(1)}, bf16[144,1024]{1,0:T(8,128)(2,1)S(1)}, u32[]{:S(2)}, u32[]{:S(2)}) %collective-permute-start.2) | collective-permute-done | bytes 294944 | tf_op jit(solution)/shard_map/ppermute | solution.py:35
  25.9 3.6 %collective-permute-start.10 = (bf16[12,8,128]{2,1,0:T(8,128)(2,1)S(1)}, bf16[12,8,128]{2,1,0:T(8,128)(2,1)S(1)}, u32[]{:S(2)}, u32[]{:S(2)}) collective-permute-start(bf16[12,8,128]{2,1,0:T(8,128)(2,1)S(1)} %get-tuple-element.70), channel_id=1, source_target_pairs={{0,12},{4,8},{8,4},{12,0},{1,13},{5,9},{9,5},{13,1},{2,14},{6,10},... | collective-permute-start | bytes 73736 | tf_op jit(solution)/shard_map/ppermute | solution.py:30
  29.5 2.2 %collective-permute-done.10.refs_1_ = bf16[12,8,128]{2,1,0:T(8,128)(2,1)S(1)} collective-permute-done((bf16[12,8,128]{2,1,0:T(8,128)(2,1)S(1)}, bf16[12,8,128]{2,1,0:T(8,128)(2,1)S(1)}, u32[]{:S(2)}, u32[]{:S(2)}) %collective-permute-start.10) | collective-permute-done | bytes 24608 | tf_op jit(solution)/shard_map/ppermute | solution.py:30
  31.8 1.6 %collective-permute-done.9.refs_0_ = bf16[12,8,128]{2,1,0:T(8,128)(2,1)S(1)} collective-permute-done((bf16[12,8,128]{2,1,0:T(8,128)(2,1)S(1)}, bf16[12,8,128]{2,1,0:T(8,128)(2,1)S(1)}, u32[]{:S(2)}, u32[]{:S(2)}) %collective-permute-start.9) | collective-permute-done | bytes 24608 | tf_op jit(solution)/shard_map/ppermute | solution.py:30
  33.4 3.6 %shard_map.95 = (f32[4,192,128]{2,1,0:T(8,128)S(1)}, f32[4,192,128]{2,1,0:T(8,128)S(1)}, f32[3,4,16,8,128]{4,3,2,1,0:T(8,128)S(1)}, f32[4,16,8,128]{3,2,1,0:T(8,128)S(1)}, f32[12,8,128]{2,1,0:T(8,128)S(1)}) custom-call(bf16[128,1024]{1,0:T(8,128)(2,1)S(1)} %collective-permute-done.3.far_ref, bf16[128,1024]{1,0:T(8,128)(2,1)S(1)} %collective-permute-done.7.fwd_ref, ...), custom_call_target="tpu_custom_call" | custom-call | bytes 1024 | tf_op jit(solution)/shard_map/pallas_call | solution.py:41
  37.0 3.3 %shard_map.96 = (f32[4,128,128]{2,1,0:T(8,128)S(1)}, f32[4,128,128]{2,1,0:T(8,128)S(1)}, f32[2,4,16,8,128]{4,3,2,1,0:T(8,128)S(1)}, f32[4,16,8,128]{3,2,1,0:T(8,128)S(1)}, f32[12,24,128]{2,1,0:T(8,128)S(1)}) custom-call(bf16[144,1024]{1,0:T(8,128)(2,1)S(1)} %collective-permute-done.2.far_ref, bf16[144,1024]{1,0:T(8,128)(2,1)S(1)} %collective-permute-done.8.fwd_ref, ...), custom_call_target="tpu_custom_call" | custom-call | bytes 1024 | tf_op jit(solution)/shard_map/pallas_call | solution.py:41
  40.3 0.1 collective-permute-start.11
  40.4 1.6 %collective-permute-done.11.fwd_ref = bf16[160,1024]{1,0:T(8,128)(2,1)S(1)} collective-permute-done((bf16[160,1024]{1,0:T(8,128)(2,1)S(1)}, bf16[160,1024]{1,0:T(8,128)(2,1)S(1)}, u32[]{:S(2)}, u32[]{:S(2)}) %collective-permute-start.11) | collective-permute-done | bytes 327712 | tf_op jit(solution)/shard_map/ppermute | solution.py:35
  42.0 3.4 %shard_map.97 = (f32[4,192,128]{2,1,0:T(8,128)S(1)}, f32[4,192,128]{2,1,0:T(8,128)S(1)}, f32[64,128]{1,0:T(8,128)S(1)}) custom-call(bf16[160,1024]{1,0:T(8,128)(2,1)S(1)} %collective-permute-done.1.far_ref, bf16[160,1024]{1,0:T(8,128)(2,1)S(1)} %collective-permute-done.11.fwd_ref, f32[512,128]{1,0:T(8,128)S(1)} %get-tuple-element.64.refs_4_.scale_ref, ...), custom_call_target="tpu_custom_call" | custom-call | bytes 1024 | tf_op jit(solution)/shard_map/pallas_call | solution.py:41
  45.4 2.0 %collective-permute-start.14 = (f32[64,128]{1,0:T(8,128)S(1)}, f32[64,128]{1,0:T(8,128)S(1)}, u32[]{:S(2)}, u32[]{:S(2)}) collective-permute-start(f32[64,128]{1,0:T(8,128)S(1)} %get-tuple-element.84), channel_id=1, source_target_pairs={{0,12},{4,8},{8,4},{12,0},{1,13},{5,9},{9,5},{13,1},{2,14},{6,10},... | collective-permute-start | bytes 98312 | tf_op jit(solution)/shard_map/ppermute | solution.py:30
  47.4 2.5 %collective-permute-start.12 = (f32[64,128]{1,0:T(8,128)S(1)}, f32[64,128]{1,0:T(8,128)S(1)}, u32[]{:S(2)}, u32[]{:S(2)}) collective-permute-start(f32[64,128]{1,0:T(8,128)S(1)} %get-tuple-element.84), channel_id=1, source_target_pairs={{0,4},{4,0},{8,12},{12,8},{1,5},{5,1},{9,13},{13,9},{2,6},{6,2},{1... | collective-permute-start | bytes 98312 | tf_op jit(solution)/shard_map/ppermute | solution.py:30
  49.9 2.7 %shard_map.98 = (f32[4,192,128]{2,1,0:T(8,128)S(1)}, f32[8,4,16,8,128]{4,3,2,1,0:T(8,128)S(1)}) custom-call(f32[4,16,8,128]{3,2,1,0:T(8,128)S(1)} %get-tuple-element.52.fac_ref, f32[4,16,8,128]{3,2,1,0:T(8,128)S(1)} %get-tuple-element.54.rin_ref, f32[3,4,16,8,128]{4,3,2,1,0:T(8,128)S(1)} %get-tuple-element.55.scan_ref, f32[1,512]{1,0:T(1,128)S(1)} %bitcast.21, ...), custom_call_target="tpu_custom_call" | custom-call | bytes 1024 | tf_op jit(solution)/shard_map/pallas_call | solution.py:41
  52.7 2.6 %shard_map.99 = bf16[512,512]{1,0:T(8,128)(2,1)} custom-call(f32[4,16,8,128]{3,2,1,0:T(8,128)S(1)} %get-tuple-element.52.fac_ref, f32[8,4,16,8,128]{4,3,2,1,0:T(8,128)S(1)} %get-tuple-element.53.reach_ref, f32[8,4,16,8,128]{4,3,2,1,0:T(8,128)S(1)} %get-tuple-element.81.begin_ref, f32[16,512]{1,0:T(8,128)S(1)} %get-tuple-element.50.inj_ref, ...), custom_call_target="tpu_custom_call" | custom-call | bytes 1024 | tf_op jit(solution)/shard_map/pallas_call | solution.py:41
  (16 shorter events, 0.0 us)
Async XLA Ops:
  1.6 8.6 %collective-permute-start = (bf16[88,1024]{1,0:T(8,128)(2,1)S(1)}, bf16[88,1024]{1,0:T(8,128)(2,1)S(1)}, u32[]{:S(2)}, u32[]{:S(2)}) collective-permute-start(bf16[88,1024]{1,0:T(8,128)(2,1)S(1)} %get-tuple-element.60.a_ref), channel_id=1, source_target_pairs={{0,2},{1,3},{2,0},{3,1},{4,6},{5,7},{6,4},{7,5},{8,10},{9,11},{10,... | collective-permute-start | bytes 540680 | tf_op jit(solution)/shard_map/ppermute | solution.py:35
  5.5 4.9 %copy-start.3 = (bf16[512,1024]{1,0:T(8,128)(2,1)S(1)}, bf16[512,1024]{1,0:T(8,128)(2,1)}, u32[]{:S(2)}) copy-start(bf16[512,1024]{1,0:T(8,128)(2,1)} %h_any.1) | copy-start | bytes 3145732
  5.5 8.0 %copy-start.1 = (f32[4096]{0:T(1024)S(1)}, f32[4096]{0:T(1024)}, u32[]{:S(2)}) copy-start(f32[4096]{0:T(1024)} %param.10) | copy-start | bytes 49156
  10.3 6.6 %collective-permute-start.4 = (bf16[512,1024]{1,0:T(8,128)(2,1)S(1)}, bf16[512,1024]{1,0:T(8,128)(2,1)S(1)}, u32[]{:S(2)}, u32[]{:S(2)}) collective-permute-start(bf16[512,1024]{1,0:T(8,128)(2,1)S(1)} %copy-done.3), channel_id=1, source_target_pairs={{0,1},{1,0},{2,3},{3,2},{4,5},{5,4},{6,7},{7,6},{8,9},{9,8},{10,11... | collective-permute-start | bytes 3145736 | tf_op jit(solution)/shard_map/ppermute | solution.py:35
  10.4 11.1 %collective-permute-start.3 = (bf16[128,1024]{1,0:T(8,128)(2,1)S(1)}, bf16[128,1024]{1,0:T(8,128)(2,1)S(1)}, u32[]{:S(2)}, u32[]{:S(2)}) collective-permute-start(bf16[128,1024]{1,0:T(8,128)(2,1)S(1)} %get-tuple-element.58.refs_0_), channel_id=1, source_target_pairs={{0,2},{1,3},{2,0},{3,1},{4,6},{5,7},{6,4},{7,5},{8,10},{9,11},{10,... | collective-permute-start | bytes 786440 | tf_op jit(solution)/shard_map/ppermute | solution.py:35
  11.0 2.3 %collective-permute-start.5 = (bf16[88,1024]{1,0:T(8,128)(2,1)S(1)}, bf16[88,1024]{1,0:T(8,128)(2,1)S(1)}, u32[]{:S(2)}, u32[]{:S(2)}) collective-permute-start(bf16[88,1024]{1,0:T(8,128)(2,1)S(1)} %get-tuple-element.60.a_ref), channel_id=1, source_target_pairs={{0,1},{1,0},{2,3},{3,2},{4,5},{5,4},{6,7},{7,6},{8,9},{9,8},{10,11... | collective-permute-start | bytes 540680 | tf_op jit(solution)/shard_map/ppermute | solution.py:35
  11.2 2.3 %collective-permute-start.6 = (bf16[88,1024]{1,0:T(8,128)(2,1)S(1)}, bf16[88,1024]{1,0:T(8,128)(2,1)S(1)}, u32[]{:S(2)}, u32[]{:S(2)}) collective-permute-start(bf16[88,1024]{1,0:T(8,128)(2,1)S(1)} %collective-permute-done.far_ref), channel_id=1, source_target_pairs={{0,1},{1,0},{2,3},{3,2},{4,5},{5,4},{6,7},{7,6},{8,9},{9,8},{10,11... | collective-permute-start | bytes 540680 | tf_op jit(solution)/shard_map/ppermute | solution.py:35
  11.5 14.5 %collective-permute-start.2 = (bf16[144,1024]{1,0:T(8,128)(2,1)S(1)}, bf16[144,1024]{1,0:T(8,128)(2,1)S(1)}, u32[]{:S(2)}, u32[]{:S(2)}) collective-permute-start(bf16[144,1024]{1,0:T(8,128)(2,1)S(1)} %get-tuple-element.57.refs_1_), channel_id=1, source_target_pairs={{0,2},{1,3},{2,0},{3,1},{4,6},{5,7},{6,4},{7,5},{8,10},{9,11},{10,... | collective-permute-start | bytes 884744 | tf_op jit(solution)/shard_map/ppermute | solution.py:35
  17.0 16.4 %copy-start = (f32[7,3,512]{2,0,1:T(8,128)S(1)}, f32[7,3,512]{2,0,1:T(8,128)}, u32[]{:S(2)}) copy-start(f32[7,3,512]{2,0,1:T(8,128)} %param.12) | copy-start | bytes 129028
  17.0 16.4 %copy-start.2 = (f32[512]{0:T(512)S(1)}, f32[512]{0:T(512)}, u32[]{:S(2)}) copy-start(f32[512]{0:T(512)} %param.16) | copy-start | bytes 6148
  21.5 4.4 %collective-permute-start.7 = (bf16[128,1024]{1,0:T(8,128)(2,1)S(1)}, bf16[128,1024]{1,0:T(8,128)(2,1)S(1)}, u32[]{:S(2)}, u32[]{:S(2)}) collective-permute-start(bf16[128,1024]{1,0:T(8,128)(2,1)S(1)} %collective-permute-done.3.far_ref), channel_id=1, source_target_pairs={{0,1},{1,0},{2,3},{3,2},{4,5},{5,4},{6,7},{7,6},{8,9},{9,8},{10,11... | collective-permute-start | bytes 786440 | tf_op jit(solution)/shard_map/ppermute | solution.py:35
  21.7 18.6 %collective-permute-start.1 = (bf16[160,1024]{1,0:T(8,128)(2,1)S(1)}, bf16[160,1024]{1,0:T(8,128)(2,1)S(1)}, u32[]{:S(2)}, u32[]{:S(2)}) collective-permute-start(bf16[160,1024]{1,0:T(8,128)(2,1)S(1)} %get-tuple-element.56.refs_2_), channel_id=1, source_target_pairs={{0,2},{1,3},{2,0},{3,1},{4,6},{5,7},{6,4},{7,5},{8,10},{9,11},{10,... | collective-permute-start | bytes 983048 | tf_op jit(solution)/shard_map/ppermute | solution.py:35
  25.9 11.1 %collective-permute-start.8 = (bf16[144,1024]{1,0:T(8,128)(2,1)S(1)}, bf16[144,1024]{1,0:T(8,128)(2,1)S(1)}, u32[]{:S(2)}, u32[]{:S(2)}) collective-permute-start(bf16[144,1024]{1,0:T(8,128)(2,1)S(1)} %collective-permute-done.2.far_ref), channel_id=1, source_target_pairs={{0,1},{1,0},{2,3},{3,2},{4,5},{5,4},{6,7},{7,6},{8,9},{9,8},{10,11... | collective-permute-start | bytes 884744 | tf_op jit(solution)/shard_map/ppermute | solution.py:35
  25.9 5.8 %collective-permute-start.10 = (bf16[12,8,128]{2,1,0:T(8,128)(2,1)S(1)}, bf16[12,8,128]{2,1,0:T(8,128)(2,1)S(1)}, u32[]{:S(2)}, u32[]{:S(2)}) collective-permute-start(bf16[12,8,128]{2,1,0:T(8,128)(2,1)S(1)} %get-tuple-element.70), channel_id=1, source_target_pairs={{0,12},{4,8},{8,4},{12,0},{1,13},{5,9},{9,5},{13,1},{2,14},{6,10},... | collective-permute-start | bytes 73736 | tf_op jit(solution)/shard_map/ppermute | solution.py:30
  29.5 3.8 %collective-permute-start.9 = (bf16[12,8,128]{2,1,0:T(8,128)(2,1)S(1)}, bf16[12,8,128]{2,1,0:T(8,128)(2,1)S(1)}, u32[]{:S(2)}, u32[]{:S(2)}) collective-permute-start(bf16[12,8,128]{2,1,0:T(8,128)(2,1)S(1)} %get-tuple-element.70), channel_id=1, source_target_pairs={{0,4},{4,0},{8,12},{12,8},{1,5},{5,1},{9,13},{13,9},{2,6},{6,2},{1... | collective-permute-start | bytes 73736 | tf_op jit(solution)/shard_map/ppermute | solution.py:30
  40.3 1.7 %collective-permute-start.11 = (bf16[160,1024]{1,0:T(8,128)(2,1)S(1)}, bf16[160,1024]{1,0:T(8,128)(2,1)S(1)}, u32[]{:S(2)}, u32[]{:S(2)}) collective-permute-start(bf16[160,1024]{1,0:T(8,128)(2,1)S(1)} %collective-permute-done.1.far_ref), channel_id=1, source_target_pairs={{0,1},{1,0},{2,3},{3,2},{4,5},{5,4},{6,7},{7,6},{8,9},{9,8},{10,11... | collective-permute-start | bytes 983048 | tf_op jit(solution)/shard_map/ppermute | solution.py:35
  45.4 7.2 %collective-permute-start.14 = (f32[64,128]{1,0:T(8,128)S(1)}, f32[64,128]{1,0:T(8,128)S(1)}, u32[]{:S(2)}, u32[]{:S(2)}) collective-permute-start(f32[64,128]{1,0:T(8,128)S(1)} %get-tuple-element.84), channel_id=1, source_target_pairs={{0,12},{4,8},{8,4},{12,0},{1,13},{5,9},{9,5},{13,1},{2,14},{6,10},... | collective-permute-start | bytes 98312 | tf_op jit(solution)/shard_map/ppermute | solution.py:30
  47.4 5.2 %collective-permute-start.13 = (f32[64,128]{1,0:T(8,128)S(1)}, f32[64,128]{1,0:T(8,128)S(1)}, u32[]{:S(2)}, u32[]{:S(2)}) collective-permute-start(f32[64,128]{1,0:T(8,128)S(1)} %get-tuple-element.84), channel_id=1, source_target_pairs={{0,8},{4,12},{8,0},{12,4},{1,9},{5,13},{9,1},{13,5},{2,10},{6,14},... | collective-permute-start | bytes 98312 | tf_op jit(solution)/shard_map/ppermute | solution.py:30
  47.4 5.3 %collective-permute-start.12 = (f32[64,128]{1,0:T(8,128)S(1)}, f32[64,128]{1,0:T(8,128)S(1)}, u32[]{:S(2)}, u32[]{:S(2)}) collective-permute-start(f32[64,128]{1,0:T(8,128)S(1)} %get-tuple-element.84), channel_id=1, source_target_pairs={{0,4},{4,0},{8,12},{12,8},{1,5},{5,1},{9,13},{13,9},{2,6},{6,2},{1... | collective-permute-start | bytes 98312 | tf_op jit(solution)/shard_map/ppermute | solution.py:30

commit v5 on v4

--- a/solution.py
+++ b/solution.py
@@ -224,21 +224,22 @@
     count = squares_ref.shape[0]
     at = far_ref.shape[0] - NOTES
     notes = jnp.zeros((1, count), F32)
-    for ref in (sib_ref, far_ref, fwd_ref):
+    for ref in (far_ref, fwd_ref):
         coded = ref[at:, :count].astype(F32)
         notes = notes + ((coded[0:1] + coded[1:2]) + coded[2:3])
     for row in range(0, count, LANES):
         rows = slice(row, row + LANES)
         others = jnp.transpose(jnp.broadcast_to(notes[:, rows], (LANES, LANES)))
-        mine = jnp.sum(squares_ref[rows, :], axis=1, keepdims=True)
-        scale_ref[rows, :] = lax.rsqrt((mine + others) / D + EPS)
+        near = jnp.sum(squares_ref[rows, :] + row_squares(sib_ref, rows), axis=1, keepdims=True)
+        scale_ref[rows, :] = lax.rsqrt((near + others) / D + EPS)
     at = 0
     for start, rows in parts:
         here = slice(at, at + rows)
+        there = slice(start, start + rows)
         at += rows
-        for bits, ref in enumerate((a_ref, sib_ref, far_ref, fwd_ref)):
+        for bits, (ref, where) in enumerate(((a_ref, here), (sib_ref, there), (far_ref, here), (fwd_ref, here))):
             index = t ^ bits
-            put_block(normed_ref, here, index, normed_block(ref, here, scale_ref, start, gain_ref, index))
+            put_block(normed_ref, here, index, normed_block(ref, where, scale_ref, start, gain_ref, index))
 
     def put(at, products):
         streams = rounded(products)
@@ -474,6 +475,8 @@
         anywhere=(0,),
     )
     far = [flipped(block, 2) for block in own]
+    hidden, own = lax.optimization_barrier((hidden, own))
+    sib = flipped(hidden, 1)
     filt = short_filter.transpose(1, 0, 2)
     gain = norm_gain[None]
     skip = skip_gain[None]
@@ -483,7 +486,7 @@
     from_cache = jnp.exp(-dec * (count * position)) * cached_state.T
     tile = (groups, poles, SEGS, LANES)
     w = in_proj.transpose(1, 0, 2)
-    w, inj, jump, from_cache = lax.optimization_barrier((w, inj, jump, from_cache))
+    w, inj, jump, from_cache, own = lax.optimization_barrier((w, inj, jump, from_cache, own))
     w, fac, rin, scan, span, end, reach, cache = call(
         functools.partial(stage_kernel, seg, units),
         [
@@ -501,14 +504,13 @@
     def streams_of(rows, dtype=F32):
         return sds(3 * groups, rows, LANES, dtype=dtype)
 
-    arrived, mine, hidden, fac = lax.optimization_barrier((far[0], own[0], hidden, fac))
-    fwd, sib_first = flipped(arrived, 1), flipped(mine, 1)
-    sib = flipped(hidden, 1)
+    arrived, fac = lax.optimization_barrier((far[0], fac))
+    fwd = flipped(arrived, 1)
     scale, tail, send, body = call(
         functools.partial(head_kernel, head),
         [sds(count, LANES), streams_of(TAIL), streams_of(HALO, BF16), streams_of(tokens)],
         [pltpu.VMEM((TAIL + tokens, D), BF16)],
-        (own[0], sib_first, arrived, fwd, squares, gain, w),
+        (own[0], sib, arrived, fwd, squares, gain, w),
     )
     if contexts == 4:
         prior = paired_with(send, 1), paired_with(send, 3)
@@ -521,12 +523,14 @@
         [pltpu.VMEM((later, 2 * width), BF16)],
         (*own[1:], sib, scale, gain, w),
     )
-    other, after = cache, part
+    other, after = cache, (part, *prior)
     qs, zs, ends = [], [], []
     offset = 0
     for k, ((a, n), some) in enumerate(zip(rest, taken)):
         plane = (groups, some * tokens, LANES)
         arrived, after = lax.optimization_barrier((far[1 + k], after))
+        if k == 0:
+            prior = after[1:]
         fwd = after = flipped(arrived, 1)
         args = (arrived, fwd, scale, gain, w, part, filt, fac)
         own_rows = (body.shape[1] + HALO if k == 0 else prior[0].shape[1]) + n

time: 55.4 us -> 49.7 us (0.90)
  waiting for transfers between devices: 9.55 us -> 3.5 us
    ppermute x5, waiting for transfers between devices: 3.83 us -> 0.24 us  [paired_with(): return lax.ppermute(block, 'context', [(i, i ^ bits) for i in range(size)])]
    ppermute x10 -> x9, waiting for transfers between devices: 5.72 us -> 3.26 us  [flipped(): return lax.ppermute(block, 'tensor', [(i, i ^ bit) for i in range(size)])]
    ppermute x10 -> x9, starting transfers between devices: 6.64 us -> 6.89 us  [flipped(): return lax.ppermute(block, 'tensor', [(i, i ^ bit) for i in range(size)])]
  transfers between devices with their start and end apart: 15 -> 14, of which waited for: 6 -> 4; matrix products, arithmetic and copies ran while one was open for 1% -> 2% of each run, Pallas kernels for 40% -> 45%
where the time goes in v5:
time: 49.7 us; the launch traced here: 49.4 us
  Pallas kernels  29.9 us (60%)
  starting transfers between devices  15 us (30%)
  waiting for transfers between devices  3.5 us (7%)
  other arithmetic  0.81 us (2%)
    pallas_call x9, Pallas kernels, call(): pl.pallas_call(kernel, out_shape=outs, in_specs=specs, out_specs=jax.tree...  29.9 us
    ppermute x5, starting transfers between devices, paired_with(): return lax.ppermute(block, 'context', [(i, i ^ bits) for i in range(size)])  8.12 us
    ppermute x9, starting transfers between devices, flipped(): return lax.ppermute(block, 'tensor', [(i, i ^ bit) for i in range(size)])  6.89 us
    ppermute x9, waiting for transfers between devices, flipped(): return lax.ppermute(block, 'tensor', [(i, i ^ bit) for i in range(size)])  3.26 us
  transfers between devices with their start and end apart: 14, of which 4 were waited for; matrix products, arithmetic and copies ran while one was open for 2% of the time, Pallas kernels for 45%

profile of v5, /device:TPU:0, one launch (start us, length us, event | category | flops | bytes accessed | tf_op | source)
XLA Modules:
  0.0 49.4 jit_solution(1285925796611945426)
XLA Ops:
  0.0 1.6 %shard_map.91 = (bf16[88,1024]{1,0:T(8,128)(2,1)S(1)}, bf16[128,1024]{1,0:T(8,128)(2,1)S(1)}, bf16[144,1024]{1,0:T(8,128)(2,1)S(1)}, bf16[160,1024]{1,0:T(8,128)(2,1)S(1)}, f32[512,128]{1,0:T(8,128)S(1)}) custom-call(bf16[512,1024]{1,0:T(8,128)(2,1)} %h_any.1), custom_call_target="tpu_custom_call" | custom-call | bytes 1024 | tf_op jit(solution)/shard_map/pallas_call | solution.py:41
  1.6 0.6 %collective-permute-start.4 = (bf16[512,1024]{1,0:T(8,128)(2,1)}, bf16[512,1024]{1,0:T(8,128)(2,1)S(1)}, u32[]{:S(2)}, u32[]{:S(2)}) collective-permute-start(bf16[512,1024]{1,0:T(8,128)(2,1)} %h_any.1), channel_id=1, source_target_pairs={{0,1},{1,0},{2,3},{3,2},{4,5},{5,4},{6,7},{7,6},{8,9},{9,8},{10,11... | collective-permute-start | bytes 3145736 | tf_op jit(solution)/shard_map/ppermute | solution.py:35
  2.2 2.6 %collective-permute-start = (bf16[88,1024]{1,0:T(8,128)(2,1)S(1)}, bf16[88,1024]{1,0:T(8,128)(2,1)S(1)}, u32[]{:S(2)}, u32[]{:S(2)}) collective-permute-start(bf16[88,1024]{1,0:T(8,128)(2,1)S(1)} %get-tuple-element.76.a_ref), channel_id=1, source_target_pairs={{0,2},{1,3},{2,0},{3,1},{4,6},{5,7},{6,4},{7,5},{8,10},{9,11},{10,... | collective-permute-start | bytes 540680 | tf_op jit(solution)/shard_map/ppermute | solution.py:35
  4.7 0.1 collective-permute-start.3
  4.8 0.8 %bitcast_multiply_fusion = (f32[16,512]{1,0:T(8,128)S(1)}, f32[16,512]{1,0:T(8,128)S(1)}, f32[16,512]{1,0:T(8,128)S(1)}) fusion(f32[512,16]{0,1:T(8,128)} %param.17, f32[]{:T(128)S(6)} %mul.28, f32[512,16]{0,1:T(8,128)} %param.14), kind=kLoop, calls=%fused_computation | loop fusion | flops 49152 | bytes 163844 | tf_op jit(solution)/shard_map/mul | solution.py:486
  5.6 0.0 copy-start.1
  5.7 4.7 %shard_map.92 = (bf16[3,4096,512]{2,1,0:T(8,128)(2,1)S(1)}, f32[4,16,8,128]{3,2,1,0:T(8,128)S(1)}, f32[4,16,8,128]{3,2,1,0:T(8,128)S(1)}, f32[3,4,16,8,128]{4,3,...) custom-call(bf16[3,4096,512]{2,1,0:T(8,128)(2,1)} %bitcast.22, ...), custom_call_target="tpu_custom_call" | custom-call | bytes 1024 | tf_op jit(solution)/shard_map/pallas_call | solution.py:41
  10.3 0.0 collective-permute-done.far_ref
  10.3 0.2 collective-permute-start.5
  10.5 1.9 %collective-permute-start.2 = (bf16[144,1024]{1,0:T(8,128)(2,1)S(1)}, bf16[144,1024]{1,0:T(8,128)(2,1)S(1)}, u32[]{:S(2)}, u32[]{:S(2)}) collective-permute-start(bf16[144,1024]{1,0:T(8,128)(2,1)S(1)} %get-tuple-element.73.refs_1_), channel_id=1, source_target_pairs={{0,2},{1,3},{2,0},{3,1},{4,6},{5,7},{6,4},{7,5},{8,10},{9,11},{10,... | collective-permute-start | bytes 884744 | tf_op jit(solution)/shard_map/ppermute | solution.py:35
  12.4 3.5 %shard_map.93 = (f32[512,128]{1,0:T(8,128)S(1)}, f32[12,16,128]{2,1,0:T(8,128)S(1)}, bf16[12,8,128]{2,1,0:T(8,128)(2,1)S(1)}, f32[12,64,128]{2,1,0:T(8,128)S(1)}) custom-call(bf16[88,1024]{1,0:T(8,128)(2,1)S(1)} %get-tuple-element.76.a_ref, bf16[512,1024]{1,0:T(8,128)(2,1)S(1)} %collective-permute-done.4.sib_ref.refs_3_, ...), custom_call_target="tpu_custom_call" | custom-call | bytes 1024 | tf_op jit(solution)/shard_map/pallas_call | solution.py:41
  16.0 3.7 %collective-permute-start.7 = (bf16[12,8,128]{2,1,0:T(8,128)(2,1)S(1)}, bf16[12,8,128]{2,1,0:T(8,128)(2,1)S(1)}, u32[]{:S(2)}, u32[]{:S(2)}) collective-permute-start(bf16[12,8,128]{2,1,0:T(8,128)(2,1)S(1)} %get-tuple-element.81), channel_id=1, source_target_pairs={{0,12},{4,8},{8,4},{12,0},{1,13},{5,9},{9,5},{13,1},{2,14},{6,10},... | collective-permute-start | bytes 73736 | tf_op jit(solution)/shard_map/ppermute | solution.py:30
  19.6 0.0 collective-permute-start.6
  19.6 4.5 %shard_map.94.part_ref = f32[12,432,128]{2,1,0:T(8,128)S(1)} custom-call(bf16[128,1024]{1,0:T(8,128)(2,1)S(1)} %get-tuple-element.72.refs_0_, bf16[144,1024]{1,0:T(8,128)(2,1)S(1)} %get-tuple-element.73.refs_1_, bf16[160,1024]{1,0:T(8,128)(2,1)S(1)} %get-tuple-element.74.refs_2_, bf16[512,1024]{1,0:T(8,128)(2,1)S(1)} %collective-permute-done.4.sib_ref.refs_3_, ...), custom_call_target="tpu_custom_call" | custom-call | bytes 1024 | tf_op jit(solution)/shard_map/pallas_call | solution.py:41
  24.1 0.0 collective-permute-done.3.far_ref
  24.1 0.0 collective-permute-done.7.refs_1_
  24.1 0.1 collective-permute-start.8
  24.2 1.4 %collective-permute-start.1 = (bf16[160,1024]{1,0:T(8,128)(2,1)S(1)}, bf16[160,1024]{1,0:T(8,128)(2,1)S(1)}, u32[]{:S(2)}, u32[]{:S(2)}) collective-permute-start(bf16[160,1024]{1,0:T(8,128)(2,1)S(1)} %get-tuple-element.74.refs_2_), channel_id=1, source_target_pairs={{0,2},{1,3},{2,0},{3,1},{4,6},{5,7},{6,4},{7,5},{8,10},{9,11},{10,... | collective-permute-start | bytes 983048 | tf_op jit(solution)/shard_map/ppermute | solution.py:35
  25.6 0.0 collective-permute-done.2.far_ref
  25.6 0.1 collective-permute-done.8.fwd_ref
  25.7 0.1 collective-permute-start.9
  25.9 3.7 %shard_map.95 = (f32[4,192,128]{2,1,0:T(8,128)S(1)}, f32[4,192,128]{2,1,0:T(8,128)S(1)}, f32[3,4,16,8,128]{4,3,2,1,0:T(8,128)S(1)}, f32[4,16,8,128]{3,2,1,0:T(8,128)S(1)}, f32[12,8,128]{2,1,0:T(8,128)S(1)}) custom-call(bf16[128,1024]{1,0:T(8,128)(2,1)S(1)} %collective-permute-done.3.far_ref, bf16[128,1024]{1,0:T(8,128)(2,1)S(1)} %collective-permute-done.8.fwd_ref, ...), custom_call_target="tpu_custom_call" | custom-call | bytes 1024 | tf_op jit(solution)/shard_map/pallas_call | solution.py:41
  29.6 3.3 %shard_map.96 = (f32[4,128,128]{2,1,0:T(8,128)S(1)}, f32[4,128,128]{2,1,0:T(8,128)S(1)}, f32[2,4,16,8,128]{4,3,2,1,0:T(8,128)S(1)}, f32[4,16,8,128]{3,2,1,0:T(8,128)S(1)}, f32[12,24,128]{2,1,0:T(8,128)S(1)}) custom-call(bf16[144,1024]{1,0:T(8,128)(2,1)S(1)} %collective-permute-done.2.far_ref, bf16[144,1024]{1,0:T(8,128)(2,1)S(1)} %collective-permute-done.9.fwd_ref, ...), custom_call_target="tpu_custom_call" | custom-call | bytes 1024 | tf_op jit(solution)/shard_map/pallas_call | solution.py:41
  32.8 1.5 %collective-permute-done.1.far_ref = bf16[160,1024]{1,0:T(8,128)(2,1)S(1)} collective-permute-done((bf16[160,1024]{1,0:T(8,128)(2,1)S(1)}, bf16[160,1024]{1,0:T(8,128)(2,1)S(1)}, u32[]{:S(2)}, u32[]{:S(2)}) %collective-permute-start.1) | collective-permute-done | bytes 327712 | tf_op jit(solution)/shard_map/ppermute | solution.py:35
  34.3 1.6 %collective-permute-done.10.fwd_ref = bf16[160,1024]{1,0:T(8,128)(2,1)S(1)} collective-permute-done((bf16[160,1024]{1,0:T(8,128)(2,1)S(1)}, bf16[160,1024]{1,0:T(8,128)(2,1)S(1)}, u32[]{:S(2)}, u32[]{:S(2)}) %collective-permute-start.10) | collective-permute-done | bytes 327712 | tf_op jit(solution)/shard_map/ppermute | solution.py:35
  36.0 3.4 %shard_map.97 = (f32[4,192,128]{2,1,0:T(8,128)S(1)}, f32[4,192,128]{2,1,0:T(8,128)S(1)}, f32[64,128]{1,0:T(8,128)S(1)}) custom-call(bf16[160,1024]{1,0:T(8,128)(2,1)S(1)} %collective-permute-done.1.far_ref, bf16[160,1024]{1,0:T(8,128)(2,1)S(1)} %collective-permute-done.10.fwd_ref, f32[512,128]{1,0:T(8,128)S(1)} %get-tuple-element.80.refs_4_.scale_ref, ...), custom_call_target="tpu_custom_call" | custom-call | bytes 1024 | tf_op jit(solution)/shard_map/pallas_call | solution.py:41
  39.4 1.1 %collective-permute-start.13 = (f32[64,128]{1,0:T(8,128)S(1)}, f32[64,128]{1,0:T(8,128)S(1)}, u32[]{:S(2)}, u32[]{:S(2)}) collective-permute-start(f32[64,128]{1,0:T(8,128)S(1)} %get-tuple-element.102), channel_id=1, source_target_pairs={{0,12},{4,8},{8,4},{12,0},{1,13},{5,9},{9,5},{13,1},{2,14},{6,10},... | collective-permute-start | bytes 98312 | tf_op jit(solution)/shard_map/ppermute | solution.py:30
  40.5 2.4 %collective-permute-start.12 = (f32[64,128]{1,0:T(8,128)S(1)}, f32[64,128]{1,0:T(8,128)S(1)}, u32[]{:S(2)}, u32[]{:S(2)}) collective-permute-start(f32[64,128]{1,0:T(8,128)S(1)} %get-tuple-element.102), channel_id=1, source_target_pairs={{0,8},{4,12},{8,0},{12,4},{1,9},{5,13},{9,1},{13,5},{2,10},{6,14},... | collective-permute-start | bytes 98312 | tf_op jit(solution)/shard_map/ppermute | solution.py:30
  42.9 0.9 %collective-permute-start.11 = (f32[64,128]{1,0:T(8,128)S(1)}, f32[64,128]{1,0:T(8,128)S(1)}, u32[]{:S(2)}, u32[]{:S(2)}) collective-permute-start(f32[64,128]{1,0:T(8,128)S(1)} %get-tuple-element.102), channel_id=1, source_target_pairs={{0,4},{4,0},{8,12},{12,8},{1,5},{5,1},{9,13},{13,9},{2,6},{6,2},{1... | collective-permute-start | bytes 98312 | tf_op jit(solution)/shard_map/ppermute | solution.py:30
  43.8 2.8 %shard_map.98 = (f32[4,192,128]{2,1,0:T(8,128)S(1)}, f32[8,4,16,8,128]{4,3,2,1,0:T(8,128)S(1)}) custom-call(f32[4,16,8,128]{3,2,1,0:T(8,128)S(1)} %get-tuple-element.68.fac_ref, f32[4,16,8,128]{3,2,1,0:T(8,128)S(1)} %get-tuple-element.70.rin_ref, f32[3,4,16,8,128]{4,3,2,1,0:T(8,128)S(1)} %get-tuple-element.71.scan_ref, f32[1,512]{1,0:T(1,128)S(1)} %bitcast.21, ...), custom_call_target="tpu_custom_call" | custom-call | bytes 1024 | tf_op jit(solution)/shard_map/pallas_call | solution.py:41
  46.6 0.2 collective-permute-done.11.refs_0_
  46.9 2.6 %shard_map.99 = bf16[512,512]{1,0:T(8,128)(2,1)} custom-call(f32[4,16,8,128]{3,2,1,0:T(8,128)S(1)} %get-tuple-element.68.fac_ref, f32[8,4,16,8,128]{4,3,2,1,0:T(8,128)S(1)} %get-tuple-element.69.reach_ref, f32[8,4,16,8,128]{4,3,2,1,0:T(8,128)S(1)} %get-tuple-element.99.begin_ref, f32[16,512]{1,0:T(8,128)S(1)} %get-tuple-element.66.inj_ref, ...), custom_call_target="tpu_custom_call" | custom-call | bytes 1024 | tf_op jit(solution)/shard_map/pallas_call | solution.py:41
  (12 shorter events, 0.0 us)
Async XLA Ops:
  1.6 10.8 %collective-permute-start.4 = (bf16[512,1024]{1,0:T(8,128)(2,1)}, bf16[512,1024]{1,0:T(8,128)(2,1)S(1)}, u32[]{:S(2)}, u32[]{:S(2)}) collective-permute-start(bf16[512,1024]{1,0:T(8,128)(2,1)} %h_any.1), channel_id=1, source_target_pairs={{0,1},{1,0},{2,3},{3,2},{4,5},{5,4},{6,7},{7,6},{8,9},{9,8},{10,11... | collective-permute-start | bytes 3145736 | tf_op jit(solution)/shard_map/ppermute | solution.py:35
  2.2 8.1 %collective-permute-start = (bf16[88,1024]{1,0:T(8,128)(2,1)S(1)}, bf16[88,1024]{1,0:T(8,128)(2,1)S(1)}, u32[]{:S(2)}, u32[]{:S(2)}) collective-permute-start(bf16[88,1024]{1,0:T(8,128)(2,1)S(1)} %get-tuple-element.76.a_ref), channel_id=1, source_target_pairs={{0,2},{1,3},{2,0},{3,1},{4,6},{5,7},{6,4},{7,5},{8,10},{9,11},{10,... | collective-permute-start | bytes 540680 | tf_op jit(solution)/shard_map/ppermute | solution.py:35
  4.7 19.4 %collective-permute-start.3 = (bf16[128,1024]{1,0:T(8,128)(2,1)S(1)}, bf16[128,1024]{1,0:T(8,128)(2,1)S(1)}, u32[]{:S(2)}, u32[]{:S(2)}) collective-permute-start(bf16[128,1024]{1,0:T(8,128)(2,1)S(1)} %get-tuple-element.72.refs_0_), channel_id=1, source_target_pairs={{0,2},{1,3},{2,0},{3,1},{4,6},{5,7},{6,4},{7,5},{8,10},{9,11},{10,... | collective-permute-start | bytes 786440 | tf_op jit(solution)/shard_map/ppermute | solution.py:35
  5.6 6.8 %copy-start.1 = (f32[4096]{0:T(1024)S(1)}, f32[4096]{0:T(1024)}, u32[]{:S(2)}) copy-start(f32[4096]{0:T(1024)} %param.10) | copy-start | bytes 49156
  10.3 2.1 %collective-permute-start.5 = (bf16[88,1024]{1,0:T(8,128)(2,1)S(1)}, bf16[88,1024]{1,0:T(8,128)(2,1)S(1)}, u32[]{:S(2)}, u32[]{:S(2)}) collective-permute-start(bf16[88,1024]{1,0:T(8,128)(2,1)S(1)} %collective-permute-done.far_ref), channel_id=1, source_target_pairs={{0,1},{1,0},{2,3},{3,2},{4,5},{5,4},{6,7},{7,6},{8,9},{9,8},{10,11... | collective-permute-start | bytes 540680 | tf_op jit(solution)/shard_map/ppermute | solution.py:35
  10.5 15.1 %collective-permute-start.2 = (bf16[144,1024]{1,0:T(8,128)(2,1)S(1)}, bf16[144,1024]{1,0:T(8,128)(2,1)S(1)}, u32[]{:S(2)}, u32[]{:S(2)}) collective-permute-start(bf16[144,1024]{1,0:T(8,128)(2,1)S(1)} %get-tuple-element.73.refs_1_), channel_id=1, source_target_pairs={{0,2},{1,3},{2,0},{3,1},{4,6},{5,7},{6,4},{7,5},{8,10},{9,11},{10,... | collective-permute-start | bytes 884744 | tf_op jit(solution)/shard_map/ppermute | solution.py:35
  16.0 8.2 %collective-permute-start.7 = (bf16[12,8,128]{2,1,0:T(8,128)(2,1)S(1)}, bf16[12,8,128]{2,1,0:T(8,128)(2,1)S(1)}, u32[]{:S(2)}, u32[]{:S(2)}) collective-permute-start(bf16[12,8,128]{2,1,0:T(8,128)(2,1)S(1)} %get-tuple-element.81), channel_id=1, source_target_pairs={{0,12},{4,8},{8,4},{12,0},{1,13},{5,9},{9,5},{13,1},{2,14},{6,10},... | collective-permute-start | bytes 73736 | tf_op jit(solution)/shard_map/ppermute | solution.py:30
  19.6 4.5 %collective-permute-start.6 = (bf16[12,8,128]{2,1,0:T(8,128)(2,1)S(1)}, bf16[12,8,128]{2,1,0:T(8,128)(2,1)S(1)}, u32[]{:S(2)}, u32[]{:S(2)}) collective-permute-start(bf16[12,8,128]{2,1,0:T(8,128)(2,1)S(1)} %get-tuple-element.81), channel_id=1, source_target_pairs={{0,4},{4,0},{8,12},{12,8},{1,5},{5,1},{9,13},{13,9},{2,6},{6,2},{1... | collective-permute-start | bytes 73736 | tf_op jit(solution)/shard_map/ppermute | solution.py:30
  19.6 6.2 %copy-start = (f32[7,3,512]{2,0,1:T(8,128)S(1)}, f32[7,3,512]{2,0,1:T(8,128)}, u32[]{:S(2)}) copy-start(f32[7,3,512]{2,0,1:T(8,128)} %param.12) | copy-start | bytes 129028
  19.6 6.2 %copy-start.2 = (f32[512]{0:T(512)S(1)}, f32[512]{0:T(512)}, u32[]{:S(2)}) copy-start(f32[512]{0:T(512)} %param.16) | copy-start | bytes 6148
  24.1 1.6 %collective-permute-start.8 = (bf16[128,1024]{1,0:T(8,128)(2,1)S(1)}, bf16[128,1024]{1,0:T(8,128)(2,1)S(1)}, u32[]{:S(2)}, u32[]{:S(2)}) collective-permute-start(bf16[128,1024]{1,0:T(8,128)(2,1)S(1)} %collective-permute-done.3.far_ref), channel_id=1, source_target_pairs={{0,1},{1,0},{2,3},{3,2},{4,5},{5,4},{6,7},{7,6},{8,9},{9,8},{10,11... | collective-permute-start | bytes 786440 | tf_op jit(solution)/shard_map/ppermute | solution.py:35
  24.2 10.1 %collective-permute-start.1 = (bf16[160,1024]{1,0:T(8,128)(2,1)S(1)}, bf16[160,1024]{1,0:T(8,128)(2,1)S(1)}, u32[]{:S(2)}, u32[]{:S(2)}) collective-permute-start(bf16[160,1024]{1,0:T(8,128)(2,1)S(1)} %get-tuple-element.74.refs_2_), channel_id=1, source_target_pairs={{0,2},{1,3},{2,0},{3,1},{4,6},{5,7},{6,4},{7,5},{8,10},{9,11},{10,... | collective-permute-start | bytes 983048 | tf_op jit(solution)/shard_map/ppermute | solution.py:35
  25.7 3.8 %collective-permute-start.9 = (bf16[144,1024]{1,0:T(8,128)(2,1)S(1)}, bf16[144,1024]{1,0:T(8,128)(2,1)S(1)}, u32[]{:S(2)}, u32[]{:S(2)}) collective-permute-start(bf16[144,1024]{1,0:T(8,128)(2,1)S(1)} %collective-permute-done.2.far_ref), channel_id=1, source_target_pairs={{0,1},{1,0},{2,3},{3,2},{4,5},{5,4},{6,7},{7,6},{8,9},{9,8},{10,11... | collective-permute-start | bytes 884744 | tf_op jit(solution)/shard_map/ppermute | solution.py:35
  34.3 1.6 %collective-permute-start.10 = (bf16[160,1024]{1,0:T(8,128)(2,1)S(1)}, bf16[160,1024]{1,0:T(8,128)(2,1)S(1)}, u32[]{:S(2)}, u32[]{:S(2)}) collective-permute-start(bf16[160,1024]{1,0:T(8,128)(2,1)S(1)} %collective-permute-done.1.far_ref), channel_id=1, source_target_pairs={{0,1},{1,0},{2,3},{3,2},{4,5},{5,4},{6,7},{7,6},{8,9},{9,8},{10,11... | collective-permute-start | bytes 983048 | tf_op jit(solution)/shard_map/ppermute | solution.py:35
  39.4 7.2 %collective-permute-start.13 = (f32[64,128]{1,0:T(8,128)S(1)}, f32[64,128]{1,0:T(8,128)S(1)}, u32[]{:S(2)}, u32[]{:S(2)}) collective-permute-start(f32[64,128]{1,0:T(8,128)S(1)} %get-tuple-element.102), channel_id=1, source_target_pairs={{0,12},{4,8},{8,4},{12,0},{1,13},{5,9},{9,5},{13,1},{2,14},{6,10},... | collective-permute-start | bytes 98312 | tf_op jit(solution)/shard_map/ppermute | solution.py:30
  40.5 6.1 %collective-permute-start.12 = (f32[64,128]{1,0:T(8,128)S(1)}, f32[64,128]{1,0:T(8,128)S(1)}, u32[]{:S(2)}, u32[]{:S(2)}) collective-permute-start(f32[64,128]{1,0:T(8,128)S(1)} %get-tuple-element.102), channel_id=1, source_target_pairs={{0,8},{4,12},{8,0},{12,4},{1,9},{5,13},{9,1},{13,5},{2,10},{6,14},... | collective-permute-start | bytes 98312 | tf_op jit(solution)/shard_map/ppermute | solution.py:30
  42.9 3.9 %collective-permute-start.11 = (f32[64,128]{1,0:T(8,128)S(1)}, f32[64,128]{1,0:T(8,128)S(1)}, u32[]{:S(2)}, u32[]{:S(2)}) collective-permute-start(f32[64,128]{1,0:T(8,128)S(1)} %get-tuple-element.102), channel_id=1, source_target_pairs={{0,4},{4,0},{8,12},{12,8},{1,5},{5,1},{9,13},{13,9},{2,6},{6,2},{1... | collective-permute-start | bytes 98312 | tf_op jit(solution)/shard_map/ppermute | solution.py:30
